TPU v7x, 32 devices: a whole 2x2x4 slice. The times are simulated.
32 devices in a mesh: ctx: 16 (over z, y, x), fsdp: 2 (over core).
Axes of the slice: x: 2, y: 2, z: 4, core: 2. Of those that a mesh axis runs over, the one named last changes fastest.
Arguments:
- tokens: bfloat16 [2, 4096, 1024], P('fsdp', 'ctx'), may hold values from -6 to 6
- seg_ids: int32 [2, 4096], P('fsdp', 'ctx'), may hold values from 0 to 3, as said below
- doc_pos: int32 [2, 4096], P('fsdp', 'ctx'), may hold values from 0 to 1999, as said below
- attn_gain: float32 [1024], replicated, may hold values from 0.5 to 1.5
- w_query: bfloat16 [1024, 1024], P('fsdp'), may hold values from -0.1875 to 0.1875
- w_key: bfloat16 [1024, 512], P('fsdp'), may hold values from -0.1875 to 0.1875
- w_value: bfloat16 [1024, 512], P('fsdp'), may hold values from -0.1875 to 0.1875
- query_gain: float32 [64], replicated, may hold values from 1 to 2
- key_gain: float32 [64], replicated, may hold values from 1 to 2
- w_out: bfloat16 [1024, 1024], P('fsdp'), may hold values from -1.5 to 1.5
- ffn_gain: float32 [1024], replicated, may hold values from 0.5 to 1.5
- w_gate: bfloat16 [1024, 4608], P('fsdp'), may hold values from -0.1875 to 0.1875
- w_up: bfloat16 [1024, 4608], P('fsdp'), may hold values from -0.1875 to 0.1875
- w_down: bfloat16 [4608, 1024], P('fsdp'), may hold values from -0.09375 to 0.09375
- d_output: bfloat16 [2, 4096, 1024], P('fsdp', 'ctx'), may hold values from -6 to 6
Outputs:
- output: bfloat16 [2, 4096, 1024], P('fsdp', 'ctx')
- d_tokens: float32 [2, 4096, 1024], P('fsdp', 'ctx')
- d_attn_gain: float32 [1024], replicated
- d_w_query: float32 [1024, 1024], P('fsdp', 'ctx')
- d_w_key: float32 [1024, 512], P('fsdp', 'ctx')
- d_w_value: float32 [1024, 512], P('fsdp', 'ctx')
- d_query_gain: float32 [64], replicated
- d_key_gain: float32 [64], replicated
- d_w_out: float32 [1024, 1024], P('fsdp', 'ctx')
- d_ffn_gain: float32 [1024], replicated
- d_w_gate: float32 [1024, 4608], P('fsdp', 'ctx')
- d_w_up: float32 [1024, 4608], P('fsdp', 'ctx')
- d_w_down: float32 [4608, 1024], P('fsdp', 'ctx')
Inputs may be any that keep to these rules, and one draw needn't show every extreme that they name: `seg_ids`: within each sequence the ids start at 0 and never fall; each run of equal ids is a document of 1 to 2000 tokens, every sequence begins with a document of exactly 2000 tokens, and every sequence holds 4 documents. `doc_pos`: the token's place within its document: 0 at the first token of each run of equal seg_ids, rising by one along it.
All inputs are finite; a program needn't handle non-finite values.
Results may differ from a plain program's by a relative error of at most 0.015.
The roundings to bfloat16 on the way count: a program that leaves them out, or rounds other values in their place, can miss the bound.
Values may be sent and summed in bfloat16 or wider, within the bound.
A program may use at most 320 MiB of HBM per device.

v0:
```python
import jax
import jax.numpy as jnp
from jax import lax
from jax.sharding import PartitionSpec as P

HEADS = 16
KV_HEADS = 8
HEAD_DIM = 64
HOPS = 8


EPSILON = 1e-05
THETA = 1000000.0
MASKED = -1e30


def from_behind(block, axis, distance):
    devices = range(lax.axis_size(axis))
    route = [(i - distance, i) for i in devices if i - distance in devices]
    return lax.ppermute(block, axis, route)


def rms_norm(values, norm_gain):
    return (
        values * lax.rsqrt(jnp.mean(values * values, axis=-1, keepdims=True) + EPSILON) * norm_gain
    )


def rms_back(values, norm_gain, upstream):
    inverse = lax.rsqrt(jnp.mean(values * values, axis=-1, keepdims=True) + EPSILON)
    scaled = upstream * norm_gain
    row_width = values.shape[-1]
    d_values = (
        inverse * scaled
        - values * inverse**3 * jnp.sum(scaled * values, axis=-1, keepdims=True) / row_width
    )
    return (d_values, upstream * values * inverse)


def rotary(values, positions, turn_sign):
    half_dim = values.shape[-1] // 2
    inverse_freq = THETA ** (-(2.0 / values.shape[-1]) * jnp.arange(half_dim, dtype=jnp.float32))
    angles = positions.astype(jnp.float32)[:, None] * inverse_freq[None, :]
    cosine = jnp.cos(angles)[:, None, :]
    sine_part = turn_sign * jnp.sin(angles)[:, None, :]
    first_half = values[..., :half_dim]
    second_half = values[..., half_dim:]
    return jnp.concatenate(
        [
            first_half * cosine - second_half * sine_part,
            second_half * cosine + first_half * sine_part,
        ],
        axis=-1,
    )


def outer_product(left_mat, right_mat):
    return lax.dot_general(
        left_mat, right_mat, (((0,), (0,)), ((), ())), preferred_element_type=jnp.float32
    )


def against(left_mat, right_mat):
    return lax.dot_general(
        left_mat, right_mat, (((1,), (1,)), ((), ())), preferred_element_type=jnp.float32
    )


def body(
    tokens,
    seg_ids,
    doc_pos,
    attn_gain,
    w_query,
    w_key,
    w_value,
    query_gain,
    key_gain,
    w_out,
    ffn_gain,
    w_gate,
    w_up,
    w_down,
    d_output,
):
    cycle_place = lax.axis_index("ctx")
    tok_rows = tokens.shape[1]
    resid_in = tokens[0].astype(jnp.float32)
    seg_local = seg_ids[0]
    pos_local = doc_pos[0]
    q_per_kv = HEADS // KV_HEADS
    group_cols = q_per_kv * HEAD_DIM
    score_scale = HEAD_DIM ** (-0.5)
    q_full, k_full, v_full, o_full = (
        lax.all_gather(w_query, "fsdp", axis=0, tiled=True),
        lax.all_gather(w_key, "fsdp", axis=0, tiled=True),
        lax.all_gather(w_value, "fsdp", axis=0, tiled=True),
        lax.all_gather(w_out, "fsdp", axis=0, tiled=True),
    )
    gate_full, up_full, down_full = (
        lax.all_gather(w_gate, "fsdp", axis=0, tiled=True),
        lax.all_gather(w_up, "fsdp", axis=0, tiled=True),
        lax.all_gather(w_down, "fsdp", axis=0, tiled=True),
    )
    normed = rms_norm(resid_in, attn_gain)
    normed_low = normed.astype(jnp.bfloat16)
    query_raw = jnp.dot(normed_low, q_full, preferred_element_type=jnp.float32).reshape(
        tok_rows, HEADS, HEAD_DIM
    )
    key_raw = jnp.dot(normed_low, k_full, preferred_element_type=jnp.float32).reshape(
        tok_rows, KV_HEADS, HEAD_DIM
    )
    value_raw = jnp.dot(normed_low, v_full, preferred_element_type=jnp.float32)
    query_rot = rotary(rms_norm(query_raw, query_gain), pos_local, 1.0)
    key_rot = rotary(rms_norm(key_raw, key_gain), pos_local, 1.0)
    query_low = query_rot.astype(jnp.bfloat16).reshape(tok_rows, HEADS * HEAD_DIM)
    key_low = key_rot.astype(jnp.bfloat16).reshape(tok_rows, KV_HEADS * HEAD_DIM)
    value_low = value_raw.astype(jnp.bfloat16)
    own_kv = (key_low, value_low, seg_local)
    kv_blocks = [own_kv]
    carried = own_kv
    for hop_index in range(HOPS):
        carried = from_behind((carried[0], carried[1], carried[2]), "ctx", 1)
        kv_blocks.append(carried)
    key_all = jnp.concatenate([kv_entry[0] for kv_entry in kv_blocks], axis=0)
    value_all = jnp.concatenate([kv_entry[1] for kv_entry in kv_blocks], axis=0)
    seg_all = jnp.concatenate([kv_entry[2] for kv_entry in kv_blocks], axis=0)
    key_owner = cycle_place - jnp.arange(HOPS + 1, dtype=jnp.int32)
    owner_valid = jnp.repeat(key_owner >= 0, tok_rows)
    key_index = (
        key_owner[:, None] * tok_rows + jnp.arange(tok_rows, dtype=jnp.int32)[None, :]
    ).reshape(-1)
    query_index = cycle_place * tok_rows + jnp.arange(tok_rows, dtype=jnp.int32)
    allowed = (
        (seg_local[:, None] == seg_all[None, :])
        & (key_index[None, :] <= query_index[:, None])
        & owner_valid[None, :]
    )

    def group_scores(kv_group):
        query_part = lax.dynamic_slice_in_dim(query_low, kv_group * group_cols, group_cols, 1)
        query_part = query_part.reshape(tok_rows, q_per_kv, HEAD_DIM)
        key_part = lax.dynamic_slice_in_dim(key_all, kv_group * HEAD_DIM, HEAD_DIM, 1)
        value_part = lax.dynamic_slice_in_dim(value_all, kv_group * HEAD_DIM, HEAD_DIM, 1)
        scores = (
            jnp.einsum("trd,kd->rtk", query_part, key_part, preferred_element_type=jnp.float32)
            * score_scale
        )
        return (jnp.where(allowed[None], scores, MASKED), query_part, key_part, value_part)

    def forward_group(kv_group):
        scores, query_part, key_part, value_part = group_scores(kv_group)
        row_top = jnp.max(scores, axis=-1, keepdims=True)
        log_total = row_top + jnp.log(jnp.sum(jnp.exp(scores - row_top), axis=-1, keepdims=True))
        attn_probs = jnp.exp(scores - log_total)
        mixed_part = jnp.einsum(
            "rtk,kd->trd",
            attn_probs.astype(jnp.bfloat16),
            value_part,
            preferred_element_type=jnp.float32,
        )
        return (mixed_part.reshape(tok_rows, group_cols), log_total[..., 0])

    mixed_groups, total_groups = lax.map(forward_group, jnp.arange(KV_HEADS, dtype=jnp.int32))
    mixed = mixed_groups.transpose(1, 0, 2).reshape(tok_rows, HEADS * HEAD_DIM)
    mixed_low = mixed.astype(jnp.bfloat16)
    middle = resid_in + jnp.dot(mixed_low, o_full, preferred_element_type=jnp.float32)
    ffn_low = rms_norm(middle, ffn_gain).astype(jnp.bfloat16)
    gate_pre = jnp.dot(ffn_low, gate_full, preferred_element_type=jnp.float32)
    up_pre = jnp.dot(ffn_low, up_full, preferred_element_type=jnp.float32)
    gate_sig = jax.nn.sigmoid(gate_pre)
    gate_act = gate_pre * gate_sig
    hidden_low = (gate_act * up_pre).astype(jnp.bfloat16)
    result = middle + jnp.dot(hidden_low, down_full, preferred_element_type=jnp.float32)
    output = result.astype(jnp.bfloat16)[None]
    cot_low = d_output[0]
    cotangent = cot_low.astype(jnp.float32)
    grad_w_down = outer_product(hidden_low, cot_low)
    grad_hidden = against(cot_low, down_full)
    gate_back = (grad_hidden * up_pre * (gate_sig * (1.0 + gate_pre * (1.0 - gate_sig)))).astype(
        jnp.bfloat16
    )
    up_back = (grad_hidden * gate_act).astype(jnp.bfloat16)
    grad_w_gate = outer_product(ffn_low, gate_back)
    grad_w_up = outer_product(ffn_low, up_back)
    grad_ffn_in = against(gate_back, gate_full) + against(up_back, up_full)
    middle_part, ffn_terms = rms_back(middle, ffn_gain, grad_ffn_in)
    grad_middle = cotangent + middle_part
    middle_low = grad_middle.astype(jnp.bfloat16)
    grad_w_out = outer_product(mixed_low, middle_low)
    grad_mixed = against(middle_low, o_full).astype(jnp.bfloat16)

    def backward_group(kv_group):
        scores, query_part, key_part, value_part = group_scores(kv_group)
        attn_probs = jnp.exp(scores - total_groups[kv_group][..., None])
        mixed_grad_part = lax.dynamic_slice_in_dim(grad_mixed, kv_group * group_cols, group_cols, 1)
        mixed_grad_part = mixed_grad_part.reshape(tok_rows, q_per_kv, HEAD_DIM)
        grad_probs = jnp.einsum(
            "trd,kd->rtk", mixed_grad_part, value_part, preferred_element_type=jnp.float32
        )
        grad_value = jnp.einsum(
            "rtk,trd->kd",
            attn_probs.astype(jnp.bfloat16),
            mixed_grad_part,
            preferred_element_type=jnp.float32,
        )
        row_delta = jnp.sum(grad_probs * attn_probs, axis=-1, keepdims=True)
        grad_scores = (attn_probs * (grad_probs - row_delta)).astype(jnp.bfloat16)
        grad_query = (
            jnp.einsum("rtk,kd->trd", grad_scores, key_part, preferred_element_type=jnp.float32)
            * score_scale
        )
        grad_key = (
            jnp.einsum("rtk,trd->kd", grad_scores, query_part, preferred_element_type=jnp.float32)
            * score_scale
        )
        return (grad_query.reshape(tok_rows, group_cols), grad_key, grad_value)

    query_groups, key_groups, value_groups = lax.map(
        backward_group, jnp.arange(KV_HEADS, dtype=jnp.int32)
    )
    grad_query_rot = query_groups.transpose(1, 0, 2).reshape(tok_rows, HEADS, HEAD_DIM)
    key_blocks = key_groups.transpose(1, 0, 2).reshape(HOPS + 1, tok_rows, KV_HEADS * HEAD_DIM)
    value_blocks = value_groups.transpose(1, 0, 2).reshape(HOPS + 1, tok_rows, KV_HEADS * HEAD_DIM)
    home_key = key_blocks[HOPS]
    home_value = value_blocks[HOPS]
    for hop_index in range(HOPS, 0, -1):
        moved_key, moved_value = (
            from_behind(home_key.astype(jnp.bfloat16), "ctx", -1).astype(home_key.dtype),
            from_behind(home_value.astype(jnp.bfloat16), "ctx", -1).astype(home_value.dtype),
        )
        home_key = moved_key + key_blocks[hop_index - 1]
        home_value = moved_value + value_blocks[hop_index - 1]
    query_turned = rotary(grad_query_rot, pos_local, -1.0)
    key_turned = rotary(home_key.reshape(tok_rows, KV_HEADS, HEAD_DIM), pos_local, -1.0)
    query_back, query_terms = rms_back(query_raw, query_gain, query_turned)
    key_back, key_terms = rms_back(key_raw, key_gain, key_turned)
    query_back = query_back.reshape(tok_rows, HEADS * HEAD_DIM).astype(jnp.bfloat16)
    key_back = key_back.reshape(tok_rows, KV_HEADS * HEAD_DIM).astype(jnp.bfloat16)
    value_back = home_value.astype(jnp.bfloat16)
    grad_w_query = outer_product(normed_low, query_back)
    grad_w_key = outer_product(normed_low, key_back)
    grad_w_value = outer_product(normed_low, value_back)
    grad_normed = (
        against(query_back, q_full) + against(key_back, k_full) + against(value_back, v_full)
    )
    input_part, attn_terms = rms_back(resid_in, attn_gain, grad_normed)
    d_tokens = (grad_middle + input_part)[None]
    gain_totals = lax.psum(
        (
            jnp.sum(attn_terms, axis=0),
            jnp.sum(ffn_terms, axis=0),
            jnp.sum(query_terms, axis=(0, 1)),
            jnp.sum(key_terms, axis=(0, 1)),
        ),
        ("ctx", "fsdp"),
    )
    weight_grads = (
        grad_w_query,
        grad_w_key,
        grad_w_value,
        grad_w_out,
        grad_w_gate,
        grad_w_up,
        grad_w_down,
    )
    spread = (
        lax.psum_scatter(
            weight_grads[0].astype(jnp.bfloat16), "fsdp", scatter_dimension=0, tiled=True
        ).astype(jnp.float32),
        lax.psum_scatter(
            weight_grads[1].astype(jnp.bfloat16), "fsdp", scatter_dimension=0, tiled=True
        ).astype(jnp.float32),
        lax.psum_scatter(
            weight_grads[2].astype(jnp.bfloat16), "fsdp", scatter_dimension=0, tiled=True
        ).astype(jnp.float32),
        lax.psum_scatter(
            weight_grads[3].astype(jnp.bfloat16), "fsdp", scatter_dimension=0, tiled=True
        ).astype(jnp.float32),
        lax.psum_scatter(
            weight_grads[4].astype(jnp.bfloat16), "fsdp", scatter_dimension=0, tiled=True
        ).astype(jnp.float32),
        lax.psum_scatter(
            weight_grads[5].astype(jnp.bfloat16), "fsdp", scatter_dimension=0, tiled=True
        ).astype(jnp.float32),
        lax.psum_scatter(
            weight_grads[6].astype(jnp.bfloat16), "fsdp", scatter_dimension=0, tiled=True
        ).astype(jnp.float32),
    )
    shares = (
        lax.psum_scatter(spread[0], "ctx", scatter_dimension=1, tiled=True),
        lax.psum_scatter(spread[1], "ctx", scatter_dimension=1, tiled=True),
        lax.psum_scatter(spread[2], "ctx", scatter_dimension=1, tiled=True),
        lax.psum_scatter(spread[3], "ctx", scatter_dimension=1, tiled=True),
        lax.psum_scatter(spread[4], "ctx", scatter_dimension=1, tiled=True),
        lax.psum_scatter(spread[5], "ctx", scatter_dimension=1, tiled=True),
        lax.psum_scatter(spread[6], "ctx", scatter_dimension=1, tiled=True),
    )
    return (
        output,
        d_tokens,
        gain_totals[0],
        shares[0],
        shares[1],
        shares[2],
        gain_totals[2],
        gain_totals[3],
        shares[3],
        gain_totals[1],
        shares[4],
        shares[5],
        shares[6],
    )


def solution(mesh):
    in_specs = (
        P("fsdp", "ctx", None),
        P("fsdp", "ctx"),
        P("fsdp", "ctx"),
        P(),
        P("fsdp", None),
        P("fsdp", None),
        P("fsdp", None),
        P(),
        P(),
        P("fsdp", None),
        P(),
        P("fsdp", None),
        P("fsdp", None),
        P("fsdp", None),
        P("fsdp", "ctx", None),
    )
    out_specs = (
        P("fsdp", "ctx", None),
        P("fsdp", "ctx", None),
        P(),
        P("fsdp", "ctx"),
        P("fsdp", "ctx"),
        P("fsdp", "ctx"),
        P(),
        P(),
        P("fsdp", "ctx"),
        P(),
        P("fsdp", "ctx"),
        P("fsdp", "ctx"),
        P("fsdp", "ctx"),
    )
    return jax.shard_map(body, mesh=mesh, in_specs=in_specs, out_specs=out_specs, check_vma=False)
```

profile of v0, /device:TPU:15, one launch (start us, length us, event | category | flops | bytes accessed | tf_op | source)
XLA Modules:
  0.0 1542.1 jit_solution(17260667860843081421)
XLA Ops:
  85.9 5.9 collective-permute-start.3
  153.4 67.1 %while.30 = (s32[]{:T(128)}, bf16[8,256,128]{1,2,0:T(8,128)(2,1)S(1)}, f32[8,2,256]{2,1,0:T(2,128)S(1)}, s32[8]{0:T(128)S(1)}, bf16[2304,512]{0,1:T(8,128)(2,1)}...) while((s32[]{:T(128)}, ...), condition=%wide.region_6.7_spmd.clone.clone, body=%wide.region_3.6_spmd.clone.sunk.clone | while | flops 312606208 | bytes 16357897 | solution.py:164
  224.0 8.1 fusion.106
  232.1 8.0 fusion.107
  240.0 13.3 multiply_convert_fusion.1
  253.3 7.2 fusion.108
  267.5 178.0 %while.31 = (s32[]{:T(128)}, f32[8,256,128]{1,2,0:T(8,128)}, f32[8,2304,64]{1,2,0:T(8,128)}, f32[8,2304,64]{1,2,0:T(8,128)}, s32[8]{0:T(128)S(1)}, /*index=5*/bf...) while((s32[]{:T(128)}, f32[8,256,128]{1,2,0:T(8,128)}, ...), condition=%wide.region_11.12_spmd.clone.clone, body=%wide.region_9.11_spmd.clone.sunk.clone | while | flops 768130560 | bytes 53871216 | solution.py:219
  457.8 7.0 collective-permute-done.25
  466.8 7.0 collective-permute-done.26
  497.2 7.0 collective-permute-done.29
  535.9 10.1 collective-permute-done.37
  549.0 8.5 collective-permute-done.38
  559.5 9.0 collective-permute-done.39
  577.9 6.7 convolution_convert_fusion.2
  584.7 6.7 convolution_convert_fusion.1
  592.4 7.0 convolution_convert_fusion
  604.2 9.5 reduce-scatter.29.cloned.1.call-done
  616.4 10.4 reduce-scatter.35.cloned.1.call-done
  629.5 18.6 %reduce-scatter.37.cloned.1.call-done = bf16[512,4608]{1,0:T(8,128)(2,1)} async-done(((bf16[1024,4608]{1,0:T(8,128)(2,1)}), bf16[512,4608]{1,0:T(8,128)(2,1)}) %reduce-scatter.37.cloned.1.call-update) | async-done | bytes 4718608 | tf_op jit(solution)/shard_map/reduce_scatter | solution.py:280
  648.1 7.4 copy.72
  655.5 13.9 reduce-scatter.39.cloned.1.call-done
  669.5 7.4 copy.74
  677.3 13.5 reduce-scatter.41.cloned.1.call-done
  690.8 7.5 copy.76
  703.7 7.2 fusion.48
  712.9 40.0 %all-reduce = (f32[1024]{0:T(1024)}, f32[64]{0:T(128)}, f32[64]{0:T(128)}, f32[1024]{0:T(1024)}) all-reduce(f32[1024]{0:T(1024)S(1)} %get-tuple-element.270, f32[64]{0:T(128)S(1)} %multiply_reduce_fusion.2, f32[64]{0:T(128)S(1)} %multiply_reduce_fusion.6, ...), channel_id=1, replica_groups=mesh['ctx'=16,'fsdp'=2] {'ctx','fsdp'}, use_global_device_ids=true, to_apply=%region_16.17 | all-reduce | flops 2176 | bytes 17408 | tf_op jit(solution)/shard_map/psum | solution.py:249
  754.2 69.3 %reduce-scatter.47.cloned.1.call-done = f32[32,512]{1,0:T(8,128)} async-done(((f32[512,512]{1,0:T(8,128)}), f32[32,512]{1,0:T(8,128)}) %reduce-scatter.47.cloned.1.call-update) | async-done | bytes 65552
  823.5 82.7 %reduce-scatter.43.cloned.1.call-done = f32[64,512]{1,0:T(8,128)} async-done(((f32[1024,512]{1,0:T(8,128)}), f32[64,512]{1,0:T(8,128)}) %reduce-scatter.43.cloned.1.call-update) | async-done | bytes 131088
  906.2 79.9 %reduce-scatter.49.cloned.1.call-done = f32[64,512]{1,0:T(8,128)} async-done(((f32[1024,512]{1,0:T(8,128)}), f32[64,512]{1,0:T(8,128)}) %reduce-scatter.49.cloned.1.call-update) | async-done | bytes 131088
  986.1 195.3 %reduce-scatter.51.cloned.1.call-done = f32[288,512]{1,0:T(8,128)} async-done(((f32[4608,512]{1,0:T(8,128)}), f32[288,512]{1,0:T(8,128)}) %reduce-scatter.51.cloned.1.call-update) | async-done | bytes 589840
  1181.4 177.1 %reduce-scatter.53.cloned.1.call-done = f32[288,512]{1,0:T(8,128)} async-done(((f32[4608,512]{1,0:T(8,128)}), f32[288,512]{1,0:T(8,128)}) %reduce-scatter.53.cloned.1.call-update) | async-done | bytes 589840
  1358.5 176.3 %reduce-scatter.55.cloned.1.call-done = f32[64,2304]{1,0:T(8,128)} async-done(((f32[1024,2304]{1,0:T(8,128)}), f32[64,2304]{1,0:T(8,128)}) %reduce-scatter.55.cloned.1.call-update) | async-done | bytes 589840
  (520 shorter events, 461.3 us)
Async XLA Ops:
  7.2 43.9 %all-gather.8.cloned.1.call-start = ((), (), s32[]{:S(2)}) async-start(), calls=%async_computation.14 | async-start | bytes 1572864 | tf_op jit(solution)/shard_map/all_gather | solution.py:97
  7.9 47.8 %all-gather.10.cloned.1.call-start = ((), (), s32[]{:S(2)}) async-start(), calls=%async_computation.15 | async-start | bytes 1572864 | tf_op jit(solution)/shard_map/all_gather | solution.py:96
  8.7 87.8 %all-gather.12.cloned.1.call-start = ((), (), s32[]{:S(2)}) async-start(), calls=%async_computation.16 | async-start | bytes 3145728 | tf_op jit(solution)/shard_map/all_gather | solution.py:95
  9.4 211.2 %all-gather.14.cloned.1.call-start = ((), (), s32[]{:S(2)}) async-start(), calls=%async_computation.17 | async-start | bytes 3145728 | tf_op jit(solution)/shard_map/all_gather | solution.py:98
  10.0 214.0 %all-gather.16.cloned.1.call-start = ((), (), s32[]{:S(2)}) async-start(), calls=%async_computation.18 | async-start | bytes 14155776 | tf_op jit(solution)/shard_map/all_gather | solution.py:101
  10.6 221.5 %all-gather.18.cloned.1.call-start = ((), (), s32[]{:S(2)}) async-start(), calls=%async_computation.19 | async-start | bytes 14155776 | tf_op jit(solution)/shard_map/all_gather | solution.py:102
  11.1 228.9 %all-gather.20.cloned.1.call-start = ((), (), s32[]{:S(2)}) async-start(), calls=%async_computation.20 | async-start | bytes 14155776 | tf_op jit(solution)/shard_map/all_gather | solution.py:103
  14.5 584.9 %reduce-scatter.31.cloned.1.call-start = ((), (), s32[]{:S(2)}) async-start(), calls=%async_computation.22 | async-start | bytes 1572864 | tf_op jit(solution)/shard_map/reduce_scatter | solution.py:271
  45.7 14.3 collective-permute-start.14
  80.5 12.0 collective-permute-start.18
  85.9 17.8 %collective-permute-start.3 = (bf16[256,512]{1,0:T(8,128)(2,1)S(1)}, bf16[256,512]{1,0:T(8,128)(2,1)S(1)}, u32[]{:S(2)}, u32[]{:S(2)}) collective-permute-start(bf16[256,512]{1,0:T(8,128)(2,1)S(1)} %collective-permute-done.2), channel_id=1, source_target_pairs={{0,2},{2,4},{4,6},{6,8},{8,10},{10,12},{12,14},{14,16},{16,18},{18... | collective-permute-start | bytes 786440 | tf_op jit(solution)/shard_map/ppermute | solution.py:20
  92.5 13.4 collective-permute-start.19
  122.5 12.3 collective-permute-start.6
  129.1 12.0 collective-permute-start.22
  134.8 12.7 collective-permute-start.7
  492.2 12.1 collective-permute-start.29
  495.3 12.8 collective-permute-start.34
  508.2 12.1 collective-permute-start.35
  528.4 73.4 %reduce-scatter.33.cloned.1.call-start = ((), (), s32[]{:S(2)}) async-start(), calls=%async_computation.23 | async-start | bytes 1572864 | tf_op jit(solution)/shard_map/reduce_scatter | solution.py:274
  534.0 12.0 collective-permute-start.37
  570.2 43.5 %reduce-scatter.29.cloned.1.call-start = ((), (), s32[]{:S(2)}) async-start(), calls=%async_computation.21 | async-start | bytes 3145728 | tf_op jit(solution)/shard_map/reduce_scatter | solution.py:268
  575.7 51.2 %reduce-scatter.35.cloned.1.call-start = ((), (), s32[]{:S(2)}) async-start(), calls=%async_computation.24 | async-start | bytes 3145728 | tf_op jit(solution)/shard_map/reduce_scatter | solution.py:277
  577.8 70.2 %reduce-scatter.37.cloned.1.call-start = ((), (), s32[]{:S(2)}) async-start(), calls=%async_computation.25 | async-start | bytes 14155776 | tf_op jit(solution)/shard_map/reduce_scatter | solution.py:280
  584.6 84.9 %reduce-scatter.39.cloned.1.call-start = ((), (), s32[]{:S(2)}) async-start(), calls=%async_computation.26 | async-start | bytes 14155776 | tf_op jit(solution)/shard_map/reduce_scatter | solution.py:283
  591.4 99.4 %reduce-scatter.41.cloned.1.call-start = ((), (), s32[]{:S(2)}) async-start(), calls=%async_computation.27 | async-start | bytes 14155776 | tf_op jit(solution)/shard_map/reduce_scatter | solution.py:286
  599.4 154.8 %reduce-scatter.45.cloned.1.call-start = ((), (), s32[]{:S(2)}) async-start(), calls=%async_computation.29 | async-start | bytes 1114112
  601.8 221.7 %reduce-scatter.47.cloned.1.call-start = ((), (), s32[]{:S(2)}) async-start(), calls=%async_computation.30 | async-start | bytes 1114112
  604.1 302.1 %reduce-scatter.43.cloned.1.call-start = ((), (), s32[]{:S(2)}) async-start(), calls=%async_computation.28 | async-start | bytes 2228224
  616.3 369.7 %reduce-scatter.49.cloned.1.call-start = ((), (), s32[]{:S(2)}) async-start(), calls=%async_computation.31 | async-start | bytes 2228224
  629.4 551.9 %reduce-scatter.51.cloned.1.call-start = ((), (), s32[]{:S(2)}) async-start(), calls=%async_computation.32 | async-start | bytes 10027008
  655.5 703.0 %reduce-scatter.53.cloned.1.call-start = ((), (), s32[]{:S(2)}) async-start(), calls=%async_computation.33 | async-start | bytes 10027008
  677.0 857.8 %reduce-scatter.55.cloned.1.call-start = ((), (), s32[]{:S(2)}) async-start(), calls=%async_computation.34 | async-start | bytes 10027008
  (86 other events, 687.6 us)
Sparse Core Ops, SparseCore 0:
  9.6 10.9 all-gather.7
  22.1 10.1 all-gather.9
  33.8 11.7 all-gather.11
  46.9 11.7 all-gather.13
  60.1 23.0 all-gather.15
  84.6 23.0 all-gather.17
  109.2 23.0 all-gather.19
  528.6 30.9 reduce-scatter.30
  570.3 30.4 reduce-scatter.32
  602.9 10.7 reduce-scatter.28
  616.0 10.7 reduce-scatter.34
  629.0 19.0 reduce-scatter.36
  650.4 19.0 reduce-scatter.38
  671.6 19.0 reduce-scatter.40
  693.5 53.5 reduce-scatter.44
  749.9 73.5 reduce-scatter.46
  826.2 79.9 reduce-scatter.42
  908.9 77.1 reduce-scatter.48
  992.3 189.0 reduce-scatter.50
  1188.4 169.9 reduce-scatter.52
  1364.7 169.9 reduce-scatter.54
where the time goes:
time: 1550 us; the launch traced here: 1540 us
  waiting for transfers between devices  941 us (61%)
  matrix products  218 us (14%)
  starting transfers between devices  131 us (8%)
  local copies, waits for them, and re-layouts  102 us (7%)
  other arithmetic  57 us (4%)
  blocking collectives  40 us (3%)
  loops' own time  37.3 us (2%)
  between operations  16.1 us (1%)
    unnamed x28, waiting for transfers between devices  784 us
    ppermute x40, starting transfers between devices, from_behind(): return lax.ppermute(block, axis, route)  130 us
    ppermute x40, waiting for transfers between devices, from_behind(): return lax.ppermute(block, axis, route)  90.4 us
    unnamed x113, local copies, waits for them, and re-layouts  56.7 us
    dot_general x16, matrix products, group_scores(): jnp.einsum('trd,kd->rtk', query_part, key_part, preferred_element_type=jn...  48.9 us
    psum x1, blocking collectives, body(): lax.psum((jnp.sum(attn_terms, axis=0), jnp.sum(ffn_terms, axis=0), jnp.su...  40 us
    and x16, other arithmetic, body(): (seg_local[:, None] == seg_all[None, :]) & (key_index[None, :] <= query_i...  34.7 us
  transfers between devices with their start and end apart: 61, of which 35 were waited for; matrix products, arithmetic and copies ran while one was open for 12% of the time, Pallas kernels for 0%

commit v1 on v0

--- a/solution.py
+++ b/solution.py
@@ -1,6 +1,10 @@
+import functools
+
 import jax
 import jax.numpy as jnp
 from jax import lax
+from jax.experimental import pallas as pl
+from jax.experimental.pallas import tpu as pltpu
 from jax.sharding import PartitionSpec as P
 
 HEADS = 16
@@ -66,7 +70,7 @@
     )
 
 
-def body(
+def ring_body(
     tokens,
     seg_ids,
     doc_pos,
@@ -313,6 +317,598 @@
     )
 
 
+MESH = pl.DeviceIdType.MESH
+BLOCK = 256
+RING = 16
+VMEM_SPEC = pl.BlockSpec(memory_space=pltpu.VMEM)
+SMEM_SPEC = pl.BlockSpec(memory_space=pltpu.SMEM)
+F32 = jnp.float32
+BF16 = jnp.bfloat16
+
+
+def dot_dims(left_mat, right_mat, left_dim, right_dim):
+    return lax.dot_general(
+        left_mat, right_mat, (((left_dim,), (right_dim,)), ((), ())), preferred_element_type=F32
+    )
+
+
+def exchange_kernel(src, dst, own_sem, send_sem, recv_sem):
+    place, core = lax.axis_index("ctx"), lax.axis_index("fsdp")
+    barrier = pltpu.get_barrier_semaphore()
+    for step in range(1, RING):
+        peer = lax.rem(place + step, RING)
+        pl.semaphore_signal(barrier, inc=1, device_id=(peer, core), device_id_type=MESH)
+    own = pltpu.make_async_copy(src.at[place], dst.at[place], own_sem)
+    own.start()
+    pl.semaphore_wait(barrier, RING - 1)
+    copies = []
+    for step in range(1, RING):
+        peer = lax.rem(place + step, RING)
+        copy = pltpu.make_async_remote_copy(
+            src_ref=src.at[peer],
+            dst_ref=dst.at[place],
+            send_sem=send_sem.at[step],
+            recv_sem=recv_sem.at[step],
+            device_id=(peer, core),
+            device_id_type=MESH,
+        )
+        copy.start()
+        copies.append(copy)
+    own.wait()
+    for copy in copies:
+        copy.wait()
+
+
+def exchange(blocks, call_id):
+    return pl.pallas_call(
+        exchange_kernel,
+        out_shape=jax.ShapeDtypeStruct(blocks.shape, blocks.dtype),
+        in_specs=[VMEM_SPEC],
+        out_specs=VMEM_SPEC,
+        scratch_shapes=[
+            pltpu.SemaphoreType.DMA,
+            pltpu.SemaphoreType.DMA((RING,)),
+            pltpu.SemaphoreType.DMA((RING,)),
+        ],
+        compiler_params=pltpu.CompilerParams(collective_id=call_id, has_side_effects=True),
+        name="exchange_heads",
+    )(blocks)
+
+
+def transposed(block):
+    return block.astype(F32).T.astype(BF16)
+
+
+def block_probs(key_nat, query_t, first_key, start, query_place, diagonal, masked):
+    scores = jnp.dot(key_nat, query_t, preferred_element_type=F32)
+    probs = jnp.exp(scores)
+    if masked:
+        key_place = first_key + lax.broadcasted_iota(jnp.int32, probs.shape, 0)
+        ok = key_place >= start
+        if diagonal:
+            ok = ok & (key_place <= query_place)
+        probs = jnp.where(ok, probs, 0.0)
+    return probs
+
+
+def attend_kernel(first_ref, clear_ref, qkv_ref, start_ref, mixed_ref, inv_ref, key_nat):
+    blocks = qkv_ref.shape[0]
+
+    def turn(j, carry):
+        key_nat[j] = transposed(qkv_ref[j, HEAD_DIM : 2 * HEAD_DIM, :])
+        return carry
+
+    lax.fori_loop(0, blocks, turn, 0)
+
+    def per_query(i, nothing):
+        query_t = qkv_ref[i, 0:HEAD_DIM, :] * jnp.asarray(HEAD_DIM**-0.5, BF16)
+        start = start_ref[i]
+        query_place = i * BLOCK + lax.broadcasted_iota(jnp.int32, (1, BLOCK), 1)
+
+        def step(diagonal, masked, j, carry):
+            total, acc = carry
+            probs = block_probs(
+                key_nat[j], query_t, j * BLOCK, start, query_place, diagonal, masked
+            )
+            total = total + jnp.sum(probs, axis=0, keepdims=True)
+            acc = acc + jnp.dot(
+                qkv_ref[j, 2 * HEAD_DIM : 3 * HEAD_DIM, :],
+                probs.astype(BF16),
+                preferred_element_type=F32,
+            )
+            return total, acc
+
+        carry = (jnp.zeros((1, BLOCK), F32), jnp.zeros((HEAD_DIM, BLOCK), F32))
+        carry = lax.fori_loop(
+            first_ref[i], clear_ref[i], functools.partial(step, False, True), carry
+        )
+        carry = lax.fori_loop(clear_ref[i], i, functools.partial(step, False, False), carry)
+        total, acc = step(True, True, i, carry)
+        inverse = 1.0 / total
+        mixed_ref[i] = (acc * inverse).astype(BF16)
+        inv_ref[i] = inverse
+        return nothing
+
+    lax.fori_loop(0, blocks, per_query, 0)
+
+
+def attend(first, clear, qkv, start):
+    blocks = qkv.shape[0]
+    return pl.pallas_call(
+        attend_kernel,
+        out_shape=(
+            jax.ShapeDtypeStruct((blocks, HEAD_DIM, BLOCK), BF16),
+            jax.ShapeDtypeStruct((blocks, 1, BLOCK), F32),
+        ),
+        in_specs=[SMEM_SPEC, SMEM_SPEC, VMEM_SPEC, VMEM_SPEC],
+        out_specs=(VMEM_SPEC, VMEM_SPEC),
+        scratch_shapes=[pltpu.VMEM((blocks, BLOCK, HEAD_DIM), BF16)],
+        name="attend_forward",
+    )(first, clear, qkv, start)
+
+
+def attend_back_kernel(
+    first_ref,
+    clear_ref,
+    qkv_ref,
+    start_ref,
+    mixed_ref,
+    inv_ref,
+    cot_ref,
+    out_ref,
+    key_nat,
+    value_nat,
+    key_acc,
+    value_acc,
+):
+    blocks = qkv_ref.shape[0]
+    scale = HEAD_DIM**-0.5
+
+    def turn(j, carry):
+        key_nat[j] = transposed(qkv_ref[j, HEAD_DIM : 2 * HEAD_DIM, :])
+        value_nat[j] = transposed(qkv_ref[j, 2 * HEAD_DIM : 3 * HEAD_DIM, :])
+        key_acc[j] = jnp.zeros((BLOCK, HEAD_DIM), F32)
+        value_acc[j] = jnp.zeros((BLOCK, HEAD_DIM), F32)
+        return carry
+
+    lax.fori_loop(0, blocks, turn, 0)
+
+    def per_query(i, nothing):
+        query_t = qkv_ref[i, 0:HEAD_DIM, :] * jnp.asarray(scale, BF16)
+        query_nat = transposed(query_t)
+        cot_t = cot_ref[i]
+        cot_nat = transposed(cot_t)
+        start = start_ref[i]
+        inverse = inv_ref[i]
+        delta = jnp.sum(
+            cot_t.astype(F32) * mixed_ref[i].astype(F32), axis=0, keepdims=True
+        )
+        query_place = i * BLOCK + lax.broadcasted_iota(jnp.int32, (1, BLOCK), 1)
+
+        def step(diagonal, masked, j, acc):
+            probs = (
+                block_probs(key_nat[j], query_t, j * BLOCK, start, query_place, diagonal, masked)
+                * inverse
+            )
+            grad_probs = jnp.dot(value_nat[j], cot_t, preferred_element_type=F32)
+            grad_scores = (probs * (grad_probs - delta)).astype(BF16)
+            value_acc[j] += jnp.dot(probs.astype(BF16), cot_nat, preferred_element_type=F32)
+            key_acc[j] += jnp.dot(grad_scores, query_nat, preferred_element_type=F32)
+            return acc + jnp.dot(
+                qkv_ref[j, HEAD_DIM : 2 * HEAD_DIM, :], grad_scores, preferred_element_type=F32
+            )
+
+        acc = jnp.zeros((HEAD_DIM, BLOCK), F32)
+        acc = lax.fori_loop(first_ref[i], clear_ref[i], functools.partial(step, False, True), acc)
+        acc = lax.fori_loop(clear_ref[i], i, functools.partial(step, False, False), acc)
+        acc = step(True, True, i, acc)
+        out_ref[i, 0:HEAD_DIM, :] = (acc * scale).astype(BF16)
+        return nothing
+
+    lax.fori_loop(0, blocks, per_query, 0)
+
+    def flush(j, carry):
+        out_ref[j, HEAD_DIM : 2 * HEAD_DIM, :] = key_acc[j].T.astype(BF16)
+        out_ref[j, 2 * HEAD_DIM : 3 * HEAD_DIM, :] = value_acc[j].T.astype(BF16)
+        return carry
+
+    lax.fori_loop(0, blocks, flush, 0)
+
+
+def attend_back(first, clear, qkv, start, mixed, inverse, cot):
+    blocks = qkv.shape[0]
+    return pl.pallas_call(
+        attend_back_kernel,
+        out_shape=jax.ShapeDtypeStruct(qkv.shape, BF16),
+        in_specs=[SMEM_SPEC, SMEM_SPEC] + [VMEM_SPEC] * 5,
+        out_specs=VMEM_SPEC,
+        scratch_shapes=[
+            pltpu.VMEM((blocks, BLOCK, HEAD_DIM), BF16),
+            pltpu.VMEM((blocks, BLOCK, HEAD_DIM), BF16),
+            pltpu.VMEM((blocks, BLOCK, HEAD_DIM), F32),
+            pltpu.VMEM((blocks, BLOCK, HEAD_DIM), F32),
+        ],
+        name="attend_backward",
+    )(first, clear, qkv, start, mixed, inverse, cot)
+
+
+def spread_kernel(parts, rows, n_in, n_out, *refs):
+    inputs, outputs, scratch = refs[:n_in], refs[n_in : n_in + n_out], refs[n_in + n_out :]
+    sent = (scratch[0:3], scratch[3:6])
+    came = (scratch[6:9], scratch[9:12])
+    send_sems, recv_sems = scratch[12], scratch[13]
+    compute, finish = parts
+    place, core = lax.axis_index("ctx"), lax.axis_index("fsdp")
+    x, y, z = lax.rem(place, 2), lax.rem(place // 2, 2), place // 4
+
+    def at(chain, first, second, depth):
+        if chain == 0:
+            return depth * 4 + second * 2 + first
+        return depth * 4 + first * 2 + second
+
+    coords = ((x, y), (y, x))
+    barrier = pltpu.get_barrier_semaphore()
+    peers = [at(0, 1 - x, y, z), at(0, x, 1 - y, z)]
+    peers += [at(0, x, y, lax.rem(z + step, 4)) for step in range(1, 4)]
+    for peer in peers:
+        pl.semaphore_signal(barrier, inc=1, device_id=(peer, core), device_id_type=MESH)
+    pl.semaphore_wait(barrier, len(peers))
+
+    def copy(chain, stage, slot, sem, peer):
+        return pltpu.make_async_remote_copy(
+            src_ref=sent[chain][stage].at[slot],
+            dst_ref=came[chain][stage].at[slot],
+            send_sem=send_sems.at[chain, sem],
+            recv_sem=recv_sems.at[chain, sem],
+            device_id=(peer, core),
+            device_id_type=MESH,
+        )
+
+    def one(index, nothing):
+        turned = 1 - index // 4
+        depth = lax.rem(index + 1, 4)
+        slot = turned * 4 + depth
+        for chain in range(2):
+            first, second = coords[chain]
+            other = second + turned - 2 * second * turned
+            owner = at(chain, 1 - first, other, lax.rem(z + depth, 4))
+            for row, value in compute(chain, owner, inputs):
+                sent[chain][0][slot, row : row + value.shape[0], :] = value.astype(BF16)
+            copy(chain, 0, slot, slot, at(chain, 1 - first, second, z)).start()
+        return nothing
+
+    lax.fori_loop(0, 8, one, 0)
+
+    def two(index, nothing):
+        depth = lax.rem(index + 1, 4)
+        for chain in range(2):
+            first, second = coords[chain]
+            copy(chain, 0, 4 + depth, 4 + depth, at(chain, 1 - first, second, z)).wait_recv()
+            owner = at(chain, first, 1 - second, lax.rem(z + depth, 4))
+            for row, value in compute(chain, owner, inputs):
+                window = slice(row, row + value.shape[0])
+                value = value + came[chain][0][4 + depth, window, :].astype(F32)
+                sent[chain][1][depth, window, :] = value.astype(BF16)
+            copy(chain, 1, depth, 8 + depth, at(chain, first, 1 - second, z)).start()
+        return nothing
+
+    lax.fori_loop(0, 4, two, 0)
+
+    def three(depth, nothing):
+        for chain in range(2):
+            first, second = coords[chain]
+            copy(chain, 0, depth, depth, at(chain, 1 - first, second, z)).wait_recv()
+            copy(chain, 1, depth, 8 + depth, at(chain, first, 1 - second, z)).wait_recv()
+            far = at(chain, first, second, lax.rem(z + depth, 4))
+            for row, value in compute(chain, far, inputs):
+                window = slice(row, row + value.shape[0])
+                value = value + came[chain][0][depth, window, :].astype(F32)
+                value = value + came[chain][1][depth, window, :].astype(F32)
+                sent[chain][2][depth - 1, window, :] = value.astype(BF16)
+            copy(chain, 2, depth - 1, 11 + depth, far).start()
+        return nothing
+
+    lax.fori_loop(1, 4, three, 0)
+
+    for chain in range(2):
+        first, second = coords[chain]
+        copy(chain, 0, 0, 0, at(chain, 1 - first, second, z)).wait_recv()
+        copy(chain, 1, 0, 8, at(chain, first, 1 - second, z)).wait_recv()
+        for depth in range(1, 4):
+            far = at(chain, first, second, lax.rem(z + depth, 4))
+            copy(chain, 2, depth - 1, 11 + depth, far).wait_recv()
+        for row, value in compute(chain, place, inputs):
+            window = slice(row, row + value.shape[0])
+            value = value + came[chain][0][0, window, :].astype(F32)
+            value = value + came[chain][1][0, window, :].astype(F32)
+            for depth in range(3):
+                value = value + came[chain][2][depth, window, :].astype(F32)
+            finish(chain, row, value, outputs)
+        for slot in range(8):
+            copy(chain, 0, slot, slot, at(chain, 1 - first, second, z)).wait_send()
+        for depth in range(4):
+            copy(chain, 1, depth, 8 + depth, at(chain, first, 1 - second, z)).wait_send()
+        for depth in range(1, 4):
+            far = at(chain, first, second, lax.rem(z + depth, 4))
+            copy(chain, 2, depth - 1, 11 + depth, far).wait_send()
+
+
+def spread_call(parts, rows, inputs, out_shape, call_id, name):
+    lanes = 256
+    buffers = [
+        pltpu.VMEM((slots, rows[chain], lanes), BF16) for chain in range(2) for slots in (8, 4, 3)
+    ]
+    return pl.pallas_call(
+        functools.partial(spread_kernel, parts, rows, len(inputs), len(out_shape)),
+        out_shape=out_shape,
+        in_specs=[VMEM_SPEC] * len(inputs),
+        out_specs=tuple([VMEM_SPEC] * len(out_shape)),
+        scratch_shapes=buffers
+        + buffers
+        + [pltpu.SemaphoreType.DMA((2, 15)), pltpu.SemaphoreType.DMA((2, 15))],
+        compiler_params=pltpu.CompilerParams(
+            collective_id=call_id, has_side_effects=True, vmem_limit_bytes=60 << 20
+        ),
+        name=name,
+    )(*inputs)
+
+
+def rows_of(ref, owner, count, base=0):
+    return ref[pl.ds(pl.multiple_of(base + owner * count, 16), count), :]
+
+
+def ffn_parts():
+    def compute(chain, owner, inputs):
+        gate_t, up_t, cot_t, mid_t, normed, hidden, mixed = inputs
+        lanes = slice(chain * 256, chain * 256 + 256)
+        width = gate_t.shape[0] // RING
+        values = [
+            (0, jnp.dot(rows_of(gate_t, owner, width), normed[:, lanes], preferred_element_type=F32)),
+            (width, jnp.dot(rows_of(up_t, owner, width), normed[:, lanes], preferred_element_type=F32)),
+        ]
+        narrow = cot_t.shape[0] // RING
+        down_rows = rows_of(cot_t, owner, narrow)
+        row = 2 * width
+        for chunk in range(5) if chain == 0 else range(5, 9):
+            piece = hidden[:, chunk * 256 : chunk * 256 + 256]
+            values.append((row, jnp.dot(down_rows, piece, preferred_element_type=F32)))
+            row += narrow
+        values.append(
+            (row, jnp.dot(rows_of(mid_t, owner, narrow), mixed[:, lanes], preferred_element_type=F32))
+        )
+        return values
+
+    def finish(chain, row, value, outputs):
+        gate, up, down, out = outputs
+        lanes = slice(chain * 256, chain * 256 + 256)
+        width = gate.shape[0]
+        narrow = down.shape[0]
+        if row < width:
+            gate[:, lanes] = value
+        elif row < 2 * width:
+            up[:, lanes] = value
+        else:
+            chunk = (row - 2 * width) // narrow
+            if chunk == (5 if chain == 0 else 4):
+                out[:, lanes] = value
+            else:
+                chunk += 5 * chain
+                down[:, chunk * 256 : chunk * 256 + 256] = value
+
+    return compute, finish
+
+
+def qkv_parts():
+    def compute(chain, owner, inputs):
+        back_t, normed = inputs
+        lanes = slice(chain * 256, chain * 256 + 256)
+        values = []
+        row, base = 0, 0
+        for count in (64, 32, 32):
+            values.append(
+                (
+                    row,
+                    jnp.dot(
+                        rows_of(back_t, owner, count, base),
+                        normed[:, lanes],
+                        preferred_element_type=F32,
+                    ),
+                )
+            )
+            row += count
+            base += count * RING
+        return values
+
+    def finish(chain, row, value, outputs):
+        outputs[0][row : row + value.shape[0], chain * 256 : chain * 256 + 256] = value
+
+    return compute, finish
+
+
+def turn_heads(values_t, positions, sign):
+    half = HEAD_DIM // 2
+    inverse_freq = THETA ** (-(2.0 / HEAD_DIM) * jnp.arange(half, dtype=F32))
+    angles = inverse_freq[:, None] * positions.astype(F32)[None, :]
+    cosine, sine = jnp.cos(angles)[None], sign * jnp.sin(angles)[None]
+    first, second = values_t[:, :half], values_t[:, half:]
+    return jnp.concatenate(
+        [first * cosine - second * sine, second * cosine + first * sine], axis=1
+    )
+
+
+def head_norm(values_t, gain):
+    mean = jnp.mean(values_t * values_t, axis=1, keepdims=True)
+    return values_t * lax.rsqrt(mean + EPSILON) * gain[None, :, None]
+
+
+def head_norm_back(values_t, gain, upstream):
+    inverse = lax.rsqrt(jnp.mean(values_t * values_t, axis=1, keepdims=True) + EPSILON)
+    scaled = upstream * gain[None, :, None]
+    d_values = (
+        inverse * scaled
+        - values_t
+        * inverse**3
+        * jnp.sum(scaled * values_t, axis=1, keepdims=True)
+        / values_t.shape[1]
+    )
+    return d_values, jnp.sum(upstream * values_t * inverse, axis=(0, 2))
+
+
+def both(block, axis):
+    return lax.all_gather(block, "fsdp", axis=axis, tiled=True)
+
+
+def heads_body(
+    tokens,
+    seg_ids,
+    doc_pos,
+    attn_gain,
+    w_query,
+    w_key,
+    w_value,
+    query_gain,
+    key_gain,
+    w_out,
+    ffn_gain,
+    w_gate,
+    w_up,
+    w_down,
+    d_output,
+):
+    place, core = lax.axis_index("ctx"), lax.axis_index("fsdp")
+    rows, width = tokens.shape[1], tokens.shape[2]
+    resid_in = tokens[0].astype(F32)
+    pos_local = doc_pos[0]
+    q_full, k_full, v_full, o_full = (
+        both(w_query, 0),
+        both(w_key, 0),
+        both(w_value, 0),
+        both(w_out, 0),
+    )
+    gate_full, up_full, down_full = both(w_gate, 0), both(w_up, 0), both(w_down, 0)
+    starts_local = place * rows + jnp.arange(rows, dtype=jnp.int32) - pos_local
+    starts = lax.all_gather(starts_local, "ctx", axis=0, tiled=False)
+    first = starts[:, 0] // BLOCK
+    own_index = jnp.arange(RING, dtype=jnp.int32)
+    clear = jnp.minimum((starts[:, -1] + BLOCK - 1) // BLOCK, own_index)
+    starts = starts[:, None, :]
+
+    normed_low = rms_norm(resid_in, attn_gain).astype(BF16)
+    query_raw = dot_dims(q_full, normed_low, 0, 1).reshape(HEADS, HEAD_DIM, rows)
+    key_raw = dot_dims(k_full, normed_low, 0, 1).reshape(KV_HEADS, HEAD_DIM, rows)
+    value_raw = dot_dims(v_full, normed_low, 0, 1).reshape(KV_HEADS, HEAD_DIM, rows)
+    query_low = turn_heads(head_norm(query_raw, query_gain), pos_local, 1.0).astype(BF16)
+    key_low = turn_heads(head_norm(key_raw, key_gain), pos_local, 1.0).astype(BF16)
+    value_low = value_raw.astype(BF16)
+    group = HEADS // KV_HEADS
+    qkv_home = jnp.concatenate(
+        [query_low, jnp.repeat(key_low, group, axis=0), jnp.repeat(value_low, group, axis=0)],
+        axis=1,
+    )
+    qkv = exchange(qkv_home, 1)
+    mixed_far, inverse_total = attend(first, clear, qkv, starts)
+    mixed_t = exchange(mixed_far, 2).reshape(HEADS * HEAD_DIM, rows)
+
+    middle = resid_in + dot_dims(mixed_t, o_full, 0, 0)
+    ffn_low = rms_norm(middle, ffn_gain).astype(BF16)
+    gate_pre = jnp.dot(ffn_low, gate_full, preferred_element_type=F32)
+    up_pre = jnp.dot(ffn_low, up_full, preferred_element_type=F32)
+    gate_sig = jax.nn.sigmoid(gate_pre)
+    gate_act = gate_pre * gate_sig
+    hidden_low = (gate_act * up_pre).astype(BF16)
+    result = middle + jnp.dot(hidden_low, down_full, preferred_element_type=F32)
+    output = result.astype(BF16)[None]
+    cot_low = d_output[0]
+    cotangent = cot_low.astype(F32)
+    grad_hidden = against(cot_low, down_full)
+    gate_back = (grad_hidden * up_pre * (gate_sig * (1.0 + gate_pre * (1.0 - gate_sig)))).astype(
+        BF16
+    )
+    up_back = (grad_hidden * gate_act).astype(BF16)
+    grad_ffn_in = against(gate_back, gate_full) + against(up_back, up_full)
+    middle_part, ffn_terms = rms_back(middle, ffn_gain, grad_ffn_in)
+    grad_middle = cotangent + middle_part
+    middle_low = grad_middle.astype(BF16)
+    grad_mixed = dot_dims(o_full, middle_low, 1, 1).astype(BF16)
+
+    cot_far = exchange(grad_mixed.reshape(HEADS, HEAD_DIM, rows), 3)
+    back_far = attend_back(first, clear, qkv, starts, mixed_far, inverse_total, cot_far)
+    back_home = exchange(back_far, 4).astype(F32)
+
+    def half_of(block):
+        gathered = both(block, 0)
+        part = gathered.shape[1] // 2
+        return lax.dynamic_slice_in_dim(gathered, core * part, part, 1)
+
+    wide = gate_back.shape[1] // RING
+    narrow = width // RING
+    grads_t = spread_call(
+        ffn_parts(),
+        (2 * wide + 6 * narrow, 2 * wide + 5 * narrow),
+        (
+            both(gate_back.T, 1),
+            both(up_back.T, 1),
+            both(cot_low.T, 1),
+            both(middle_low.T, 1),
+            half_of(ffn_low),
+            half_of(hidden_low),
+            half_of(mixed_t.T),
+        ),
+        (
+            jax.ShapeDtypeStruct((wide, width // 2), F32),
+            jax.ShapeDtypeStruct((wide, width // 2), F32),
+            jax.ShapeDtypeStruct((narrow, gate_back.shape[1] // 2), F32),
+            jax.ShapeDtypeStruct((narrow, width // 2), F32),
+        ),
+        5,
+        "spread_ffn",
+    )
+
+    query_turned = turn_heads(back_home[:, :HEAD_DIM], pos_local, -1.0)
+    key_value = back_home[:, HEAD_DIM:].reshape(KV_HEADS, group, 2 * HEAD_DIM, rows).sum(axis=1)
+    key_turned = turn_heads(key_value[:, :HEAD_DIM], pos_local, -1.0)
+    query_back, query_terms = head_norm_back(query_raw, query_gain, query_turned)
+    key_back, key_terms = head_norm_back(key_raw, key_gain, key_turned)
+    query_back = query_back.astype(BF16).reshape(HEADS * HEAD_DIM, rows)
+    key_back = key_back.astype(BF16).reshape(KV_HEADS * HEAD_DIM, rows)
+    value_back = key_value[:, HEAD_DIM:].astype(BF16).reshape(KV_HEADS * HEAD_DIM, rows)
+    back_t = jnp.concatenate([query_back, key_back, value_back], axis=0)
+    (qkv_grads,) = spread_call(
+        qkv_parts(),
+        (128, 128),
+        (both(back_t, 1), half_of(normed_low)),
+        (jax.ShapeDtypeStruct((128, width // 2), F32),),
+        6,
+        "spread_qkv",
+    )
+    grad_normed = (
+        dot_dims(query_back, q_full, 0, 1)
+        + dot_dims(key_back, k_full, 0, 1)
+        + dot_dims(value_back, v_full, 0, 1)
+    )
+    input_part, attn_terms = rms_back(resid_in, attn_gain, grad_normed)
+    d_tokens = (grad_middle + input_part)[None]
+    gain_totals = lax.psum(
+        (jnp.sum(attn_terms, axis=0), jnp.sum(ffn_terms, axis=0), query_terms, key_terms),
+        ("ctx", "fsdp"),
+    )
+    return (
+        output,
+        d_tokens,
+        gain_totals[0],
+        qkv_grads[:64].T,
+        qkv_grads[64:96].T,
+        qkv_grads[96:].T,
+        gain_totals[2],
+        gain_totals[3],
+        grads_t[3].T,
+        gain_totals[1],
+        grads_t[0].T,
+        grads_t[1].T,
+        grads_t[2].T,
+    )
+
+
 def solution(mesh):
     in_specs = (
         P("fsdp", "ctx", None),
@@ -346,4 +942,5 @@
         P("fsdp", "ctx"),
         P("fsdp", "ctx"),
     )
-    return jax.shard_map(body, mesh=mesh, in_specs=in_specs, out_specs=out_specs, check_vma=False)
+    chosen = heads_body if (mesh.shape["ctx"], mesh.shape["fsdp"]) == (HEADS, 2) else ring_body
+    return jax.shard_map(chosen, mesh=mesh, in_specs=in_specs, out_specs=out_specs, check_vma=False)

time: 1550 us -> 648 us (0.42)
  waiting for transfers between devices: 941 us -> 9.43 us
  Pallas kernels: 0 us -> 397 us
  matrix products: 218 us -> 75 us
  starting transfers between devices: 131 us -> 0.8 us
  local copies, waits for them, and re-layouts: 102 us -> 49.9 us
  loops' own time: 37.3 us -> 0 us
  other arithmetic: 57 us -> 29.4 us
  blocking collectives: 40 us -> 62.1 us
    unnamed x28 -> x16, waiting for transfers between devices: 784 us -> 6.17 us
    pallas_call x0 -> x8, Pallas kernels: none -> 397 us  [the longest x2 213 us: spread_call(): pl.pallas_call(functools.partial(spread_kernel, parts, rows, len(inputs),...]
    dot_general x70 -> x11, matrix products: 189 us -> 46.7 us  [the longest x8 19 us: dot_dims(): lax.dot_general(left_mat, right_mat, (((left_dim,), (right_dim,)), ((), (...]
    ppermute x40 -> x0, starting transfers between devices: 130 us -> none  [from_behind(): return lax.ppermute(block, axis, route)]
    ppermute x40 -> x0, waiting for transfers between devices: 90.4 us -> none  [from_behind(): return lax.ppermute(block, axis, route)]
    reduce_scatter x7 -> x0, waiting for transfers between devices: 66 us -> none  [the longest x1 18.6 us: body(): lax.psum_scatter(weight_grads[4].astype(jnp.bfloat16), 'fsdp', scatter_di...]
    unnamed x113 -> x53, local copies, waits for them, and re-layouts: 56.7 us -> 9.82 us
    another operation x2 -> x0, loops' own time: 37.3 us -> none  [the longest x1 26.4 us: body(): lax.map(backward_group, jnp.arange(KV_HEADS, dtype=jnp.int32))]
  transfers between devices with their start and end apart: 61 -> 16, of which waited for: 35 -> 1; matrix products, arithmetic and copies ran while one was open for 12% -> 23% of each run, Pallas kernels for 0% -> 33%
where the time goes in v1:
time: 648 us; the launch traced here: 638 us
  Pallas kernels  397 us (61%)
  matrix products  75 us (12%)
  blocking collectives  62.1 us (10%)
  local copies, waits for them, and re-layouts  49.9 us (8%)
  other arithmetic  29.4 us (5%)
  between operations  15 us (2%)
  waiting for transfers between devices  9.43 us (1%)
    pallas_call x2, Pallas kernels, spread_call(): pl.pallas_call(functools.partial(spread_kernel, parts, rows, len(inputs),...  213 us
    pallas_call x4, Pallas kernels, exchange(): pl.pallas_call(exchange_kernel, out_shape=jax.ShapeDtypeStruct(blocks.sha...  124 us
    psum x1, blocking collectives, heads_body(): lax.psum((jnp.sum(attn_terms, axis=0), jnp.sum(ffn_terms, axis=0), query_...  40.7 us
    pallas_call x1, Pallas kernels, attend_back(): pl.pallas_call(attend_back_kernel, out_shape=jax.ShapeDtypeStruct(qkv.sha...  32.9 us
    dot_general x3, matrix products, against(): lax.dot_general(left_mat, right_mat, (((1,), (1,)), ((), ())), preferred_...  28.3 us
    pallas_call x1, Pallas kernels, attend(): pl.pallas_call(attend_kernel, out_shape=(jax.ShapeDtypeStruct((blocks, HE...  27 us
    all_gather x1, blocking collectives, heads_body(): starts = lax.all_gather(starts_local, 'ctx', axis=0, tiled=False)  21.4 us
    dot_general x8, matrix products, dot_dims(): lax.dot_general(left_mat, right_mat, (((left_dim,), (right_dim,)), ((), (...  19 us
  transfers between devices with their start and end apart: 16, of which 1 were waited for; matrix products, arithmetic and copies ran while one was open for 23% of the time, Pallas kernels for 33%

profile of v1, /device:TPU:15, one launch (start us, length us, event | category | flops | bytes accessed | tf_op | source)
XLA Modules:
  0.0 638.5 jit_solution(9028305786355125555)
XLA Ops:
  14.6 21.4 %all-gather.start_ref = s32[16,1,256]{2,1,0:T(1,128)S(1)} all-gather(s32[1,1,256]{2,1,0:T(1,128)S(1)} %get-tuple-element.65), channel_id=1, replica_groups=mesh['ctx'=16,'fsdp'=2] {'ctx'}, dimensions={0}, use_global_device_ids=true | all-gather | bytes 17408 | tf_op jit(solution)/shard_map/all_gather | solution.py:790
  42.4 3.1 all-gather.18.cloned.1.call-done
  45.6 2.6 multiply_reduce_fusion.4
  50.6 49.9 %exchange_heads.4.qkv_ref = bf16[16,192,256]{2,1,0:T(8,128)(2,1)} custom-call(bf16[16,192,256]{2,1,0:T(8,128)(2,1)} %pad_maximum_fusion.src), custom_call_target="tpu_custom_call" | custom-call | tf_op jit(solution)/shard_map/exchange_heads/pallas_call | solution.py:363
  100.5 27.0 %attend_forward.1 = (bf16[16,64,256]{2,1,0:T(8,128)(2,1)}, f32[16,1,256]{2,1,0:T(1,128)}) custom-call(s32[16]{0:T(128)} %get-tuple-element.76.first_ref, s32[16]{0:T(128)} %get-tuple-element.77.clear_ref, bf16[16,192,256]{2,1,0:T(8,128)(2,1)} %exchange_heads.4.qkv_ref, s32[16,1,256]{2,1,0:T(1,128)} %copy-done.14), custom_call_target="tpu_custom_call" | custom-call | tf_op jit(solution)/shard_map/attend_forward/pallas_call | solution.py:437
  127.5 17.0 %exchange_heads.5 = bf16[16,64,256]{2,1,0:T(8,128)(2,1)} custom-call(bf16[16,64,256]{2,1,0:T(8,128)(2,1)} %get-tuple-element.19.src.mixed_ref), custom_call_target="tpu_custom_call" | custom-call | tf_op jit(solution)/shard_map/exchange_heads/pallas_call | solution.py:363
  144.6 2.6 multiply_reduce_fusion.3
  150.9 8.9 %fusion.52 = f32[256,4608]{1,0:T(8,128)} fusion(bf16[256,1024]{1,0:T(8,128)(2,1)} %multiply_convert_fusion.7, bf16[1024,4608]{1,0:T(8,128)(2,1)} %all-gather.26.cloned.1.call-done), kind=kOutput, calls=%fused_computation.141 | convolution fusion | flops 2415919104 | bytes 14680064 | tf_op jit(solution)/shard_map/dot_general | solution.py:814
  159.8 8.7 %fusion.41 = f32[256,4608]{1,0:T(8,128)} fusion(bf16[4608,1024]{1,0:T(8,128)(2,1)} %all-gather.30.cloned.1.call-done, bf16[1,256,1024]{2,1,0:T(8,128)(2,1)} %param.28), kind=kOutput, calls=%fused_computation.85 | convolution fusion | flops 2415919104 | bytes 14680064 | tf_op jit(solution)/shard_map/dot_general | solution.py:68
  168.6 11.0 %multiply_convert_fusion.2 = (bf16[256,4608]{1,0:T(8,128)(2,1)}, f32[256,4608]{1,0:T(8,128)}) fusion(f32[256,4608]{1,0:T(8,128)} %fusion.52, bf16[256,1024]{1,0:T(8,128)(2,1)} %multiply_convert_fusion.7, bf16[1024,4608]{1,0:T(8,128)(2,1)} %all-gather.28.cloned.1.call-done), kind=kOutput, calls=%fused_computation.17 | convolution fusion | flops 2422996992 | bytes 21757952 | tf_op jit(solution)/shard_map/dot_general | solution.py:815
  179.5 7.5 %fusion.12 = f32[256,1024]{1,0:T(8,128)} fusion(bf16[1024,4608]{1,0:T(8,128)(2,1)} %all-gather.28.cloned.1.call-done, f32[256,4608]{1,0:T(8,128)S(1)} %copy-done.8, f32[256,4608]{1,0:T(8,128)S(1)} %copy-done), kind=kOutput, calls=%fused_computation.20 | convolution fusion | flops 2422996992 | bytes 19922944 | tf_op jit(solution)/shard_map/dot_general | solution.py:68
  187.0 12.1 %multiply_reduce_fusion = (f32[1024]{0:T(1024)}, f32[256]{0:T(256)S(1)}, f32[256,1024]{1,0:T(8,128)}) fusion(f32[256,1024]{1,0:T(8,128)S(1)} %get-tuple-element.71, f32[256]{0:T(256)S(1)} %get-tuple-element.63, f32[1024]{0:T(1024)S(1)} %copy-done.17, f32[256,1024]{1,0:T(8,128)} %fusion.12, bf16[1024,4608]{1,0:T(8,128)(2,1)} %all-gather.26.cloned.1.call-done, ...), kind=kOutput, calls=%fused_computation.63 | convolution fusion | flops 2429549312 | bytes 26748928 | tf_op jit(solution)/shard_map/dot_general | solution.py:68
  199.2 3.0 convert_bitcast_fusion
  202.2 3.1 fusion.16
  205.3 2.1 copy.60
  207.4 16.7 %exchange_heads.6.cot_ref = bf16[16,64,256]{2,1,0:T(8,128)(2,1)} custom-call(bf16[16,64,256]{2,1,0:T(8,128)(2,1)} %bitcast.183), custom_call_target="tpu_custom_call" | custom-call | tf_op jit(solution)/shard_map/exchange_heads/pallas_call | solution.py:363
  224.1 32.9 %attend_backward.1.src = bf16[16,192,256]{2,1,0:T(8,128)(2,1)} custom-call(s32[16]{0:T(128)} %get-tuple-element.76.first_ref, s32[16]{0:T(128)} %get-tuple-element.77.clear_ref, bf16[16,192,256]{2,1,0:T(8,128)(2,1)} %exchange_heads.4.qkv_ref, s32[16,1,256]{2,1,0:T(1,128)} %copy-done.14, bf16[16,64,256]{2,1,0:T(8,128)(2,1)} %get-tuple-element.19.src.mixed_ref, ...), custom_call_target="tpu_custom_call" | custom-call | tf_op jit(solution)/shard_map/attend_backward/pallas_call | solution.py:520
  257.0 40.7 %exchange_heads.7 = bf16[16,192,256]{2,1,0:T(8,128)(2,1)} custom-call(bf16[16,192,256]{2,1,0:T(8,128)(2,1)} %attend_backward.1.src), custom_call_target="tpu_custom_call" | custom-call | tf_op jit(solution)/shard_map/exchange_heads/pallas_call | solution.py:363
  309.5 6.2 copy.63
  315.7 6.1 copy.61
  321.8 6.3 copy.62
  328.1 7.6 %fusion.10 = (bf16[4608,256]{1,0:T(8,128)(2,1)}, bf16[4608,256]{1,0:T(8,128)(2,1)}) fusion(f32[256,4608]{0,1:T(8,128)} %copy.63, f32[256,4608]{0,1:T(8,128)} %copy.61, f32[256,4608]{0,1:T(8,128)} %copy.62), kind=kLoop, calls=%fused_computation.13 | loop fusion | flops 15335424 | bytes 18874368 | tf_op jit(solution)/shard_map/convert_element_type | solution.py:827
  336.3 2.5 copy.65.refs_2_
  344.7 2.3 fusion.53
  348.9 2.8 fusion.32
  351.7 40.7 %all-reduce = (f32[1024]{0:T(1024)}, f32[64]{0:T(128)}, f32[64]{0:T(128)}, f32[1024]{0:T(1024)}) all-reduce(f32[1024]{0:T(1024)S(1)} %get-tuple-element.27, f32[64]{0:T(128)S(1)} %reduce_sum.159, f32[64]{0:T(128)S(1)} %reduce_sum.162, f32[1024]{0:T(1024)S(1)} %copy-done.22), channel_id=1, replica_groups=mesh['ctx'=16,'fsdp'=2] {'ctx','fsdp'}, use_global_device_ids=true, to_apply=%region_10.11 | all-reduce | flops 2176 | bytes 17408 | tf_op jit(solution)/shard_map/psum | solution.py:891
  392.4 2.5 fusion.29
  395.0 7.8 %fusion.17 = bf16[1,256,1024]{2,1,0:T(8,128)(2,1)} fusion(f32[256,1024]{1,0:T(8,128)S(1)} %copy-done.5, bf16[256,4608]{1,0:T(8,128)(2,1)} %get-tuple-element.72, bf16[4608,1024]{1,0:T(8,128)(2,1)} %all-gather.30.cloned.1.call-done), kind=kOutput, calls=%fused_computation.39 | convolution fusion | flops 2416443392 | bytes 13369344 | tf_op jit(solution)/shard_map/dot_general | solution.py:819
  402.8 2.3 copy.66.refs_3_
  405.0 24.3 %spread_qkv.1 = f32[128,512]{1,0:T(8,128)} custom-call(bf16[2048,512]{1,0:T(8,128)(2,1)} %all-gather.32.cloned.1.call-done.refs_0_, bf16[512,512]{1,0:T(8,128)(2,1)} %constant_dynamic-slice_fusion.3.refs_1_), custom_call_target="tpu_custom_call" | custom-call | tf_op jit(solution)/shard_map/spread_qkv/pallas_call | solution.py:641
  432.4 3.3 constant_dynamic-slice_fusion.1.refs_5_
  435.8 188.4 %spread_ffn.1 = (f32[288,512]{1,0:T(8,128)}, f32[288,512]{1,0:T(8,128)}, f32[64,2304]{1,0:T(8,128)}, f32[64,512]{1,0:T(8,128)}) custom-call(bf16[4608,512]{1,0:T(8,128)(2,1)} %all-gather.36.cloned.1.call-done.refs_0_, bf16[4608,512]{1,0:T(8,128)(2,1)} %all-gather.38.cloned.1.call-done.refs_1_, bf16[1024,512]{1,0:T(8,128)(2,1)} %copy.65.refs_2_, ...), custom_call_target="tpu_custom_call" | custom-call | tf_op jit(solution)/shard_map/spread_ffn/pallas_call | solution.py:641
  (150 shorter events, 50.1 us)
Async XLA Ops:
  7.2 29.8 %all-gather.22.cloned.1.call-start = ((), (), s32[]{:S(2)}) async-start(), calls=%async_computation.2 | async-start | bytes 1572864 | tf_op jit(solution)/shard_map/all_gather | solution.py:758
  7.9 31.0 %all-gather.20.cloned.1.call-start = ((), (), s32[]{:S(2)}) async-start(), calls=%async_computation.1 | async-start | bytes 1572864 | tf_op jit(solution)/shard_map/all_gather | solution.py:758
  8.7 36.9 %all-gather.18.cloned.1.call-start = ((), (), s32[]{:S(2)}) async-start(), calls=%async_computation | async-start | bytes 3145728 | tf_op jit(solution)/shard_map/all_gather | solution.py:758
  9.4 135.2 %all-gather.24.cloned.1.call-start = ((), (), s32[]{:S(2)}) async-start(), calls=%async_computation.3 | async-start | bytes 3145728 | tf_op jit(solution)/shard_map/all_gather | solution.py:758
  10.0 140.9 %all-gather.26.cloned.1.call-start = ((), (), s32[]{:S(2)}) async-start(), calls=%async_computation.4 | async-start | bytes 14155776 | tf_op jit(solution)/shard_map/all_gather | solution.py:758
  10.6 149.3 %all-gather.30.cloned.1.call-start = ((), (), s32[]{:S(2)}) async-start(), calls=%async_computation.6 | async-start | bytes 14155776 | tf_op jit(solution)/shard_map/all_gather | solution.py:758
  11.2 157.4 %all-gather.28.cloned.1.call-start = ((), (), s32[]{:S(2)}) async-start(), calls=%async_computation.5 | async-start | bytes 14155776 | tf_op jit(solution)/shard_map/all_gather | solution.py:758
  11.9 29.6 %copy-start.18 = (f32[64]{0:T(128)S(1)}, f32[64]{0:T(128)}, u32[]{:S(2)}) copy-start(f32[64]{0:T(128)} %param.22) | copy-start | bytes 772
  11.9 324.4 %all-gather.40.cloned.1.call-start = ((), (), s32[]{:S(2)}) async-start(), calls=%async_computation.11 | async-start | bytes 1572864 | tf_op jit(solution)/shard_map/all_gather | solution.py:758
  12.7 326.1 %all-gather.34.cloned.1.call-start = ((), (), s32[]{:S(2)}) async-start(), calls=%async_computation.8 | async-start | bytes 1572864 | tf_op jit(solution)/shard_map/all_gather | solution.py:758
  14.5 31.1 %copy-start.2 = (bf16[256,1024]{1,0:T(8,128)(2,1)S(1)}, bf16[256,1024]{1,0:T(8,128)(2,1)}, u32[]{:S(2)}) copy-start(bf16[256,1024]{1,0:T(8,128)(2,1)} %fusion.24) | copy-start | bytes 1572868
  14.5 326.2 %all-gather.44.cloned.1.call-start = ((), (), s32[]{:S(2)}) async-start(), calls=%async_computation.13 | async-start | bytes 1572864 | tf_op jit(solution)/shard_map/all_gather | solution.py:758
  36.0 12.1 %copy-start.14 = (s32[16,1,256]{2,1,0:T(1,128)}, s32[16,1,256]{2,1,0:T(1,128)S(1)}, u32[]{:S(2)}) copy-start(s32[16,1,256]{2,1,0:T(1,128)S(1)} %all-gather.start_ref) | copy-start | bytes 49156
  45.6 3.7 copy-start.13
  50.6 96.6 %copy-start.17 = (f32[1024]{0:T(1024)S(1)}, f32[1024]{0:T(1024)}, u32[]{:S(2)}) copy-start(f32[1024]{0:T(1024)} %param.24) | copy-start | bytes 12292
  100.5 47.9 %copy-start.20 = (f32[64]{0:T(128)S(1)}, f32[64]{0:T(128)}, u32[]{:S(2)}) copy-start(f32[64]{0:T(128)} %param.21) | copy-start | bytes 772
  100.5 48.0 %copy-start.19 = (f32[64]{0:T(128)S(1)}, f32[64]{0:T(128)}, u32[]{:S(2)}) copy-start(f32[64]{0:T(128)} %param.22) | copy-start | bytes 772
  147.2 39.9 %copy-start.4 = (f32[256,1024]{1,0:T(8,128)}, f32[256,1024]{1,0:T(8,128)S(1)}, u32[]{:S(2)}) copy-start(f32[256,1024]{1,0:T(8,128)S(1)} %get-tuple-element.71) | copy-start | bytes 3145732
  148.4 194.2 %all-gather.48.cloned.1.call-start = ((), (), s32[]{:S(2)}) async-start(), calls=%async_computation.15 | async-start | bytes 1572864 | tf_op jit(solution)/shard_map/all_gather | solution.py:758
  150.7 252.1 %all-gather.42.cloned.1.call-start = ((), (), s32[]{:S(2)}) async-start(), calls=%async_computation.12 | async-start | bytes 1572864 | tf_op jit(solution)/shard_map/all_gather | solution.py:758
  168.6 11.0 %copy-start = (f32[256,4608]{1,0:T(8,128)S(1)}, f32[256,4608]{1,0:T(8,128)}, u32[]{:S(2)}) copy-start(f32[256,4608]{1,0:T(8,128)} %fusion.52) | copy-start | bytes 14155780
  168.6 11.0 %copy-start.8 = (f32[256,4608]{1,0:T(8,128)S(1)}, f32[256,4608]{1,0:T(8,128)}, u32[]{:S(2)}) copy-start(f32[256,4608]{1,0:T(8,128)} %fusion.41) | copy-start | bytes 14155780
  302.3 102.8 %all-gather.32.cloned.1.call-start = ((), (), s32[]{:S(2)}) async-start(), calls=%async_computation.7 | async-start | bytes 3145728 | tf_op jit(solution)/shard_map/all_gather | solution.py:758
  302.3 3.5 copy-start.9
  308.9 123.6 %all-gather.46.cloned.1.call-start = ((), (), s32[]{:S(2)}) async-start(), calls=%async_computation.14 | async-start | bytes 7077888 | tf_op jit(solution)/shard_map/all_gather | solution.py:758
  309.4 126.3 %all-gather.36.cloned.1.call-start = ((), (), s32[]{:S(2)}) async-start(), calls=%async_computation.9 | async-start | bytes 7077888 | tf_op jit(solution)/shard_map/all_gather | solution.py:758
  335.7 9.0 %copy-start.7 = (bf16[1024,256]{1,0:T(8,128)(2,1)S(1)}, bf16[1024,256]{1,0:T(8,128)(2,1)}, u32[]{:S(2)}) copy-start(bf16[1024,256]{1,0:T(8,128)(2,1)} %copy-done.6) | copy-start | bytes 1572868
  335.7 100.1 %all-gather.38.cloned.1.call-start = ((), (), s32[]{:S(2)}) async-start(), calls=%async_computation.10 | async-start | bytes 7077888 | tf_op jit(solution)/shard_map/all_gather | solution.py:758
  336.3 10.8 %copy-start.12 = (bf16[512,256]{1,0:T(8,128)(2,1)S(1)}, bf16[512,256]{1,0:T(8,128)(2,1)}, u32[]{:S(2)}) copy-start(bf16[512,256]{1,0:T(8,128)(2,1)} %copy-done.11) | copy-start | bytes 786436
  344.7 7.0 %copy-start.22 = (f32[1024]{0:T(1024)S(1)}, f32[1024]{0:T(1024)}, u32[]{:S(2)}) copy-start(f32[1024]{0:T(1024)} %get-tuple-element.25) | copy-start | bytes 12292
  344.7 47.8 %copy-start.21 = (f32[256]{0:T(256)S(1)}, f32[256]{0:T(256)}, u32[]{:S(2)}) copy-start(f32[256]{0:T(256)} %get-tuple-element.60) | copy-start | bytes 3076
  347.0 47.9 %copy-start.5 = (f32[256,1024]{1,0:T(8,128)S(1)}, f32[256,1024]{1,0:T(8,128)}, u32[]{:S(2)}) copy-start(f32[256,1024]{1,0:T(8,128)} %copy-done.4) | copy-start | bytes 3145732
  (8 other events, 16.1 us)
Sparse Core Ops, SparseCore 0:
  9.6 10.8 all-gather.21
  22.0 10.1 all-gather.19
  33.8 11.7 all-gather.17
  46.9 11.7 all-gather.23
  60.1 23.0 all-gather.25
  84.6 23.1 all-gather.29
  109.4 23.0 all-gather.27
  134.0 10.1 all-gather.39
  146.3 10.1 all-gather.33
  158.5 10.1 all-gather.43
  170.3 10.1 all-gather.47
  302.4 11.1 all-gather.41
  315.1 11.4 all-gather.31
  328.0 15.6 all-gather.45
  345.1 14.8 all-gather.35
  361.4 14.8 all-gather.37

commit v2 on v1

--- a/solution.py
+++ b/solution.py
@@ -447,89 +447,474 @@
     )(first, clear, qkv, start)
 
 
-def attend_back_kernel(
-    first_ref,
-    clear_ref,
+def flip(bit, turned):
+    return bit + turned - 2 * bit * turned
+
+
+class Spread:
+    def __init__(self, chain, compute, sent, came, send_sems, recv_sems):
+        place, self.core = lax.axis_index("ctx"), lax.axis_index("fsdp")
+        x, y, self.z = lax.rem(place, 2), lax.rem(place // 2, 2), place // 4
+        self.chain = chain
+        self.first, self.second = (x, y) if chain == 0 else (y, x)
+        self.compute, self.sent, self.came = compute, sent, came
+        self.send_sems, self.recv_sems = send_sems, recv_sems
+
+    def at(self, first, second, depth):
+        low = second * 2 + first if self.chain == 0 else first * 2 + second
+        return depth * 4 + low
+
+    def deep(self, depth):
+        return lax.rem(self.z + depth, 4)
+
+    def copy(self, stage, slot):
+        if stage == 0:
+            peer = self.at(1 - self.first, self.second, self.z)
+            source, target, sem = self.sent.at[slot], self.came[0].at[slot], slot
+        elif stage == 1:
+            peer = self.at(self.first, 1 - self.second, self.z)
+            source, target, sem = self.came[0].at[4 + slot], self.came[1].at[slot], 8 + slot
+        else:
+            peer = self.at(self.first, self.second, self.deep(slot))
+            source, target, sem = self.came[0].at[slot], self.came[2].at[slot - 1], 11 + slot
+        return pltpu.make_async_remote_copy(
+            src_ref=source,
+            dst_ref=target,
+            send_sem=self.send_sems.at[self.chain, sem],
+            recv_sem=self.recv_sems.at[self.chain, sem],
+            device_id=(peer, self.core),
+            device_id_type=MESH,
+        )
+
+    def stage_one(self, turned, depth):
+        slot = turned * 4 + depth
+        owner = self.at(1 - self.first, flip(self.second, turned), self.deep(depth))
+        for row, value in self.compute(self.chain, owner):
+            self.sent[slot, row : row + value.shape[0], :] = value.astype(BF16)
+        self.copy(0, slot).start()
+
+    def stage_two(self, depth):
+        self.copy(0, 4 + depth).wait_recv()
+        owner = self.at(self.first, 1 - self.second, self.deep(depth))
+        for row, value in self.compute(self.chain, owner):
+            window = slice(row, row + value.shape[0])
+            value = value + self.came[0][4 + depth, window, :].astype(F32)
+            self.came[0][4 + depth, window, :] = value.astype(BF16)
+        self.copy(1, depth).start()
+
+    def stage_three(self, depth):
+        self.copy(0, depth).wait_recv()
+        self.copy(1, depth).wait_recv()
+        owner = self.at(self.first, self.second, self.deep(depth))
+        for row, value in self.compute(self.chain, owner):
+            window = slice(row, row + value.shape[0])
+            value = value + self.came[0][depth, window, :].astype(F32)
+            value = value + self.came[1][depth, window, :].astype(F32)
+            self.came[0][depth, window, :] = value.astype(BF16)
+        self.copy(2, depth).start()
+
+    def close(self, finish):
+        self.copy(0, 0).wait_recv()
+        self.copy(1, 0).wait_recv()
+        for depth in range(1, 4):
+            self.copy(2, depth).wait_recv()
+        owner = self.at(self.first, self.second, self.z)
+        for row, value in self.compute(self.chain, owner):
+            window = slice(row, row + value.shape[0])
+            value = value + self.came[0][0, window, :].astype(F32)
+            value = value + self.came[1][0, window, :].astype(F32)
+            for depth in range(3):
+                value = value + self.came[2][depth, window, :].astype(F32)
+            finish(self.chain, row, value)
+
+    def drain(self):
+        for slot in range(8):
+            self.copy(0, slot).wait_send()
+        for depth in range(4):
+            self.copy(1, depth).wait_send()
+        for depth in range(1, 4):
+            self.copy(2, depth).wait_send()
+
+
+def greet(peers):
+    barrier = pltpu.get_barrier_semaphore()
+    for peer in peers:
+        pl.semaphore_signal(barrier, inc=1, device_id=peer, device_id_type=MESH)
+    pl.semaphore_wait(barrier, len(peers))
+
+
+def turn_into(source, put):
+    for column in range(0, source.shape[1], 128):
+        put(column, source[:, column : column + 128].astype(F32).T.astype(BF16))
+
+
+def back_kernel(
+    gate_ref,
+    up_ref,
+    hidden_ref,
+    cot_ref,
+    middle_ref,
+    ffn_ref,
+    mixed_ref,
+    home_ref,
     qkv_ref,
     start_ref,
-    mixed_ref,
+    part_ref,
     inv_ref,
-    cot_ref,
-    out_ref,
-    key_nat,
-    value_nat,
-    key_acc,
-    value_acc,
+    gate_out,
+    up_out,
+    down_out,
+    out_out,
+    back_out,
+    pair_own,
+    pair_far,
+    side_own,
+    side_far,
+    hidden_far,
+    ffn_far,
+    mixed_far,
+    cot_far,
+    back_own,
+    key_value,
+    grad_acc,
+    sent_a,
+    came_a0,
+    came_a1,
+    came_a2,
+    sent_b,
+    came_b0,
+    came_b1,
+    came_b2,
+    send_sems,
+    recv_sems,
+    cot_send,
+    cot_recv,
+    back_send,
+    back_recv,
+    core_send,
+    core_recv,
 ):
+    place, core = lax.axis_index("ctx"), lax.axis_index("fsdp")
     blocks = qkv_ref.shape[0]
+    wide = pair_own.shape[1] // 2
+    narrow = side_own.shape[1] // RING
+    half_hidden = hidden_far.shape[1]
+    half_width = ffn_far.shape[1]
     scale = HEAD_DIM**-0.5
 
-    def turn(j, carry):
-        key_nat[j] = transposed(qkv_ref[j, HEAD_DIM : 2 * HEAD_DIM, :])
-        value_nat[j] = transposed(qkv_ref[j, 2 * HEAD_DIM : 3 * HEAD_DIM, :])
-        key_acc[j] = jnp.zeros((BLOCK, HEAD_DIM), F32)
-        value_acc[j] = jnp.zeros((BLOCK, HEAD_DIM), F32)
-        return carry
-
-    lax.fori_loop(0, blocks, turn, 0)
+    greet(
+        [(lax.rem(place + step, RING), core) for step in range(1, RING)] + [(place, 1 - core)]
+    )
+
+    def cot_copy(step, peer):
+        return pltpu.make_async_remote_copy(
+            src_ref=home_ref.at[peer],
+            dst_ref=cot_far.at[place],
+            send_sem=cot_send.at[step],
+            recv_sem=cot_recv.at[step],
+            device_id=(peer, core),
+            device_id_type=MESH,
+        )
+
+    for step in range(1, RING):
+        cot_copy(step, lax.rem(place + step, RING)).start()
+    cot_far[place] = home_ref[place]
+
+    def core_copy(source, target, sem):
+        return pltpu.make_async_remote_copy(
+            src_ref=source,
+            dst_ref=target,
+            send_sem=core_send.at[sem],
+            recv_sem=core_recv.at[sem],
+            device_id=(place, 1 - core),
+            device_id_type=MESH,
+        )
+
+    def half(part, size):
+        return pl.ds(pl.multiple_of(part * size, 128), size)
+
+    def pair_copy(turn_x, turn_y, depth):
+        x, y, z = lax.rem(place, 2), lax.rem(place // 2, 2), place // 4
+        owner = lax.rem(z + depth, 4) * 4 + flip(y, turn_y) * 2 + flip(x, turn_x)
+        return core_copy(
+            pair_own.at[owner], pair_far.at[owner], 4 + turn_x * 8 + turn_y * 4 + depth
+        )
+
+    sides = [
+        core_copy(ffn_ref.at[:, half(1 - core, half_width)], ffn_far, 0),
+        core_copy(mixed_ref.at[half(1 - core, half_width), :], mixed_far, 1),
+        core_copy(hidden_ref.at[:, half(1 - core, half_hidden)], hidden_far, 2),
+        core_copy(side_own, side_far, 3),
+    ]
+    for copy in sides[:3]:
+        copy.start()
+
+    def put_side(which):
+        def put(column, value):
+            side_own[which, column : column + 128, :] = value
+
+        return put
+
+    turn_into(cot_ref, put_side(0))
+    turn_into(middle_ref, put_side(1))
+    sides[3].start()
+
+    def put_pair(base):
+        def put(column, value):
+            done = 0
+            while done < 128:
+                owner, row = divmod(column + done, wide)
+                count = min(128 - done, wide - row)
+                pair_own[owner, base + row : base + row + count, :] = value[done : done + count]
+                done += count
+
+        return put
+
+    turn_into(gate_ref, put_pair(0))
+    turn_into(up_ref, put_pair(wide))
+    order = [(1, 1, depth) for depth in (1, 2, 3, 0)]
+    for depth in (1, 2, 3, 0):
+        order += [(1, 0, depth), (0, 1, depth)]
+    order += [(0, 0, depth) for depth in range(4)]
+    for turn_x, turn_y, depth in order:
+        pair_copy(turn_x, turn_y, depth).start()
+
+    def compute(chain, owner):
+        lanes = pl.ds(chain * 256, 256)
+        own_lanes = pl.ds(pl.multiple_of(core * half_width + chain * 256, 128), 256)
+        both_pair = jnp.dot(pair_own[owner], ffn_ref[:, own_lanes], preferred_element_type=F32)
+        both_pair += jnp.dot(pair_far[owner], ffn_far[:, lanes], preferred_element_type=F32)
+        values = [(0, both_pair)]
+        rows = pl.ds(pl.multiple_of(owner * narrow, 16), narrow)
+        begin, chunks = (0, 5) if chain == 0 else (5, 4)
+        cols = pl.ds(pl.multiple_of(core * half_hidden + begin * 256, 128), chunks * 256)
+        down = jnp.dot(side_own[0, rows, :], hidden_ref[:, cols], preferred_element_type=F32)
+        down += jnp.dot(
+            side_far[0, rows, :],
+            hidden_far[:, begin * 256 : (begin + chunks) * 256],
+            preferred_element_type=F32,
+        )
+        row = 2 * wide
+        for chunk in range(chunks):
+            values.append((row, down[:, chunk * 256 : chunk * 256 + 256]))
+            row += narrow
+        out = dot_dims(side_own[1, rows, :], mixed_ref[own_lanes, :], 1, 1)
+        out += dot_dims(side_far[1, rows, :], mixed_far[lanes, :], 1, 1)
+        values.append((row, out))
+        return values
+
+    def finish(chain, row, value):
+        lanes = slice(chain * 256, chain * 256 + 256)
+        if row == 0:
+            gate_out[:, lanes] = value[:wide]
+            up_out[:, lanes] = value[wide:]
+            return
+        chunk = (row - 2 * wide) // narrow
+        if chunk == 5 - chain:
+            out_out[:, lanes] = value
+        else:
+            chunk += 5 * chain
+            down_out[:, chunk * 256 : chunk * 256 + 256] = value
+
+    chains = (
+        Spread(0, compute, sent_a, (came_a0, came_a1, came_a2), send_sems, recv_sems),
+        Spread(1, compute, sent_b, (came_b0, came_b1, came_b2), send_sems, recv_sems),
+    )
+    for copy in sides:
+        copy.wait_recv()
+
+    def one_near(index, nothing):
+        depth = lax.rem(index + 1, 4)
+        pair_copy(1, 1, depth).wait_recv()
+        for chain in chains:
+            chain.stage_one(1, depth)
+        return nothing
+
+    def one_far(index, nothing):
+        depth = lax.rem(index + 1, 4)
+        pair_copy(1, 0, depth).wait_recv()
+        pair_copy(0, 1, depth).wait_recv()
+        for chain in chains:
+            chain.stage_one(0, depth)
+        return nothing
+
+    lax.fori_loop(0, 4, one_near, 0)
+    lax.fori_loop(0, 4, one_far, 0)
+
+    key_value[0] = jnp.zeros(key_value.shape[1:], BF16)
+
+    def prepare(j, nothing):
+        packed = qkv_ref[j, HEAD_DIM : 3 * HEAD_DIM, :].astype(F32)
+        key_value[j + 1] = packed.T.astype(BF16)
+        grad_acc[j + 1] = jnp.zeros(grad_acc.shape[1:], F32)
+        return nothing
+
+    grad_acc[0] = jnp.zeros(grad_acc.shape[1:], F32)
+    lax.fori_loop(0, blocks, prepare, 0)
+
+    def back_copy(step, peer):
+        return pltpu.make_async_remote_copy(
+            src_ref=back_own.at[peer],
+            dst_ref=back_out.at[place],
+            send_sem=back_send.at[step],
+            recv_sem=back_recv.at[step],
+            device_id=(peer, core),
+            device_id_type=MESH,
+        )
+
+    def flush(j):
+        turned = grad_acc[j + 1].T.astype(BF16)
+        back_own[j, HEAD_DIM : 3 * HEAD_DIM, :] = turned
+
+        @pl.when(j != place)
+        def _():
+            back_copy(lax.rem(j - place + RING, RING), j).start()
 
     def per_query(i, nothing):
-        query_t = qkv_ref[i, 0:HEAD_DIM, :] * jnp.asarray(scale, BF16)
+        @pl.when(i != place)
+        def _():
+            step = lax.rem(place - i + RING, RING)
+            cot_copy(step, lax.rem(place + step, RING)).wait_recv()
+
+        empty = jnp.zeros((HEAD_DIM, BLOCK), BF16)
+        query = qkv_ref[i, 0:HEAD_DIM, :] * jnp.asarray(scale, BF16)
+        query_t = jnp.concatenate([query, empty], axis=0)
+        cot = cot_far[i]
+        cot_t = jnp.concatenate([empty, cot], axis=0)
         query_nat = transposed(query_t)
-        cot_t = cot_ref[i]
         cot_nat = transposed(cot_t)
         start = start_ref[i]
         inverse = inv_ref[i]
-        delta = jnp.sum(
-            cot_t.astype(F32) * mixed_ref[i].astype(F32), axis=0, keepdims=True
-        )
+        delta = jnp.sum(cot.astype(F32) * part_ref[i].astype(F32), axis=0, keepdims=True)
         query_place = i * BLOCK + lax.broadcasted_iota(jnp.int32, (1, BLOCK), 1)
 
-        def step(diagonal, masked, j, acc):
-            probs = (
-                block_probs(key_nat[j], query_t, j * BLOCK, start, query_place, diagonal, masked)
-                * inverse
+        def step(diagonal, j):
+            block = key_value[j + 1]
+            scores = jnp.dot(block, query_t, preferred_element_type=F32)
+            grad_probs = jnp.dot(block, cot_t, preferred_element_type=F32)
+            key_place = j * BLOCK + lax.broadcasted_iota(jnp.int32, scores.shape, 0)
+            ok = key_place >= start
+            if diagonal:
+                ok = ok & (key_place <= query_place)
+            probs = jnp.where(ok, jnp.exp(scores) * inverse, 0.0)
+            grad_scores = (probs * (grad_probs - delta)).astype(BF16)
+            update = jnp.dot(grad_scores, query_nat, preferred_element_type=F32)
+            update += jnp.dot(probs.astype(BF16), cot_nat, preferred_element_type=F32)
+            grad_acc[j + 1] += update
+            return jnp.dot(
+                qkv_ref[jnp.maximum(j, 0), HEAD_DIM : 2 * HEAD_DIM, :],
+                grad_scores,
+                preferred_element_type=F32,
             )
-            grad_probs = jnp.dot(value_nat[j], cot_t, preferred_element_type=F32)
-            grad_scores = (probs * (grad_probs - delta)).astype(BF16)
-            value_acc[j] += jnp.dot(probs.astype(BF16), cot_nat, preferred_element_type=F32)
-            key_acc[j] += jnp.dot(grad_scores, query_nat, preferred_element_type=F32)
-            return acc + jnp.dot(
-                qkv_ref[j, HEAD_DIM : 2 * HEAD_DIM, :], grad_scores, preferred_element_type=F32
-            )
-
-        acc = jnp.zeros((HEAD_DIM, BLOCK), F32)
-        acc = lax.fori_loop(first_ref[i], clear_ref[i], functools.partial(step, False, True), acc)
-        acc = lax.fori_loop(clear_ref[i], i, functools.partial(step, False, False), acc)
-        acc = step(True, True, i, acc)
-        out_ref[i, 0:HEAD_DIM, :] = (acc * scale).astype(BF16)
+
+        pairs = (jnp.minimum(i, 8) + 1) // 2
+
+        def two(index, acc):
+            j = i - 2 * pairs + 2 * index
+            return acc + step(False, j) + step(False, j + 1)
+
+        acc = lax.fori_loop(0, pairs, two, step(True, i))
+        back_own[i, 0:HEAD_DIM, :] = (acc * scale).astype(BF16)
+
+        @pl.when(i >= 8)
+        def _():
+            flush(i - 8)
+
+        @pl.when((i >= 8) & (lax.rem(i, 2) == 0))
+        def _():
+            depth = lax.rem((i - 8) // 2 + 1, 4)
+            for chain in chains:
+                chain.stage_two(depth)
+
         return nothing
 
     lax.fori_loop(0, blocks, per_query, 0)
 
-    def flush(j, carry):
-        out_ref[j, HEAD_DIM : 2 * HEAD_DIM, :] = key_acc[j].T.astype(BF16)
-        out_ref[j, 2 * HEAD_DIM : 3 * HEAD_DIM, :] = value_acc[j].T.astype(BF16)
-        return carry
-
-    lax.fori_loop(0, blocks, flush, 0)
-
-
-def attend_back(first, clear, qkv, start, mixed, inverse, cot):
+    def rest(j, nothing):
+        flush(j)
+        return nothing
+
+    lax.fori_loop(blocks - 8, blocks, rest, 0)
+    back_out[place] = back_own[place]
+    for depth in range(4):
+        pair_copy(0, 0, depth).wait_recv()
+
+    def three(depth, nothing):
+        for chain in chains:
+            chain.stage_three(depth)
+        return nothing
+
+    lax.fori_loop(1, 4, three, 0)
+    for chain in chains:
+        chain.close(finish)
+
+    def settle(step, nothing):
+        peer = lax.rem(place + step, RING)
+        back_copy(step, peer).wait()
+        cot_copy(step, peer).wait_send()
+        return nothing
+
+    lax.fori_loop(1, RING, settle, 0)
+    for copy in sides:
+        copy.wait_send()
+    for turn_x, turn_y, depth in order:
+        pair_copy(turn_x, turn_y, depth).wait_send()
+    for chain in chains:
+        chain.drain()
+
+
+def back_call(call_id, *inputs):
+    gate_back, qkv = inputs[0], inputs[8]
+    rows, hidden_width = gate_back.shape
+    width = inputs[3].shape[1]
     blocks = qkv.shape[0]
+    wide, narrow = hidden_width // RING, width // RING
+    chain_rows = (2 * wide + 6 * narrow, 2 * wide + 5 * narrow)
+    buffers = [
+        pltpu.VMEM((slots, chain_rows[chain], 256), BF16)
+        for chain in range(2)
+        for slots in (8, 8, 4, 3)
+    ]
     return pl.pallas_call(
-        attend_back_kernel,
-        out_shape=jax.ShapeDtypeStruct(qkv.shape, BF16),
-        in_specs=[SMEM_SPEC, SMEM_SPEC] + [VMEM_SPEC] * 5,
-        out_specs=VMEM_SPEC,
+        back_kernel,
+        out_shape=(
+            jax.ShapeDtypeStruct((wide, width // 2), F32),
+            jax.ShapeDtypeStruct((wide, width // 2), F32),
+            jax.ShapeDtypeStruct((narrow, hidden_width // 2), F32),
+            jax.ShapeDtypeStruct((narrow, width // 2), F32),
+            jax.ShapeDtypeStruct(qkv.shape, BF16),
+        ),
+        in_specs=[VMEM_SPEC] * len(inputs),
+        out_specs=(VMEM_SPEC,) * 5,
         scratch_shapes=[
-            pltpu.VMEM((blocks, BLOCK, HEAD_DIM), BF16),
-            pltpu.VMEM((blocks, BLOCK, HEAD_DIM), BF16),
-            pltpu.VMEM((blocks, BLOCK, HEAD_DIM), F32),
-            pltpu.VMEM((blocks, BLOCK, HEAD_DIM), F32),
+            pltpu.VMEM((RING, 2 * wide, rows), BF16),
+            pltpu.VMEM((RING, 2 * wide, rows), BF16),
+            pltpu.VMEM((2, width, rows), BF16),
+            pltpu.VMEM((2, width, rows), BF16),
+            pltpu.VMEM((rows, hidden_width // 2), BF16),
+            pltpu.VMEM((rows, width // 2), BF16),
+            pltpu.VMEM((width // 2, rows), BF16),
+            pltpu.VMEM((blocks, HEAD_DIM, BLOCK), BF16),
+            pltpu.VMEM(qkv.shape, BF16),
+            pltpu.VMEM((blocks + 1, BLOCK, 2 * HEAD_DIM), BF16),
+            pltpu.VMEM((blocks + 1, BLOCK, 2 * HEAD_DIM), F32),
+        ]
+        + buffers
+        + [
+            pltpu.SemaphoreType.DMA((2, 15)),
+            pltpu.SemaphoreType.DMA((2, 15)),
+            pltpu.SemaphoreType.DMA((RING,)),
+            pltpu.SemaphoreType.DMA((RING,)),
+            pltpu.SemaphoreType.DMA((RING,)),
+            pltpu.SemaphoreType.DMA((RING,)),
+            pltpu.SemaphoreType.DMA((20,)),
+            pltpu.SemaphoreType.DMA((20,)),
         ],
-        name="attend_backward",
-    )(first, clear, qkv, start, mixed, inverse, cot)
+        compiler_params=pltpu.CompilerParams(
+            collective_id=call_id, has_side_effects=True, vmem_limit_bytes=63 << 20
+        ),
+        name="backward_spread",
+    )(*inputs)
 
 
 def spread_kernel(parts, rows, n_in, n_out, *refs):
@@ -655,47 +1040,6 @@
 
 def rows_of(ref, owner, count, base=0):
     return ref[pl.ds(pl.multiple_of(base + owner * count, 16), count), :]
-
-
-def ffn_parts():
-    def compute(chain, owner, inputs):
-        gate_t, up_t, cot_t, mid_t, normed, hidden, mixed = inputs
-        lanes = slice(chain * 256, chain * 256 + 256)
-        width = gate_t.shape[0] // RING
-        values = [
-            (0, jnp.dot(rows_of(gate_t, owner, width), normed[:, lanes], preferred_element_type=F32)),
-            (width, jnp.dot(rows_of(up_t, owner, width), normed[:, lanes], preferred_element_type=F32)),
-        ]
-        narrow = cot_t.shape[0] // RING
-        down_rows = rows_of(cot_t, owner, narrow)
-        row = 2 * width
-        for chunk in range(5) if chain == 0 else range(5, 9):
-            piece = hidden[:, chunk * 256 : chunk * 256 + 256]
-            values.append((row, jnp.dot(down_rows, piece, preferred_element_type=F32)))
-            row += narrow
-        values.append(
-            (row, jnp.dot(rows_of(mid_t, owner, narrow), mixed[:, lanes], preferred_element_type=F32))
-        )
-        return values
-
-    def finish(chain, row, value, outputs):
-        gate, up, down, out = outputs
-        lanes = slice(chain * 256, chain * 256 + 256)
-        width = gate.shape[0]
-        narrow = down.shape[0]
-        if row < width:
-            gate[:, lanes] = value
-        elif row < 2 * width:
-            up[:, lanes] = value
-        else:
-            chunk = (row - 2 * width) // narrow
-            if chunk == (5 if chain == 0 else 4):
-                out[:, lanes] = value
-            else:
-                chunk += 5 * chain
-                down[:, chunk * 256 : chunk * 256 + 256] = value
-
-    return compute, finish
 
 
 def qkv_parts():
@@ -831,38 +1175,27 @@
     middle_low = grad_middle.astype(BF16)
     grad_mixed = dot_dims(o_full, middle_low, 1, 1).astype(BF16)
 
-    cot_far = exchange(grad_mixed.reshape(HEADS, HEAD_DIM, rows), 3)
-    back_far = attend_back(first, clear, qkv, starts, mixed_far, inverse_total, cot_far)
-    back_home = exchange(back_far, 4).astype(F32)
+    gate_t, up_t, down_t, out_t, back_home = back_call(
+        3,
+        gate_back,
+        up_back,
+        hidden_low,
+        cot_low,
+        middle_low,
+        ffn_low,
+        mixed_t,
+        grad_mixed.reshape(HEADS, HEAD_DIM, rows),
+        qkv,
+        starts,
+        mixed_far,
+        inverse_total,
+    )
+    back_home = back_home.astype(F32)
 
     def half_of(block):
         gathered = both(block, 0)
         part = gathered.shape[1] // 2
         return lax.dynamic_slice_in_dim(gathered, core * part, part, 1)
-
-    wide = gate_back.shape[1] // RING
-    narrow = width // RING
-    grads_t = spread_call(
-        ffn_parts(),
-        (2 * wide + 6 * narrow, 2 * wide + 5 * narrow),
-        (
-            both(gate_back.T, 1),
-            both(up_back.T, 1),
-            both(cot_low.T, 1),
-            both(middle_low.T, 1),
-            half_of(ffn_low),
-            half_of(hidden_low),
-            half_of(mixed_t.T),
-        ),
-        (
-            jax.ShapeDtypeStruct((wide, width // 2), F32),
-            jax.ShapeDtypeStruct((wide, width // 2), F32),
-            jax.ShapeDtypeStruct((narrow, gate_back.shape[1] // 2), F32),
-            jax.ShapeDtypeStruct((narrow, width // 2), F32),
-        ),
-        5,
-        "spread_ffn",
-    )
 
     query_turned = turn_heads(back_home[:, :HEAD_DIM], pos_local, -1.0)
     key_value = back_home[:, HEAD_DIM:].reshape(KV_HEADS, group, 2 * HEAD_DIM, rows).sum(axis=1)
@@ -901,11 +1234,11 @@
         qkv_grads[96:].T,
         gain_totals[2],
         gain_totals[3],
-        grads_t[3].T,
+        out_t.T,
         gain_totals[1],
-        grads_t[0].T,
-        grads_t[1].T,
-        grads_t[2].T,
+        gate_t.T,
+        up_t.T,
+        down_t.T,
     )
 
 

time: 648 us -> 513 us (0.79)
  Pallas kernels: 397 us -> 327 us
  local copies, waits for them, and re-layouts: 49.9 us -> 14.9 us
  matrix products: 75 us -> 60 us
  other arithmetic: 29.4 us -> 14.9 us
  waiting for transfers between devices: 9.43 us -> 17.9 us
    pallas_call x2 -> x1, Pallas kernels: 213 us -> 31.7 us  [spread_call(): pl.pallas_call(functools.partial(spread_kernel, parts, rows, len(inputs),...]
    pallas_call x1, Pallas kernels: 32.9 us -> 207 us  [back_call(): pl.pallas_call(back_kernel, out_shape=(jax.ShapeDtypeStruct((wide, width...]
    pallas_call x4 -> x2, Pallas kernels: 124 us -> 60.9 us  [exchange(): pl.pallas_call(exchange_kernel, out_shape=jax.ShapeDtypeStruct(blocks.sha...]
    dot_general x3 -> x0, local copies, waits for them, and re-layouts: 18.6 us -> none  [the longest x1 6.3 us: heads_body(): up_pre = jnp.dot(ffn_low, up_full, preferred_element_type=F32)]
    all_gather x16 -> x9, waiting for transfers between devices: 3.25 us -> 13.6 us  [both(): return lax.all_gather(block, 'fsdp', axis=axis, tiled=True)]
    dynamic_slice x4 -> x1, local copies, waits for them, and re-layouts: 8.99 us -> 1.87 us  [half_of(): return lax.dynamic_slice_in_dim(gathered, core * part, part, 1)]
  transfers between devices with their start and end apart: 16 -> 9, of which waited for: 1 -> 2; matrix products, arithmetic and copies ran while one was open for 23% -> 9% of each run, Pallas kernels for 33% -> 17%
where the time goes in v2:
time: 513 us; the launch traced here: 509 us
  Pallas kernels  327 us (64%)
  matrix products  60 us (12%)
  blocking collectives  59.3 us (12%)
  waiting for transfers between devices  17.9 us (3%)
  other arithmetic  14.9 us (3%)
  local copies, waits for them, and re-layouts  14.9 us (3%)
  between operations  14.4 us (3%)
    pallas_call x1, Pallas kernels, back_call(): pl.pallas_call(back_kernel, out_shape=(jax.ShapeDtypeStruct((wide, width...  207 us
    pallas_call x2, Pallas kernels, exchange(): pl.pallas_call(exchange_kernel, out_shape=jax.ShapeDtypeStruct(blocks.sha...  60.9 us
    psum x1, blocking collectives, heads_body(): lax.psum((jnp.sum(attn_terms, axis=0), jnp.sum(ffn_terms, axis=0), query_...  38.1 us
    pallas_call x1, Pallas kernels, spread_call(): pl.pallas_call(functools.partial(spread_kernel, parts, rows, len(inputs),...  31.7 us
    pallas_call x1, Pallas kernels, attend(): pl.pallas_call(attend_kernel, out_shape=(jax.ShapeDtypeStruct((blocks, HE...  26.8 us
    dot_general x3, matrix products, against(): lax.dot_general(left_mat, right_mat, (((1,), (1,)), ((), ())), preferred_...  23.3 us
    all_gather x1, blocking collectives, heads_body(): starts = lax.all_gather(starts_local, 'ctx', axis=0, tiled=False)  21.3 us
    all_gather x9, waiting for transfers between devices, both(): return lax.all_gather(block, 'fsdp', axis=axis, tiled=True)  13.6 us
  transfers between devices with their start and end apart: 9, of which 2 were waited for; matrix products, arithmetic and copies ran while one was open for 9% of the time, Pallas kernels for 17%

profile of v2, /device:TPU:15, one launch (start us, length us, event | category | flops | bytes accessed | tf_op | source)
XLA Modules:
  0.0 508.8 jit_solution(4370658181888143899)
XLA Ops:
  8.7 1.2 fusion.10
  9.9 2.0 fusion.12
  15.4 21.3 %all-gather.start_ref = s32[16,1,256]{2,1,0:T(1,128)S(1)} all-gather(s32[1,1,256]{2,1,0:T(1,128)S(1)} %get-tuple-element.68), channel_id=1, replica_groups=mesh['ctx'=16,'fsdp'=2] {'ctx'}, dimensions={0}, use_global_device_ids=true | all-gather | bytes 17408 | tf_op jit(solution)/shard_map/all_gather | solution.py:1134
  37.8 1.7 fusion.6
  39.6 1.8 multiply_reduce_fusion.6
  42.4 2.1 all-gather.27.cloned.1.call-done
  44.6 1.9 constant_dynamic-slice_fusion.refs_1_
  46.5 11.3 %all-gather.11.cloned.1.call-done = bf16[1024,1024]{1,0:T(8,128)(2,1)} async-done(((bf16[512,1024]{1,0:T(8,128)(2,1)}), bf16[1024,1024]{1,0:T(8,128)(2,1)}) %all-gather.11.cloned.1.call-update) | async-done | bytes 2097168 | tf_op jit(solution)/shard_map/all_gather | solution.py:1102
  57.8 2.5 multiply_reduce_fusion.4
  61.8 1.3 pad_maximum_fusion.src
  63.1 44.0 %exchange_heads.2.qkv_ref = bf16[16,192,256]{2,1,0:T(8,128)(2,1)} custom-call(bf16[16,192,256]{2,1,0:T(8,128)(2,1)} %pad_maximum_fusion.src), custom_call_target="tpu_custom_call" | custom-call | tf_op jit(solution)/shard_map/exchange_heads/pallas_call | solution.py:363
  107.1 26.8 %attend_forward.1 = (bf16[16,64,256]{2,1,0:T(8,128)(2,1)}, f32[16,1,256]{2,1,0:T(1,128)}) custom-call(s32[16]{0:T(128)} %get-tuple-element.77.first_ref, s32[16]{0:T(128)} %get-tuple-element.78.clear_ref, bf16[16,192,256]{2,1,0:T(8,128)(2,1)} %exchange_heads.2.qkv_ref, s32[16,1,256]{2,1,0:T(1,128)} %copy-done.24), custom_call_target="tpu_custom_call" | custom-call | tf_op jit(solution)/shard_map/attend_forward/pallas_call | solution.py:437
  133.9 16.9 %exchange_heads.3 = bf16[16,64,256]{2,1,0:T(8,128)(2,1)} custom-call(bf16[16,64,256]{2,1,0:T(8,128)(2,1)} %get-tuple-element.20.src.part_ref), custom_call_target="tpu_custom_call" | custom-call | tf_op jit(solution)/shard_map/exchange_heads/pallas_call | solution.py:363
  150.9 2.6 multiply_reduce_fusion.3
  153.8 8.2 %fusion.37 = f32[256,4608]{1,0:T(8,128)} fusion(bf16[256,1024]{1,0:T(8,128)(2,1)S(1)} %multiply_convert_fusion.3.ffn_ref, bf16[1024,4608]{1,0:T(8,128)(2,1)} %all-gather.19.cloned.1.call-done), kind=kOutput, calls=%fused_computation.120 | convolution fusion | flops 2415919104 | bytes 14680064 | tf_op jit(solution)/shard_map/dot_general | solution.py:1158
  162.0 8.0 %fusion.38 = f32[256,4608]{1,0:T(8,128)} fusion(bf16[256,1024]{1,0:T(8,128)(2,1)S(1)} %multiply_convert_fusion.3.ffn_ref, bf16[1024,4608]{1,0:T(8,128)(2,1)} %all-gather.21.cloned.1.call-done), kind=kOutput, calls=%fused_computation.121 | convolution fusion | flops 2415919104 | bytes 14680064 | tf_op jit(solution)/shard_map/dot_general | solution.py:1159
  170.1 13.3 %multiply_convert_fusion = (bf16[256,4608]{1,0:T(8,128)(2,1)S(1)}, bf16[256,4608]{1,0:T(8,128)(2,1)S(1)}, bf16[256,4608]{1,0:T(8,128)(2,1)}) fusion(f32[256,4608]{1,0:T(8,128)} %fusion.37, f32[256,4608]{1,0:T(8,128)} %fusion.38, bf16[4608,1024]{1,0:T(8,128)(2,1)} %all-gather.23.cloned.1.call-done, bf16[1,256,1024]{2,1,0:T(8,128)(2,1)S(1)} %copy-done.18), kind=kOutput, calls=%fused_computation.2 | convolution fusion | flops 2433613824 | bytes 26476544 | tf_op jit(solution)/shard_map/dot_general | solution.py:68
  183.4 7.1 %fusion.39 = f32[256,1024]{1,0:T(8,128)S(1)} fusion(bf16[256,4608]{1,0:T(8,128)(2,1)S(1)} %get-tuple-element.40.gate_ref, bf16[1024,4608]{1,0:T(8,128)(2,1)} %all-gather.19.cloned.1.call-done), kind=kOutput, calls=%fused_computation.122 | convolution fusion | flops 2415919104 | bytes 12845056 | tf_op jit(solution)/shard_map/dot_general | solution.py:68
  191.5 2.9 multiply_reduce_fusion
  194.4 1.4 fusion.35
  197.4 1.0 copy.42
  198.4 207.5 %backward_spread.1 = (f32[288,512]{1,0:T(8,128)}, f32[288,512]{1,0:T(8,128)}, f32[64,2304]{1,0:T(8,128)}, f32[64,512]{1,0:T(8,128)}, bf16[16,192,256]{2,1,0:T(8,128)(2,1)}) custom-call(bf16[256,4608]{1,0:T(8,128)(2,1)} %copy-done.17, bf16[256,4608]{1,0:T(8,128)(2,1)} %copy-done.16, bf16[256,4608]{1,0:T(8,128)(2,1)} %get-tuple-element.41.hidden_ref, ...), custom_call_target="tpu_custom_call" | custom-call | tf_op jit(solution)/shard_map/backward_spread/pallas_call | solution.py:878
  405.9 1.7 convert_element_type.85
  411.1 1.1 pad_maximum_fusion.2
  412.4 1.9 fusion.40
  414.9 1.6 fusion.20
  416.5 38.1 %all-reduce = (f32[1024]{0:T(1024)}, f32[64]{0:T(128)}, f32[64]{0:T(128)}, f32[1024]{0:T(1024)}) all-reduce(f32[1024]{0:T(1024)S(1)} %get-tuple-element.29, f32[64]{0:T(128)S(1)} %reduce_sum.159, f32[64]{0:T(128)S(1)} %reduce_sum.162, f32[1024]{0:T(1024)S(1)} %get-tuple-element.27), channel_id=1, replica_groups=mesh['ctx'=16,'fsdp'=2] {'ctx','fsdp'}, use_global_device_ids=true, to_apply=%region_10.11 | all-reduce | flops 2176 | bytes 17408 | tf_op jit(solution)/shard_map/psum | solution.py:1224
  454.6 2.7 fusion.17
  457.3 7.1 %fusion.5 = bf16[1,256,1024]{2,1,0:T(8,128)(2,1)} fusion(f32[256,1024]{1,0:T(8,128)S(1)} %copy-done.5, bf16[256,4608]{1,0:T(8,128)(2,1)S(1)} %copy-done.15, bf16[4608,1024]{1,0:T(8,128)(2,1)} %all-gather.23.cloned.1.call-done), kind=kOutput, calls=%fused_computation.24 | convolution fusion | flops 2416443392 | bytes 13369344 | tf_op jit(solution)/shard_map/dot_general | solution.py:1163
  464.4 31.7 %spread_qkv.1 = f32[128,512]{1,0:T(8,128)} custom-call(bf16[2048,512]{1,0:T(8,128)(2,1)} %all-gather.25.cloned.1.call-done.refs_0_, bf16[512,512]{1,0:T(8,128)(2,1)} %constant_dynamic-slice_fusion.refs_1_), custom_call_target="tpu_custom_call" | custom-call | tf_op jit(solution)/shard_map/spread_qkv/pallas_call | solution.py:1026
  496.1 1.5 slice_bitcast_fusion.1
  497.6 1.6 slice_bitcast_fusion
  (130 shorter events, 18.5 us)
Async XLA Ops:
  7.2 30.6 %all-gather.15.cloned.1.call-start = ((), (), s32[]{:S(2)}) async-start(), calls=%async_computation.2 | async-start | bytes 1572864 | tf_op jit(solution)/shard_map/all_gather | solution.py:1102
  7.9 31.7 %all-gather.13.cloned.1.call-start = ((), (), s32[]{:S(2)}) async-start(), calls=%async_computation.1 | async-start | bytes 1572864 | tf_op jit(solution)/shard_map/all_gather | solution.py:1102
  8.7 35.9 %all-gather.27.cloned.1.call-start = ((), (), s32[]{:S(2)}) async-start(), calls=%async_computation.8 | async-start | bytes 1572864 | tf_op jit(solution)/shard_map/all_gather | solution.py:1102
  12.0 45.8 %all-gather.11.cloned.1.call-start = ((), (), s32[]{:S(2)}) async-start(), calls=%async_computation | async-start | bytes 3145728 | tf_op jit(solution)/shard_map/all_gather | solution.py:1102
  12.6 138.3 %all-gather.17.cloned.1.call-start = ((), (), s32[]{:S(2)}) async-start(), calls=%async_computation.3 | async-start | bytes 3145728 | tf_op jit(solution)/shard_map/all_gather | solution.py:1102
  13.2 140.6 %all-gather.19.cloned.1.call-start = ((), (), s32[]{:S(2)}) async-start(), calls=%async_computation.4 | async-start | bytes 14155776 | tf_op jit(solution)/shard_map/all_gather | solution.py:1102
  13.7 148.3 %all-gather.21.cloned.1.call-start = ((), (), s32[]{:S(2)}) async-start(), calls=%async_computation.5 | async-start | bytes 14155776 | tf_op jit(solution)/shard_map/all_gather | solution.py:1102
  14.5 22.1 %copy-start.28 = (f32[64]{0:T(128)S(1)}, f32[64]{0:T(128)}, u32[]{:S(2)}) copy-start(f32[64]{0:T(128)} %param.22) | copy-start | bytes 772
  14.5 22.2 %copy-start.29 = (f32[64]{0:T(128)S(1)}, f32[64]{0:T(128)}, u32[]{:S(2)}) copy-start(f32[64]{0:T(128)} %param.21) | copy-start | bytes 772
  14.5 23.2 %copy-start.3 = (bf16[256,1024]{1,0:T(8,128)(2,1)S(1)}, bf16[256,1024]{1,0:T(8,128)(2,1)}, u32[]{:S(2)}) copy-start(bf16[256,1024]{1,0:T(8,128)(2,1)} %fusion.12) | copy-start | bytes 1572868
  14.5 155.5 %all-gather.23.cloned.1.call-start = ((), (), s32[]{:S(2)}) async-start(), calls=%async_computation.6 | async-start | bytes 14155776 | tf_op jit(solution)/shard_map/all_gather | solution.py:1102
  15.3 449.1 %all-gather.25.cloned.1.call-start = ((), (), s32[]{:S(2)}) async-start(), calls=%async_computation.7 | async-start | bytes 3145728 | tf_op jit(solution)/shard_map/all_gather | solution.py:1102
  36.6 5.8 %copy-start.24 = (s32[16,1,256]{2,1,0:T(1,128)}, s32[16,1,256]{2,1,0:T(1,128)S(1)}, u32[]{:S(2)}) copy-start(s32[16,1,256]{2,1,0:T(1,128)S(1)} %all-gather.start_ref) | copy-start | bytes 49156
  63.1 87.8 %copy-start.2 = (bf16[1,256,1024]{2,1,0:T(8,128)(2,1)S(1)}, bf16[1,256,1024]{2,1,0:T(8,128)(2,1)}, u32[]{:S(2)}) copy-start(bf16[1,256,1024]{2,1,0:T(8,128)(2,1)} %param.15) | copy-start | bytes 1572868
  107.1 46.4 %copy-start.27 = (f32[1024]{0:T(1024)S(1)}, f32[1024]{0:T(1024)}, u32[]{:S(2)}) copy-start(f32[1024]{0:T(1024)} %param.24) | copy-start | bytes 12292
  153.5 40.9 %copy-start.4 = (f32[256,1024]{1,0:T(8,128)}, f32[256,1024]{1,0:T(8,128)S(1)}, u32[]{:S(2)}) copy-start(f32[256,1024]{1,0:T(8,128)S(1)} %get-tuple-element.74) | copy-start | bytes 3145732
  153.7 8.3 %copy-start.8 = (bf16[256,1024]{1,0:T(8,128)(2,1)}, bf16[256,1024]{1,0:T(8,128)(2,1)S(1)}, u32[]{:S(2)}) copy-start(bf16[256,1024]{1,0:T(8,128)(2,1)S(1)} %multiply_convert_fusion.3.ffn_ref) | copy-start | bytes 1572868
  162.0 8.0 %copy-start.18 = (bf16[1,256,1024]{2,1,0:T(8,128)(2,1)S(1)}, bf16[1,256,1024]{2,1,0:T(8,128)(2,1)}, u32[]{:S(2)}) copy-start(bf16[1,256,1024]{2,1,0:T(8,128)(2,1)} %param.28) | copy-start | bytes 1572868
  183.4 7.1 %copy-start.17 = (bf16[256,4608]{1,0:T(8,128)(2,1)}, bf16[256,4608]{1,0:T(8,128)(2,1)S(1)}, u32[]{:S(2)}) copy-start(bf16[256,4608]{1,0:T(8,128)(2,1)S(1)} %get-tuple-element.40.gate_ref) | copy-start | bytes 7077892
  183.4 7.1 %copy-start.16 = (bf16[256,4608]{1,0:T(8,128)(2,1)}, bf16[256,4608]{1,0:T(8,128)(2,1)S(1)}, u32[]{:S(2)}) copy-start(bf16[256,4608]{1,0:T(8,128)(2,1)S(1)} %get-tuple-element.39.up_ref) | copy-start | bytes 7077892
  183.4 8.1 %copy-start.6 = (bf16[1024,4608]{1,0:T(8,128)(2,1)S(1)}, bf16[1024,4608]{1,0:T(8,128)(2,1)}, u32[]{:S(2)}) copy-start(bf16[1024,4608]{1,0:T(8,128)(2,1)} %all-gather.21.cloned.1.call-done) | copy-start | bytes 28311556
  194.4 2.2 copy-start.20
  409.8 2.6 copy-start.7
  412.4 2.5 copy-start.13
  412.4 2.5 copy-start.26
  414.4 40.2 %copy-start.12 = (f32[256,1024]{1,0:T(8,128)S(1)}, f32[256,1024]{1,0:T(8,128)}, u32[]{:S(2)}) copy-start(f32[256,1024]{1,0:T(8,128)} %get-tuple-element.38) | copy-start | bytes 3145732
  414.9 42.4 %copy-start.5 = (f32[256,1024]{1,0:T(8,128)S(1)}, f32[256,1024]{1,0:T(8,128)}, u32[]{:S(2)}) copy-start(f32[256,1024]{1,0:T(8,128)} %copy-done.4) | copy-start | bytes 3145732
  454.6 2.7 copy-start.15
  464.3 34.9 %copy-start.25 = (f32[64,512]{1,0:T(8,128)S(1)}, f32[64,512]{1,0:T(8,128)}, u32[]{:S(2)}) copy-start(f32[64,512]{1,0:T(8,128)} %get-tuple-element.23) | copy-start | bytes 393220
  464.3 35.5 %copy-start.23 = (f32[288,512]{1,0:T(8,128)S(1)}, f32[288,512]{1,0:T(8,128)}, u32[]{:S(2)}) copy-start(f32[288,512]{1,0:T(8,128)} %get-tuple-element.24) | copy-start | bytes 1769476
  464.3 36.3 %copy-start.22 = (f32[288,512]{1,0:T(8,128)S(1)}, f32[288,512]{1,0:T(8,128)}, u32[]{:S(2)}) copy-start(f32[288,512]{1,0:T(8,128)} %get-tuple-element.25) | copy-start | bytes 1769476
  464.4 37.1 %copy-start.21 = (f32[64,2304]{1,0:T(8,128)S(1)}, f32[64,2304]{1,0:T(8,128)}, u32[]{:S(2)}) copy-start(f32[64,2304]{1,0:T(8,128)} %get-tuple-element.26) | copy-start | bytes 1769476
  (8 other events, 8.5 us)
Sparse Core Ops, SparseCore 0:
  9.6 10.8 all-gather.14
  22.0 10.1 all-gather.12
  34.3 10.1 all-gather.26
  46.0 11.7 all-gather.10
  59.1 11.7 all-gather.16
  72.3 23.0 all-gather.18
  96.9 23.2 all-gather.20
  121.8 23.1 all-gather.22
  412.3 10.5 all-gather.24

commit v3 on v2

--- a/solution.py
+++ b/solution.py
@@ -672,10 +672,10 @@
 
     turn_into(gate_ref, put_pair(0))
     turn_into(up_ref, put_pair(wide))
-    order = [(1, 1, depth) for depth in (1, 2, 3, 0)]
+    order = []
     for depth in (1, 2, 3, 0):
-        order += [(1, 0, depth), (0, 1, depth)]
-    order += [(0, 0, depth) for depth in range(4)]
+        order += [(1, 1, depth), (1, 0, depth), (0, 1, depth)]
+    order += [(0, 0, depth) for depth in (1, 2, 3, 0)]
     for turn_x, turn_y, depth in order:
         pair_copy(turn_x, turn_y, depth).start()
 
@@ -723,23 +723,41 @@
     for copy in sides:
         copy.wait_recv()
 
-    def one_near(index, nothing):
-        depth = lax.rem(index + 1, 4)
+    def near(depth):
         pair_copy(1, 1, depth).wait_recv()
         for chain in chains:
             chain.stage_one(1, depth)
-        return nothing
-
-    def one_far(index, nothing):
-        depth = lax.rem(index + 1, 4)
+
+    def far(depth):
         pair_copy(1, 0, depth).wait_recv()
         pair_copy(0, 1, depth).wait_recv()
         for chain in chains:
             chain.stage_one(0, depth)
-        return nothing
-
-    lax.fori_loop(0, 4, one_near, 0)
-    lax.fori_loop(0, 4, one_far, 0)
+
+    def event(number):
+        @pl.when(lax.rem(number, 2) == 1)
+        def _():
+            for chain in chains:
+                chain.stage_two(lax.rem((number + 1) // 2, 4))
+
+        @pl.when((lax.rem(number, 2) == 1) & (number >= 3))
+        def _():
+            depth = (number - 1) // 2
+            pair_copy(0, 0, depth).wait_recv()
+            for chain in chains:
+                chain.stage_three(depth)
+
+        @pl.when((lax.rem(number, 2) == 1) & (number <= 5))
+        def _():
+            far(lax.rem(number // 2 + 2, 4))
+
+        @pl.when((lax.rem(number, 2) == 0) & (number <= 5))
+        def _():
+            near(lax.rem(number // 2 + 2, 4))
+
+    near(1)
+    far(1)
+    near(2)
 
     key_value[0] = jnp.zeros(key_value.shape[1:], BF16)
 
@@ -770,7 +788,7 @@
         def _():
             back_copy(lax.rem(j - place + RING, RING), j).start()
 
-    def per_query(i, nothing):
+    def per_query(i):
         @pl.when(i != place)
         def _():
             step = lax.rem(place - i + RING, RING)
@@ -820,31 +838,28 @@
         def _():
             flush(i - 8)
 
-        @pl.when((i >= 8) & (lax.rem(i, 2) == 0))
-        def _():
-            depth = lax.rem((i - 8) // 2 + 1, 4)
-            for chain in chains:
-                chain.stage_two(depth)
-
-        return nothing
-
-    lax.fori_loop(0, blocks, per_query, 0)
-
     def rest(j, nothing):
         flush(j)
         return nothing
 
-    lax.fori_loop(blocks - 8, blocks, rest, 0)
+    def per_step(i, nothing):
+        @pl.when(i < blocks)
+        def _():
+            per_query(i)
+
+        @pl.when(i == blocks - 1)
+        def _():
+            lax.fori_loop(blocks - 8, blocks, rest, 0)
+
+        @pl.when((i >= 6) & (lax.rem(i, 3) == 0))
+        def _():
+            event(i // 3 - 1)
+
+        return nothing
+
+    lax.fori_loop(0, 25, per_step, 0)
     back_out[place] = back_own[place]
-    for depth in range(4):
-        pair_copy(0, 0, depth).wait_recv()
-
-    def three(depth, nothing):
-        for chain in chains:
-            chain.stage_three(depth)
-        return nothing
-
-    lax.fori_loop(1, 4, three, 0)
+    pair_copy(0, 0, 0).wait_recv()
     for chain in chains:
         chain.close(finish)
 
@@ -917,185 +932,469 @@
     )(*inputs)
 
 
-def spread_kernel(parts, rows, n_in, n_out, *refs):
-    inputs, outputs, scratch = refs[:n_in], refs[n_in : n_in + n_out], refs[n_in + n_out :]
-    sent = (scratch[0:3], scratch[3:6])
-    came = (scratch[6:9], scratch[9:12])
-    send_sems, recv_sems = scratch[12], scratch[13]
-    compute, finish = parts
+def turn_back(values, cosine, sine):
+    half = HEAD_DIM // 2
+    first, second = values[:half], values[half:]
+    return jnp.concatenate(
+        [first * cosine + second * sine, second * cosine - first * sine], axis=0
+    )
+
+
+def column_norm_back(values, gain, upstream):
+    inverse = lax.rsqrt(jnp.mean(values * values, axis=0, keepdims=True) + EPSILON)
+    scaled = upstream * gain
+    total = jnp.sum(scaled * values, axis=0, keepdims=True) / values.shape[0]
+    return inverse * scaled - values * inverse**3 * total, upstream * values * inverse
+
+
+def tail_kernel(
+    back_ref,
+    query_ref,
+    key_ref,
+    cosine_ref,
+    sine_ref,
+    query_gain_ref,
+    key_gain_ref,
+    weights_ref,
+    normed_ref,
+    tokens_ref,
+    attn_gain_ref,
+    middle_ref,
+    ffn_terms_ref,
+    tokens_out,
+    grads_out,
+    gains_out,
+    turned_own,
+    turned_far,
+    normed_far,
+    natural,
+    summed,
+    gain_own,
+    gain_came,
+    gain_deep,
+    sent_a,
+    came_a0,
+    came_a1,
+    came_a2,
+    sent_b,
+    came_b0,
+    came_b1,
+    came_b2,
+    send_sems,
+    recv_sems,
+    core_send,
+    core_recv,
+    gain_send,
+    gain_recv,
+):
     place, core = lax.axis_index("ctx"), lax.axis_index("fsdp")
     x, y, z = lax.rem(place, 2), lax.rem(place // 2, 2), place // 4
-
-    def at(chain, first, second, depth):
-        if chain == 0:
-            return depth * 4 + second * 2 + first
-        return depth * 4 + first * 2 + second
-
-    coords = ((x, y), (y, x))
-    barrier = pltpu.get_barrier_semaphore()
-    peers = [at(0, 1 - x, y, z), at(0, x, 1 - y, z)]
-    peers += [at(0, x, y, lax.rem(z + step, 4)) for step in range(1, 4)]
-    for peer in peers:
-        pl.semaphore_signal(barrier, inc=1, device_id=(peer, core), device_id_type=MESH)
-    pl.semaphore_wait(barrier, len(peers))
-
-    def copy(chain, stage, slot, sem, peer):
+    near_x = (place + 1 - 2 * x, core)
+    near_y = (place + 2 - 4 * y, core)
+    partner = (place, 1 - core)
+    deep = [(lax.rem(place + 4 * step, RING), core) for step in range(1, 4)]
+    greet([near_x, near_y, partner] + deep)
+    half_width = normed_far.shape[1]
+    heads, pairs = query_ref.shape[0], key_ref.shape[0]
+    group = heads // pairs
+
+    def core_copy(source, target, sem):
         return pltpu.make_async_remote_copy(
-            src_ref=sent[chain][stage].at[slot],
-            dst_ref=came[chain][stage].at[slot],
-            send_sem=send_sems.at[chain, sem],
-            recv_sem=recv_sems.at[chain, sem],
-            device_id=(peer, core),
+            src_ref=source,
+            dst_ref=target,
+            send_sem=core_send.at[sem],
+            recv_sem=core_recv.at[sem],
+            device_id=partner,
             device_id_type=MESH,
         )
 
-    def one(index, nothing):
-        turned = 1 - index // 4
-        depth = lax.rem(index + 1, 4)
-        slot = turned * 4 + depth
-        for chain in range(2):
-            first, second = coords[chain]
-            other = second + turned - 2 * second * turned
-            owner = at(chain, 1 - first, other, lax.rem(z + depth, 4))
-            for row, value in compute(chain, owner, inputs):
-                sent[chain][0][slot, row : row + value.shape[0], :] = value.astype(BF16)
-            copy(chain, 0, slot, slot, at(chain, 1 - first, second, z)).start()
-        return nothing
+    other = pl.ds(pl.multiple_of((1 - core) * half_width, 128), half_width)
+    sides = [
+        core_copy(normed_ref.at[:, other], normed_far, 0),
+        core_copy(turned_own, turned_far, 1),
+    ]
+    sides[0].start()
+    cosine, sine = cosine_ref[...], sine_ref[...]
+
+    def query_head(head, total):
+        upstream = turn_back(back_ref[head, 0:HEAD_DIM, :].astype(F32), cosine, sine)
+        back, terms = column_norm_back(query_ref[head], query_gain_ref[...], upstream)
+        rows = pl.ds(pl.multiple_of(head * HEAD_DIM, HEAD_DIM), HEAD_DIM)
+        turned_own[rows, :] = back.astype(BF16)
+        return total + terms
+
+    def key_head(pair, total):
+        upstream = jnp.zeros((2 * HEAD_DIM, back_ref.shape[2]), F32)
+        for member in range(group):
+            upstream += back_ref[group * pair + member, HEAD_DIM : 3 * HEAD_DIM, :].astype(F32)
+        back, terms = column_norm_back(
+            key_ref[pair],
+            key_gain_ref[...],
+            turn_back(upstream[:HEAD_DIM], cosine, sine),
+        )
+        base = heads * HEAD_DIM
+        rows = pl.ds(pl.multiple_of(base + pair * HEAD_DIM, HEAD_DIM), HEAD_DIM)
+        turned_own[rows, :] = back.astype(BF16)
+        base += pairs * HEAD_DIM
+        rows = pl.ds(pl.multiple_of(base + pair * HEAD_DIM, HEAD_DIM), HEAD_DIM)
+        turned_own[rows, :] = upstream[HEAD_DIM:].astype(BF16)
+        return total + terms
+
+    nothing = jnp.zeros((HEAD_DIM, back_ref.shape[2]), F32)
+    query_terms = lax.fori_loop(0, heads, query_head, nothing)
+    key_terms = lax.fori_loop(0, pairs, key_head, nothing)
+    sides[1].start()
+
+    def compute(chain, owner):
+        lanes = slice(chain * 256, chain * 256 + 256)
+        own_lanes = pl.ds(pl.multiple_of(core * half_width + chain * 256, 128), 256)
+        values, row, base = [], 0, 0
+        for size in (heads, pairs, pairs):
+            count = size * HEAD_DIM // RING
+            rows = pl.ds(pl.multiple_of(base + owner * count, 16), count)
+            value = jnp.dot(turned_own[rows, :], normed_ref[:, own_lanes], preferred_element_type=F32)
+            value += jnp.dot(turned_far[rows, :], normed_far[:, lanes], preferred_element_type=F32)
+            values.append((row, value))
+            row += count
+            base += size * HEAD_DIM
+        return values
+
+    def finish(chain, row, value):
+        grads_out[row : row + value.shape[0], chain * 256 : chain * 256 + 256] = value
+
+    chains = (
+        Spread(0, compute, sent_a, (came_a0, came_a1, came_a2), send_sems, recv_sems),
+        Spread(1, compute, sent_b, (came_b0, came_b1, came_b2), send_sems, recv_sems),
+    )
+    for copy in sides:
+        copy.wait_recv()
+
+    def one(index, carry):
+        for chain in chains:
+            chain.stage_one(1 - index // 4, lax.rem(index + 1, 4))
+        return carry
 
     lax.fori_loop(0, 8, one, 0)
 
-    def two(index, nothing):
-        depth = lax.rem(index + 1, 4)
-        for chain in range(2):
-            first, second = coords[chain]
-            copy(chain, 0, 4 + depth, 4 + depth, at(chain, 1 - first, second, z)).wait_recv()
-            owner = at(chain, first, 1 - second, lax.rem(z + depth, 4))
-            for row, value in compute(chain, owner, inputs):
-                window = slice(row, row + value.shape[0])
-                value = value + came[chain][0][4 + depth, window, :].astype(F32)
-                sent[chain][1][depth, window, :] = value.astype(BF16)
-            copy(chain, 1, depth, 8 + depth, at(chain, first, 1 - second, z)).start()
-        return nothing
+    natural[...] = jnp.zeros(natural.shape, BF16)
+    for row in range(0, turned_own.shape[0], 128):
+        natural[:, row : row + 128] = turned_own[row : row + 128, :].astype(F32).T.astype(BF16)
+
+    def two(index, carry):
+        for chain in chains:
+            chain.stage_two(lax.rem(index + 1, 4))
+        return carry
 
     lax.fori_loop(0, 4, two, 0)
 
-    def three(depth, nothing):
-        for chain in range(2):
-            first, second = coords[chain]
-            copy(chain, 0, depth, depth, at(chain, 1 - first, second, z)).wait_recv()
-            copy(chain, 1, depth, 8 + depth, at(chain, first, 1 - second, z)).wait_recv()
-            far = at(chain, first, second, lax.rem(z + depth, 4))
-            for row, value in compute(chain, far, inputs):
-                window = slice(row, row + value.shape[0])
-                value = value + came[chain][0][depth, window, :].astype(F32)
-                value = value + came[chain][1][depth, window, :].astype(F32)
-                sent[chain][2][depth - 1, window, :] = value.astype(BF16)
-            copy(chain, 2, depth - 1, 11 + depth, far).start()
-        return nothing
+    cut = 2 * pairs * HEAD_DIM
+    upstream = dot_dims(natural[:, : heads * HEAD_DIM], weights_ref[:, cut:], 1, 1)
+    upstream += dot_dims(natural[:, heads * HEAD_DIM :], weights_ref[:, :cut], 1, 1)
+    summed[...] = upstream
+
+    def three(depth, carry):
+        for chain in chains:
+            chain.stage_three(depth)
+        return carry
 
     lax.fori_loop(1, 4, three, 0)
 
-    for chain in range(2):
-        first, second = coords[chain]
-        copy(chain, 0, 0, 0, at(chain, 1 - first, second, z)).wait_recv()
-        copy(chain, 1, 0, 8, at(chain, first, 1 - second, z)).wait_recv()
-        for depth in range(1, 4):
-            far = at(chain, first, second, lax.rem(z + depth, 4))
-            copy(chain, 2, depth - 1, 11 + depth, far).wait_recv()
-        for row, value in compute(chain, place, inputs):
-            window = slice(row, row + value.shape[0])
-            value = value + came[chain][0][0, window, :].astype(F32)
-            value = value + came[chain][1][0, window, :].astype(F32)
-            for depth in range(3):
-                value = value + came[chain][2][depth, window, :].astype(F32)
-            finish(chain, row, value, outputs)
-        for slot in range(8):
-            copy(chain, 0, slot, slot, at(chain, 1 - first, second, z)).wait_send()
-        for depth in range(4):
-            copy(chain, 1, depth, 8 + depth, at(chain, first, 1 - second, z)).wait_send()
-        for depth in range(1, 4):
-            far = at(chain, first, second, lax.rem(z + depth, 4))
-            copy(chain, 2, depth - 1, 11 + depth, far).wait_send()
-
-
-def spread_call(parts, rows, inputs, out_shape, call_id, name):
-    lanes = 256
+    def token_rows(index, total):
+        rows = pl.ds(pl.multiple_of(index * 32, 32), 32)
+        values, upstream = tokens_ref[rows, :].astype(F32), summed[rows, :]
+        inverse = lax.rsqrt(jnp.mean(values * values, axis=-1, keepdims=True) + EPSILON)
+        scaled = upstream * attn_gain_ref[...]
+        weight = jnp.sum(scaled * values, axis=-1, keepdims=True) / values.shape[1]
+        tokens_out[rows, :] = (
+            middle_ref[rows, :] + inverse * scaled - values * inverse**3 * weight
+        )
+        return total + jnp.sum(upstream * values * inverse, axis=0, keepdims=True)
+
+    terms = lax.fori_loop(
+        0, tokens_ref.shape[0] // 32, token_rows, jnp.zeros((1, tokens_ref.shape[1]), F32)
+    )
+    gain_own[0] = jnp.zeros(gain_own.shape[1:], F32)
+    gain_own[0, 0:1, :] = terms
+    gain_own[0, 1:2, :] = ffn_terms_ref[...]
+    gain_own[0, 2:3, 0:HEAD_DIM] = jnp.sum(query_terms.T, axis=0, keepdims=True)
+    gain_own[0, 3:4, 0:HEAD_DIM] = jnp.sum(key_terms.T, axis=0, keepdims=True)
+
+    def gain_copy(source, target, sem, peer):
+        return pltpu.make_async_remote_copy(
+            src_ref=source,
+            dst_ref=target,
+            send_sem=gain_send.at[sem],
+            recv_sem=gain_recv.at[sem],
+            device_id=peer,
+            device_id_type=MESH,
+        )
+
+    gain_copies = []
+    for stage, peer in enumerate((near_x, near_y, partner)):
+        copy = gain_copy(gain_own.at[stage], gain_came.at[stage], stage, peer)
+        copy.start()
+        gain_copies.append(copy)
+        copy.wait_recv()
+        gain_own[stage + 1] = gain_own[stage] + gain_came[stage]
+    gain_deep[z] = gain_own[3]
+    for step in range(1, 4):
+        copy = gain_copy(gain_own.at[3], gain_deep.at[z], 2 + step, deep[step - 1])
+        copy.start()
+        gain_copies.append(copy)
+
+    for chain in chains:
+        chain.close(finish)
+    for copy in gain_copies[3:]:
+        copy.wait_recv()
+    gains_out[...] = (gain_deep[0] + gain_deep[1]) + (gain_deep[2] + gain_deep[3])
+    for copy in sides + gain_copies:
+        copy.wait_send()
+    for chain in chains:
+        chain.drain()
+
+
+def tail_call(call_id, *inputs):
+    rows, width = inputs[8].shape
+    total = (HEADS + 2 * KV_HEADS) * HEAD_DIM
+    block_rows = total // RING
     buffers = [
-        pltpu.VMEM((slots, rows[chain], lanes), BF16) for chain in range(2) for slots in (8, 4, 3)
+        pltpu.VMEM((slots, block_rows, 256), BF16) for chain in range(2) for slots in (8, 8, 4, 3)
     ]
     return pl.pallas_call(
-        functools.partial(spread_kernel, parts, rows, len(inputs), len(out_shape)),
-        out_shape=out_shape,
+        tail_kernel,
+        out_shape=(
+            jax.ShapeDtypeStruct((rows, width), F32),
+            jax.ShapeDtypeStruct((block_rows, width // 2), F32),
+            jax.ShapeDtypeStruct((4, width), F32),
+        ),
         in_specs=[VMEM_SPEC] * len(inputs),
-        out_specs=tuple([VMEM_SPEC] * len(out_shape)),
-        scratch_shapes=buffers
+        out_specs=(VMEM_SPEC,) * 3,
+        scratch_shapes=[
+            pltpu.VMEM((total, rows), BF16),
+            pltpu.VMEM((total, rows), BF16),
+            pltpu.VMEM((rows, width // 2), BF16),
+            pltpu.VMEM((rows, total), BF16),
+            pltpu.VMEM((rows, width), F32),
+            pltpu.VMEM((4, 4, width), F32),
+            pltpu.VMEM((3, 4, width), F32),
+            pltpu.VMEM((4, 4, width), F32),
+        ]
         + buffers
-        + [pltpu.SemaphoreType.DMA((2, 15)), pltpu.SemaphoreType.DMA((2, 15))],
+        + [
+            pltpu.SemaphoreType.DMA((2, 15)),
+            pltpu.SemaphoreType.DMA((2, 15)),
+            pltpu.SemaphoreType.DMA((2,)),
+            pltpu.SemaphoreType.DMA((2,)),
+            pltpu.SemaphoreType.DMA((6,)),
+            pltpu.SemaphoreType.DMA((6,)),
+        ],
         compiler_params=pltpu.CompilerParams(
             collective_id=call_id, has_side_effects=True, vmem_limit_bytes=60 << 20
         ),
-        name=name,
+        name="backward_tail",
     )(*inputs)
 
 
-def rows_of(ref, owner, count, base=0):
-    return ref[pl.ds(pl.multiple_of(base + owner * count, 16), count), :]
-
-
-def qkv_parts():
-    def compute(chain, owner, inputs):
-        back_t, normed = inputs
-        lanes = slice(chain * 256, chain * 256 + 256)
-        values = []
-        row, base = 0, 0
-        for count in (64, 32, 32):
-            values.append(
-                (
-                    row,
-                    jnp.dot(
-                        rows_of(back_t, owner, count, base),
-                        normed[:, lanes],
-                        preferred_element_type=F32,
-                    ),
-                )
-            )
-            row += count
-            base += count * RING
-        return values
-
-    def finish(chain, row, value, outputs):
-        outputs[0][row : row + value.shape[0], chain * 256 : chain * 256 + 256] = value
-
-    return compute, finish
-
-
-def turn_heads(values_t, positions, sign):
+def angle_parts(positions):
     half = HEAD_DIM // 2
     inverse_freq = THETA ** (-(2.0 / HEAD_DIM) * jnp.arange(half, dtype=F32))
     angles = inverse_freq[:, None] * positions.astype(F32)[None, :]
-    cosine, sine = jnp.cos(angles)[None], sign * jnp.sin(angles)[None]
-    first, second = values_t[:, :half], values_t[:, half:]
-    return jnp.concatenate(
-        [first * cosine - second * sine, second * cosine + first * sine], axis=1
-    )
-
-
-def head_norm(values_t, gain):
-    mean = jnp.mean(values_t * values_t, axis=1, keepdims=True)
-    return values_t * lax.rsqrt(mean + EPSILON) * gain[None, :, None]
-
-
-def head_norm_back(values_t, gain, upstream):
-    inverse = lax.rsqrt(jnp.mean(values_t * values_t, axis=1, keepdims=True) + EPSILON)
-    scaled = upstream * gain[None, :, None]
-    d_values = (
-        inverse * scaled
-        - values_t
-        * inverse**3
-        * jnp.sum(scaled * values_t, axis=1, keepdims=True)
-        / values_t.shape[1]
-    )
-    return d_values, jnp.sum(upstream * values_t * inverse, axis=(0, 2))
+    return jnp.cos(angles), jnp.sin(angles)
+
+
+def front_kernel(
+    tokens_ref,
+    gain_ref,
+    w_query_ref,
+    w_key_ref,
+    w_value_ref,
+    query_gain_ref,
+    key_gain_ref,
+    cosine_ref,
+    sine_ref,
+    own_start_ref,
+    qkv_out,
+    starts_out,
+    query_out,
+    key_out,
+    normed_out,
+    weights_out,
+    home,
+    own_sem,
+    send_sem,
+    recv_sem,
+    start_send,
+    start_recv,
+    core_send,
+    core_recv,
+):
+    place, core = lax.axis_index("ctx"), lax.axis_index("fsdp")
+    rows = tokens_ref.shape[0]
+    depth = w_query_ref.shape[0]
+    partner = (place, 1 - core)
+    greet([partner] + [(lax.rem(place + step, RING), core) for step in range(1, RING)])
+
+    def own_rows(part):
+        return pl.ds(pl.multiple_of(part * depth, 128), depth)
+
+    copies, locals_, column = [], [], 0
+    for index, source in enumerate((w_key_ref, w_value_ref, w_query_ref)):
+        window = pl.ds(column, source.shape[1])
+        target = weights_out.at[own_rows(core), window]
+        copy = pltpu.make_async_remote_copy(
+            src_ref=source,
+            dst_ref=target,
+            send_sem=core_send.at[index],
+            recv_sem=core_recv.at[index],
+            device_id=partner,
+            device_id_type=MESH,
+        )
+        copy.start()
+        copies.append(copy)
+        near = pltpu.make_async_copy(source, target, own_sem.at[index])
+        near.start()
+        locals_.append(near)
+        column += source.shape[1]
+
+    def start_copy(step):
+        peer = lax.rem(place + step, RING)
+        return pltpu.make_async_remote_copy(
+            src_ref=own_start_ref,
+            dst_ref=starts_out.at[place],
+            send_sem=start_send.at[step],
+            recv_sem=start_recv.at[step],
+            device_id=(peer, core),
+            device_id_type=MESH,
+        )
+
+    for step in range(1, RING):
+        start_copy(step).start()
+    starts_out[place] = own_start_ref[...]
+
+    def norm_rows(index, nothing):
+        window = pl.ds(pl.multiple_of(index * 32, 32), 32)
+        values = tokens_ref[window, :].astype(F32)
+        inverse = lax.rsqrt(jnp.mean(values * values, axis=-1, keepdims=True) + EPSILON)
+        normed_out[window, :] = (values * inverse * gain_ref[...]).astype(BF16)
+        return nothing
+
+    lax.fori_loop(0, rows // 32, norm_rows, 0)
+    cosine, sine = cosine_ref[...], sine_ref[...]
+    half = HEAD_DIM // 2
+
+    def project(column, count):
+        window = pl.ds(column, count)
+        product = jnp.dot(normed_out[...], weights_out[:, window], preferred_element_type=F32)
+        return product.T
+
+    def turned(values, gain):
+        mean = jnp.mean(values * values, axis=0, keepdims=True)
+        values = values * lax.rsqrt(mean + EPSILON) * gain
+        first, second = values[:half], values[half:]
+        return jnp.concatenate(
+            [first * cosine - second * sine, second * cosine + first * sine], axis=0
+        ).astype(BF16)
+
+    group = HEADS // KV_HEADS
+    kv_width = KV_HEADS * HEAD_DIM
+    copies[0].wait_recv()
+    locals_[0].wait()
+
+    def key_chunk(index, nothing):
+        products = project(pl.multiple_of(index * 256, 256), 256)
+        for member in range(4):
+            raw = products[member * HEAD_DIM : (member + 1) * HEAD_DIM]
+            pair = index * 4 + member
+            key_out[pair] = raw
+            key = turned(raw, key_gain_ref[...])
+            for twin in range(group):
+                home[group * pair + twin, HEAD_DIM : 2 * HEAD_DIM, :] = key
+        return nothing
+
+    lax.fori_loop(0, KV_HEADS // 4, key_chunk, 0)
+    copies[1].wait_recv()
+    locals_[1].wait()
+
+    def value_chunk(index, nothing):
+        products = project(pl.multiple_of(kv_width + index * 256, 256), 256)
+        for member in range(4):
+            value = products[member * HEAD_DIM : (member + 1) * HEAD_DIM].astype(BF16)
+            for twin in range(group):
+                home[group * (index * 4 + member) + twin, 2 * HEAD_DIM : 3 * HEAD_DIM, :] = value
+        return nothing
+
+    lax.fori_loop(0, KV_HEADS // 4, value_chunk, 0)
+    copies[2].wait_recv()
+    locals_[2].wait()
+
+    def block_copy(step):
+        peer = lax.rem(place + step, RING)
+        return pltpu.make_async_remote_copy(
+            src_ref=home.at[peer],
+            dst_ref=qkv_out.at[place],
+            send_sem=send_sem.at[step],
+            recv_sem=recv_sem.at[step],
+            device_id=(peer, core),
+            device_id_type=MESH,
+        )
+
+    def query_chunk(index, nothing):
+        products = project(pl.multiple_of(2 * kv_width + index * 256, 256), 256)
+        for member in range(4):
+            raw = products[member * HEAD_DIM : (member + 1) * HEAD_DIM]
+            head = index * 4 + member
+            query_out[head] = raw
+            home[head, 0:HEAD_DIM, :] = turned(raw, query_gain_ref[...])
+
+            @pl.when(head != place)
+            def _():
+                block_copy(lax.rem(head - place + RING, RING)).start()
+
+        return nothing
+
+    lax.fori_loop(0, HEADS // 4, query_chunk, 0)
+    qkv_out[place] = home[place]
+
+    def settle(step, nothing):
+        block_copy(step).wait()
+        start_copy(step).wait()
+        return nothing
+
+    lax.fori_loop(1, RING, settle, 0)
+    for copy in copies:
+        copy.wait_send()
+
+
+def front_call(call_id, *inputs):
+    rows, width = inputs[0].shape
+    total = (HEADS + 2 * KV_HEADS) * HEAD_DIM
+    return pl.pallas_call(
+        front_kernel,
+        out_shape=(
+            jax.ShapeDtypeStruct((RING, 3 * HEAD_DIM, rows), BF16),
+            jax.ShapeDtypeStruct((RING, 1, rows), jnp.int32),
+            jax.ShapeDtypeStruct((HEADS, HEAD_DIM, rows), F32),
+            jax.ShapeDtypeStruct((KV_HEADS, HEAD_DIM, rows), F32),
+            jax.ShapeDtypeStruct((rows, width), BF16),
+            jax.ShapeDtypeStruct((width, total), BF16),
+        ),
+        in_specs=[VMEM_SPEC] * len(inputs),
+        out_specs=(VMEM_SPEC,) * 6,
+        scratch_shapes=[
+            pltpu.VMEM((RING, 3 * HEAD_DIM, rows), BF16),
+            pltpu.SemaphoreType.DMA((3,)),
+            pltpu.SemaphoreType.DMA((RING,)),
+            pltpu.SemaphoreType.DMA((RING,)),
+            pltpu.SemaphoreType.DMA((RING,)),
+            pltpu.SemaphoreType.DMA((RING,)),
+            pltpu.SemaphoreType.DMA((3,)),
+            pltpu.SemaphoreType.DMA((3,)),
+        ],
+        compiler_params=pltpu.CompilerParams(
+            collective_id=call_id, has_side_effects=True, vmem_limit_bytes=48 << 20
+        ),
+        name="front_heads",
+    )(*inputs)
 
 
 def both(block, axis):
@@ -1123,33 +1422,26 @@
     rows, width = tokens.shape[1], tokens.shape[2]
     resid_in = tokens[0].astype(F32)
     pos_local = doc_pos[0]
-    q_full, k_full, v_full, o_full = (
-        both(w_query, 0),
-        both(w_key, 0),
-        both(w_value, 0),
-        both(w_out, 0),
-    )
-    gate_full, up_full, down_full = both(w_gate, 0), both(w_up, 0), both(w_down, 0)
-    starts_local = place * rows + jnp.arange(rows, dtype=jnp.int32) - pos_local
-    starts = lax.all_gather(starts_local, "ctx", axis=0, tiled=False)
-    first = starts[:, 0] // BLOCK
+    o_full, gate_full = both(w_out, 0), both(w_gate, 0)
+    up_full, down_full = both(w_up, 0), both(w_down, 0)
+    own_starts = place * rows + jnp.arange(rows, dtype=jnp.int32) - pos_local
+    cosine, sine = angle_parts(pos_local)
+    qkv, starts, query_raw, key_raw, normed_low, kvq_full = front_call(
+        1,
+        tokens[0],
+        attn_gain[None, :],
+        w_query,
+        w_key,
+        w_value,
+        query_gain[:, None],
+        key_gain[:, None],
+        cosine,
+        sine,
+        own_starts[None, :],
+    )
+    first = starts[:, 0, 0] // BLOCK
     own_index = jnp.arange(RING, dtype=jnp.int32)
-    clear = jnp.minimum((starts[:, -1] + BLOCK - 1) // BLOCK, own_index)
-    starts = starts[:, None, :]
-
-    normed_low = rms_norm(resid_in, attn_gain).astype(BF16)
-    query_raw = dot_dims(q_full, normed_low, 0, 1).reshape(HEADS, HEAD_DIM, rows)
-    key_raw = dot_dims(k_full, normed_low, 0, 1).reshape(KV_HEADS, HEAD_DIM, rows)
-    value_raw = dot_dims(v_full, normed_low, 0, 1).reshape(KV_HEADS, HEAD_DIM, rows)
-    query_low = turn_heads(head_norm(query_raw, query_gain), pos_local, 1.0).astype(BF16)
-    key_low = turn_heads(head_norm(key_raw, key_gain), pos_local, 1.0).astype(BF16)
-    value_low = value_raw.astype(BF16)
-    group = HEADS // KV_HEADS
-    qkv_home = jnp.concatenate(
-        [query_low, jnp.repeat(key_low, group, axis=0), jnp.repeat(value_low, group, axis=0)],
-        axis=1,
-    )
-    qkv = exchange(qkv_home, 1)
+    clear = jnp.minimum((starts[:, 0, -1] + BLOCK - 1) // BLOCK, own_index)
     mixed_far, inverse_total = attend(first, clear, qkv, starts)
     mixed_t = exchange(mixed_far, 2).reshape(HEADS * HEAD_DIM, rows)
 
@@ -1190,50 +1482,31 @@
         mixed_far,
         inverse_total,
     )
-    back_home = back_home.astype(F32)
-
-    def half_of(block):
-        gathered = both(block, 0)
-        part = gathered.shape[1] // 2
-        return lax.dynamic_slice_in_dim(gathered, core * part, part, 1)
-
-    query_turned = turn_heads(back_home[:, :HEAD_DIM], pos_local, -1.0)
-    key_value = back_home[:, HEAD_DIM:].reshape(KV_HEADS, group, 2 * HEAD_DIM, rows).sum(axis=1)
-    key_turned = turn_heads(key_value[:, :HEAD_DIM], pos_local, -1.0)
-    query_back, query_terms = head_norm_back(query_raw, query_gain, query_turned)
-    key_back, key_terms = head_norm_back(key_raw, key_gain, key_turned)
-    query_back = query_back.astype(BF16).reshape(HEADS * HEAD_DIM, rows)
-    key_back = key_back.astype(BF16).reshape(KV_HEADS * HEAD_DIM, rows)
-    value_back = key_value[:, HEAD_DIM:].astype(BF16).reshape(KV_HEADS * HEAD_DIM, rows)
-    back_t = jnp.concatenate([query_back, key_back, value_back], axis=0)
-    (qkv_grads,) = spread_call(
-        qkv_parts(),
-        (128, 128),
-        (both(back_t, 1), half_of(normed_low)),
-        (jax.ShapeDtypeStruct((128, width // 2), F32),),
-        6,
-        "spread_qkv",
-    )
-    grad_normed = (
-        dot_dims(query_back, q_full, 0, 1)
-        + dot_dims(key_back, k_full, 0, 1)
-        + dot_dims(value_back, v_full, 0, 1)
-    )
-    input_part, attn_terms = rms_back(resid_in, attn_gain, grad_normed)
-    d_tokens = (grad_middle + input_part)[None]
-    gain_totals = lax.psum(
-        (jnp.sum(attn_terms, axis=0), jnp.sum(ffn_terms, axis=0), query_terms, key_terms),
-        ("ctx", "fsdp"),
+    d_tokens, qkv_grads, gain_totals = tail_call(
+        4,
+        back_home,
+        query_raw,
+        key_raw,
+        cosine,
+        sine,
+        query_gain[:, None],
+        key_gain[:, None],
+        kvq_full,
+        normed_low,
+        tokens[0],
+        attn_gain[None, :],
+        grad_middle,
+        jnp.sum(ffn_terms, axis=0, keepdims=True),
     )
     return (
         output,
-        d_tokens,
+        d_tokens[None],
         gain_totals[0],
         qkv_grads[:64].T,
         qkv_grads[64:96].T,
         qkv_grads[96:].T,
-        gain_totals[2],
-        gain_totals[3],
+        gain_totals[2, :HEAD_DIM],
+        gain_totals[3, :HEAD_DIM],
         out_t.T,
         gain_totals[1],
         gate_t.T,

time: 513 us -> 409 us (0.80)
  blocking collectives: 59.3 us -> 0 us
  waiting for transfers between devices: 17.9 us -> 2.62 us
  other arithmetic: 14.9 us -> 3.04 us
  matrix products: 60 us -> 49.3 us
  Pallas kernels: 327 us -> 321 us
    pallas_call x1 -> x2, Pallas kernels: 31.7 us -> 102 us  [the longest x1 52.3 us: tail_call(): pl.pallas_call(tail_kernel, out_shape=(jax.ShapeDtypeStruct((rows, width)...]
    pallas_call x2 -> x1, Pallas kernels: 60.9 us -> 17.5 us  [exchange(): pl.pallas_call(exchange_kernel, out_shape=jax.ShapeDtypeStruct(blocks.sha...]
    psum x1 -> x0, blocking collectives: 38.1 us -> none  [heads_body(): lax.psum((jnp.sum(attn_terms, axis=0), jnp.sum(ffn_terms, axis=0), query_...]
    pallas_call x1, Pallas kernels: 207 us -> 173 us  [back_call(): pl.pallas_call(back_kernel, out_shape=(jax.ShapeDtypeStruct((wide, width...]
    all_gather x1 -> x0, blocking collectives: 21.3 us -> none  [heads_body(): starts = lax.all_gather(starts_local, 'ctx', axis=0, tiled=False)]
    all_gather x9 -> x4, waiting for transfers between devices: 13.6 us -> 0.05 us  [both(): return lax.all_gather(block, 'fsdp', axis=axis, tiled=True)]
    dot_general x8 -> x2, matrix products: 13.4 us -> 3.33 us  [dot_dims(): lax.dot_general(left_mat, right_mat, (((left_dim,), (right_dim,)), ((), (...]
  transfers between devices with their start and end apart: 9 -> 4, of which waited for: 2 -> 0; matrix products, arithmetic and copies ran while one was open for 9% -> 5% of each run, Pallas kernels for 17% -> 24%
where the time goes in v3:
time: 409 us; the launch traced here: 405 us
  Pallas kernels  321 us (78%)
  matrix products  49.3 us (12%)
  local copies, waits for them, and re-layouts  14.5 us (4%)
  between operations  14.2 us (3%)
    pallas_call x1, Pallas kernels, back_call(): pl.pallas_call(back_kernel, out_shape=(jax.ShapeDtypeStruct((wide, width...  173 us
    pallas_call x1, Pallas kernels, tail_call(): pl.pallas_call(tail_kernel, out_shape=(jax.ShapeDtypeStruct((rows, width)...  52.3 us
    pallas_call x1, Pallas kernels, front_call(): pl.pallas_call(front_kernel, out_shape=(jax.ShapeDtypeStruct((RING, 3 * H...  50.2 us
    pallas_call x1, Pallas kernels, attend(): pl.pallas_call(attend_kernel, out_shape=(jax.ShapeDtypeStruct((blocks, HE...  28.4 us
    dot_general x3, matrix products, against(): lax.dot_general(left_mat, right_mat, (((1,), (1,)), ((), ())), preferred_...  22.5 us
    pallas_call x1, Pallas kernels, exchange(): pl.pallas_call(exchange_kernel, out_shape=jax.ShapeDtypeStruct(blocks.sha...  17.5 us
    dot_general x1, matrix products, heads_body(): up_pre = jnp.dot(ffn_low, up_full, preferred_element_type=F32)  8.26 us
  transfers between devices with their start and end apart: 4, of which 0 were waited for; matrix products, arithmetic and copies ran while one was open for 5% of the time, Pallas kernels for 24%

profile of v3, /device:TPU:15, one launch (start us, length us, event | category | flops | bytes accessed | tf_op | source)
XLA Modules:
  0.0 404.8 jit_solution(4159857091059555227)
XLA Ops:
  7.2 0.7 all-gather.5.cloned.1.call-update
  8.0 0.7 all-gather.9.cloned.1.call-update
  8.8 0.7 all-gather.7.cloned.1.call-update
  10.6 50.2 %front_heads.1 = (bf16[16,192,256]{2,1,0:T(8,128)(2,1)}, s32[16,1,256]{2,1,0:T(1,128)S(1)}, f32[16,64,256]{2,1,0:T(8,128)S(1)}, f32[8,64,256]{2,1,0:T(8,128)S(1)...) custom-call(bf16[256,1024]{1,0:T(8,128)(2,1)S(1)} %bitcast.53, f32[1,1024]{1,0:T(1,128)S(1)} %bitcast.55, ...), custom_call_target="tpu_custom_call" | custom-call | tf_op jit(solution)/shard_map/front_heads/pallas_call | solution.py:1371
  60.8 1.0 copy-done.2
  61.8 0.8 copy-done.5
  62.6 0.8 copy-done.6
  63.4 0.7 add_reduce_fusion
  64.7 28.4 %attend_forward.1 = (bf16[16,64,256]{2,1,0:T(8,128)(2,1)}, f32[16,1,256]{2,1,0:T(1,128)}) custom-call(s32[16]{0:T(128)} %get-tuple-element.69.first_ref, s32[16]{0:T(128)} %get-tuple-element.70.clear_ref, bf16[16,192,256]{2,1,0:T(8,128)(2,1)} %get-tuple-element.30.qkv_ref, s32[16,1,256]{2,1,0:T(1,128)} %copy-done.11), custom_call_target="tpu_custom_call" | custom-call | tf_op jit(solution)/shard_map/attend_forward/pallas_call | solution.py:437
  93.1 17.5 %exchange_heads.1 = bf16[16,64,256]{2,1,0:T(8,128)(2,1)} custom-call(bf16[16,64,256]{2,1,0:T(8,128)(2,1)} %get-tuple-element.31.src.part_ref), custom_call_target="tpu_custom_call" | custom-call | tf_op jit(solution)/shard_map/exchange_heads/pallas_call | solution.py:363
  110.6 2.6 multiply_reduce_fusion.2
  113.5 8.3 %fusion.9 = f32[256,4608]{1,0:T(8,128)} fusion(bf16[256,1024]{1,0:T(8,128)(2,1)S(1)} %multiply_convert_fusion.3.ffn_ref, bf16[1024,4608]{1,0:T(8,128)(2,1)} %all-gather.9.cloned.1.call-done), kind=kOutput, calls=%fused_computation.44 | convolution fusion | flops 2415919104 | bytes 14680064 | tf_op jit(solution)/shard_map/dot_general | solution.py:1451
  121.8 7.9 %fusion.8 = f32[256,4608]{1,0:T(8,128)} fusion(bf16[256,1024]{1,0:T(8,128)(2,1)S(1)} %multiply_convert_fusion.3.ffn_ref, bf16[1024,4608]{1,0:T(8,128)(2,1)} %all-gather.7.cloned.1.call-done), kind=kOutput, calls=%fused_computation.43 | convolution fusion | flops 2415919104 | bytes 14680064 | tf_op jit(solution)/shard_map/dot_general | solution.py:1450
  129.7 13.4 %multiply_convert_fusion = (bf16[256,4608]{1,0:T(8,128)(2,1)S(1)}, bf16[256,4608]{1,0:T(8,128)(2,1)S(1)}, bf16[256,4608]{1,0:T(8,128)(2,1)}) fusion(f32[256,4608]{1,0:T(8,128)} %fusion.8, f32[256,4608]{1,0:T(8,128)} %fusion.9, bf16[4608,1024]{1,0:T(8,128)(2,1)} %all-gather.11.cloned.1.call-done, bf16[1,256,1024]{2,1,0:T(8,128)(2,1)S(1)} %copy-done.20), kind=kOutput, calls=%fused_computation | convolution fusion | flops 2433613824 | bytes 26476544 | tf_op jit(solution)/shard_map/dot_general | solution.py:68
  143.2 2.6 fusion.10
  145.9 6.4 %multiply_reduce_fusion = (f32[1024]{0:T(1024)}, f32[256]{0:T(256)S(1)}, f32[256,1024]{1,0:T(8,128)S(1)}) fusion(f32[256,1024]{1,0:T(8,128)S(1)} %get-tuple-element.67, f32[256]{0:T(256)S(1)} %get-tuple-element.63, f32[1024]{0:T(1024)S(1)} %copy-done.28, f32[256,1024]{1,0:T(8,128)S(1)} %fusion.10, bf16[256,4608]{1,0:T(8,128)(2,1)S(1)} %get-tuple-element.51.up_ref, ...), kind=kOutput, calls=%fused_computation.12 | convolution fusion | flops 2417752832 | bytes 14952448 | tf_op jit(solution)/shard_map/dot_general | solution.py:68
  152.3 1.4 fusion.6
  153.7 0.8 copy-done.21
  154.5 0.7 fusion.2
  155.2 1.0 copy.34
  156.2 172.6 %backward_spread.1 = (f32[288,512]{1,0:T(8,128)}, f32[288,512]{1,0:T(8,128)}, f32[64,2304]{1,0:T(8,128)}, f32[64,512]{1,0:T(8,128)}, bf16[16,192,256]{2,1,0:T(8,128)(2,1)}) custom-call(bf16[256,4608]{1,0:T(8,128)(2,1)} %copy-done.19, bf16[256,4608]{1,0:T(8,128)(2,1)} %copy-done.18, bf16[256,4608]{1,0:T(8,128)(2,1)} %get-tuple-element.53.hidden_ref, ...), custom_call_target="tpu_custom_call" | custom-call | tf_op jit(solution)/shard_map/backward_spread/pallas_call | solution.py:893
  328.9 52.3 %backward_tail.1 = (f32[256,1024]{1,0:T(8,128)}, f32[128,512]{1,0:T(8,128)}, f32[4,1024]{1,0:T(4,128)}) custom-call(bf16[16,192,256]{2,1,0:T(8,128)(2,1)} %get-tuple-element.33.back_ref, f32[16,64,256]{2,1,0:T(8,128)} %copy-done.2, f32[8,64,256]{2,1,0:T(8,128)} %copy-done.5, f32[32,256]{1,0:T(8,128)} %copy-done.10, f32[32,256]{1,0:T(8,128)} %copy-done.9, ...), custom_call_target="tpu_custom_call" | custom-call | tf_op jit(solution)/shard_map/backward_tail/pallas_call | solution.py:1163
  381.1 1.3 slice_bitcast_fusion.3
  382.4 1.4 fusion.7
  383.8 1.6 slice_bitcast_fusion
  385.4 1.5 slice_bitcast_fusion.1
  386.9 7.2 %fusion.3 = bf16[1,256,1024]{2,1,0:T(8,128)(2,1)} fusion(f32[256,1024]{1,0:T(8,128)S(1)} %copy-done.14, bf16[256,4608]{1,0:T(8,128)(2,1)S(1)} %copy-done.17, bf16[4608,1024]{1,0:T(8,128)(2,1)} %all-gather.11.cloned.1.call-done), kind=kOutput, calls=%fused_computation.11 | convolution fusion | flops 2416443392 | bytes 13369344 | tf_op jit(solution)/shard_map/dot_general | solution.py:1455
  394.2 1.0 copy.42
  395.1 0.7 copy.43
  395.8 0.8 copy.44
  396.6 0.8 copy.45
  397.4 0.8 copy.46
  (77 shorter events, 2.0 us)
Async XLA Ops:
  7.2 103.5 %all-gather.5.cloned.1.call-start = ((), (), s32[]{:S(2)}) async-start(), calls=%async_computation | async-start | bytes 3145728 | tf_op jit(solution)/shard_map/all_gather | solution.py:1401
  7.9 105.6 %all-gather.9.cloned.1.call-start = ((), (), s32[]{:S(2)}) async-start(), calls=%async_computation.2 | async-start | bytes 14155776 | tf_op jit(solution)/shard_map/all_gather | solution.py:1401
  8.7 1.4 copy-start.30
  8.7 1.5 copy-start.31
  8.7 1.6 copy-start.29
  8.7 1.8 copy-start
  8.7 1.8 copy-start.1
  8.7 1.8 copy-start.3
  8.7 1.8 copy-start.4
  8.7 1.8 copy-start.12
  8.7 113.0 %all-gather.7.cloned.1.call-start = ((), (), s32[]{:S(2)}) async-start(), calls=%async_computation.1 | async-start | bytes 14155776 | tf_op jit(solution)/shard_map/all_gather | solution.py:1401
  9.5 120.2 %all-gather.11.cloned.1.call-start = ((), (), s32[]{:S(2)}) async-start(), calls=%async_computation.3 | async-start | bytes 14155776 | tf_op jit(solution)/shard_map/all_gather | solution.py:1401
  10.2 103.1 %copy-start.7 = (f32[64,1]{1,0:T(8,128)}, f32[64,1]{1,0:T(8,128)S(1)}, u32[]{:S(2)}) copy-start(f32[64,1]{1,0:T(8,128)S(1)} %copy.32.query_gain_ref) | copy-start | bytes 772
  10.3 103.0 %copy-start.8 = (f32[64,1]{1,0:T(8,128)}, f32[64,1]{1,0:T(8,128)S(1)}, u32[]{:S(2)}) copy-start(f32[64,1]{1,0:T(8,128)S(1)} %copy.33.key_gain_ref) | copy-start | bytes 772
  10.5 102.7 %copy-start.9 = (f32[32,256]{1,0:T(8,128)}, f32[32,256]{1,0:T(8,128)S(1)}, u32[]{:S(2)}) copy-start(f32[32,256]{1,0:T(8,128)S(1)} %get-tuple-element.60.sine_ref) | copy-start | bytes 98308
  10.5 102.7 %copy-start.10 = (f32[32,256]{1,0:T(8,128)}, f32[32,256]{1,0:T(8,128)S(1)}, u32[]{:S(2)}) copy-start(f32[32,256]{1,0:T(8,128)S(1)} %get-tuple-element.61.cosine_ref) | copy-start | bytes 98308
  10.6 102.7 %copy-start.28 = (f32[1024]{0:T(1024)S(1)}, f32[1024]{0:T(1024)}, u32[]{:S(2)}) copy-start(f32[1024]{0:T(1024)} %param.24) | copy-start | bytes 12292
  63.4 1.3 copy-start.11
  113.3 39.0 %copy-start.13 = (f32[256,1024]{1,0:T(8,128)}, f32[256,1024]{1,0:T(8,128)S(1)}, u32[]{:S(2)}) copy-start(f32[256,1024]{1,0:T(8,128)S(1)} %get-tuple-element.67) | copy-start | bytes 3145732
  113.5 8.3 %copy-start.16 = (bf16[256,1024]{1,0:T(8,128)(2,1)}, bf16[256,1024]{1,0:T(8,128)(2,1)S(1)}, u32[]{:S(2)}) copy-start(bf16[256,1024]{1,0:T(8,128)(2,1)S(1)} %multiply_convert_fusion.3.ffn_ref) | copy-start | bytes 1572868
  121.8 8.0 %copy-start.20 = (bf16[1,256,1024]{2,1,0:T(8,128)(2,1)S(1)}, bf16[1,256,1024]{2,1,0:T(8,128)(2,1)}, u32[]{:S(2)}) copy-start(bf16[1,256,1024]{2,1,0:T(8,128)(2,1)} %param.28) | copy-start | bytes 1572868
  129.7 13.5 %copy-start.15 = (bf16[1024,4608]{1,0:T(8,128)(2,1)S(1)}, bf16[1024,4608]{1,0:T(8,128)(2,1)}, u32[]{:S(2)}) copy-start(bf16[1024,4608]{1,0:T(8,128)(2,1)} %all-gather.7.cloned.1.call-done) | copy-start | bytes 28311556
  143.2 2.6 copy-start.19
  143.2 2.6 copy-start.18
  145.8 8.6 %copy-start.22 = (bf16[1024,1024]{1,0:T(8,128)(2,1)S(1)}, bf16[1024,1024]{1,0:T(8,128)(2,1)}, u32[]{:S(2)}) copy-start(bf16[1024,1024]{1,0:T(8,128)(2,1)} %all-gather.5.cloned.1.call-done) | copy-start | bytes 6291460
  328.9 58.0 %copy-start.14 = (f32[256,1024]{1,0:T(8,128)S(1)}, f32[256,1024]{1,0:T(8,128)}, u32[]{:S(2)}) copy-start(f32[256,1024]{1,0:T(8,128)} %copy-done.13) | copy-start | bytes 3145732
  328.9 58.0 %copy-start.17 = (bf16[256,4608]{1,0:T(8,128)(2,1)S(1)}, bf16[256,4608]{1,0:T(8,128)(2,1)}, u32[]{:S(2)}) copy-start(bf16[256,4608]{1,0:T(8,128)(2,1)} %get-tuple-element.53.hidden_ref) | copy-start | bytes 7077892
  386.9 7.3 %copy-start.23 = (f32[256,1024]{1,0:T(8,128)S(1)}, f32[256,1024]{1,0:T(8,128)}, u32[]{:S(2)}) copy-start(f32[256,1024]{1,0:T(8,128)} %get-tuple-element.38) | copy-start | bytes 3145732
  386.9 8.2 %copy-start.27 = (f32[64,512]{1,0:T(8,128)S(1)}, f32[64,512]{1,0:T(8,128)}, u32[]{:S(2)}) copy-start(f32[64,512]{1,0:T(8,128)} %get-tuple-element.41) | copy-start | bytes 393220
  386.9 8.9 %copy-start.26 = (f32[288,512]{1,0:T(8,128)S(1)}, f32[288,512]{1,0:T(8,128)}, u32[]{:S(2)}) copy-start(f32[288,512]{1,0:T(8,128)} %get-tuple-element.42) | copy-start | bytes 1769476
  386.9 9.7 %copy-start.25 = (f32[288,512]{1,0:T(8,128)S(1)}, f32[288,512]{1,0:T(8,128)}, u32[]{:S(2)}) copy-start(f32[288,512]{1,0:T(8,128)} %get-tuple-element.43) | copy-start | bytes 1769476
  394.2 3.3 copy-start.24
  (4 other events, 3.4 us)
Sparse Core Ops, SparseCore 0:
  9.6 12.3 all-gather.4
  23.6 23.0 all-gather.8
  48.2 23.0 all-gather.6
  72.6 23.2 all-gather.10

commit v4 on v3

--- a/solution.py
+++ b/solution.py
@@ -321,6 +321,7 @@
 BLOCK = 256
 RING = 16
 VMEM_SPEC = pl.BlockSpec(memory_space=pltpu.VMEM)
+HBM_SPEC = pl.BlockSpec(memory_space=pltpu.HBM)
 SMEM_SPEC = pl.BlockSpec(memory_space=pltpu.SMEM)
 F32 = jnp.float32
 BF16 = jnp.bfloat16
@@ -527,9 +528,11 @@
                 value = value + self.came[2][depth, window, :].astype(F32)
             finish(self.chain, row, value)
 
-    def drain(self):
+    def drain_first(self):
         for slot in range(8):
             self.copy(0, slot).wait_send()
+
+    def drain_last(self):
         for depth in range(4):
             self.copy(1, depth).wait_send()
         for depth in range(1, 4):
@@ -543,17 +546,25 @@
     pl.semaphore_wait(barrier, len(peers))
 
 
-def turn_into(source, put):
-    for column in range(0, source.shape[1], 128):
-        put(column, source[:, column : column + 128].astype(F32).T.astype(BF16))
+def turn_back(values, cosine, sine):
+    half = HEAD_DIM // 2
+    first, second = values[:half], values[half:]
+    return jnp.concatenate(
+        [first * cosine + second * sine, second * cosine - first * sine], axis=0
+    )
+
+
+def column_norm_back(values, gain, upstream):
+    inverse = lax.rsqrt(jnp.mean(values * values, axis=0, keepdims=True) + EPSILON)
+    scaled = upstream * gain
+    total = jnp.sum(scaled * values, axis=0, keepdims=True) / values.shape[0]
+    return inverse * scaled - values * inverse**3 * total, upstream * values * inverse
 
 
 def back_kernel(
-    gate_ref,
-    up_ref,
-    hidden_ref,
-    cot_ref,
-    middle_ref,
+    pair_own,
+    hidden_hbm,
+    side_own,
     ffn_ref,
     mixed_ref,
     home_ref,
@@ -561,22 +572,40 @@
     start_ref,
     part_ref,
     inv_ref,
+    cosine_ref,
+    sine_ref,
+    query_gain_ref,
+    key_gain_ref,
+    normed_ref,
+    attn_gain_ref,
+    ffn_terms_ref,
+    tokens_hbm,
+    query_hbm,
+    key_hbm,
+    weights_hbm,
+    middle_hbm,
     gate_out,
     up_out,
     down_out,
     out_out,
-    back_out,
-    pair_own,
+    grads_out,
+    tokens_out,
+    gains_out,
     pair_far,
-    side_own,
     side_far,
+    hidden_own,
     hidden_far,
     ffn_far,
     mixed_far,
+    normed_far,
     cot_far,
     back_own,
-    key_value,
-    grad_acc,
+    back_far,
+    turned_own,
+    turned_far,
+    gain_own,
+    gain_came,
+    gain_deep,
     sent_a,
     came_a0,
     came_a1,
@@ -585,99 +614,96 @@
     came_b0,
     came_b1,
     came_b2,
+    tail_sent_a,
+    tail_came_a0,
+    tail_came_a1,
+    tail_came_a2,
+    tail_sent_b,
+    tail_came_b0,
+    tail_came_b1,
+    tail_came_b2,
     send_sems,
     recv_sems,
+    tail_send,
+    tail_recv,
     cot_send,
     cot_recv,
     back_send,
     back_recv,
     core_send,
     core_recv,
+    gain_send,
+    gain_recv,
+    load_sem,
+    weight_sem,
 ):
     place, core = lax.axis_index("ctx"), lax.axis_index("fsdp")
+    x, y, z = lax.rem(place, 2), lax.rem(place // 2, 2), place // 4
     blocks = qkv_ref.shape[0]
     wide = pair_own.shape[1] // 2
     narrow = side_own.shape[1] // RING
     half_hidden = hidden_far.shape[1]
     half_width = ffn_far.shape[1]
+    heads, pairs = query_hbm.shape[0], key_hbm.shape[0]
+    group = heads // pairs
     scale = HEAD_DIM**-0.5
-
-    greet(
-        [(lax.rem(place + step, RING), core) for step in range(1, RING)] + [(place, 1 - core)]
-    )
-
-    def cot_copy(step, peer):
-        return pltpu.make_async_remote_copy(
-            src_ref=home_ref.at[peer],
-            dst_ref=cot_far.at[place],
-            send_sem=cot_send.at[step],
-            recv_sem=cot_recv.at[step],
-            device_id=(peer, core),
-            device_id_type=MESH,
-        )
-
-    for step in range(1, RING):
-        cot_copy(step, lax.rem(place + step, RING)).start()
-    cot_far[place] = home_ref[place]
-
-    def core_copy(source, target, sem):
+    partner = (place, 1 - core)
+
+    def half(part, size):
+        return pl.ds(pl.multiple_of(part * size, 128), size)
+
+    own_hidden = pltpu.make_async_copy(
+        hidden_hbm.at[:, half(core, half_hidden)], hidden_own, load_sem.at[0]
+    )
+    own_hidden.start()
+    middle_load = pltpu.make_async_copy(middle_hbm, tokens_out, load_sem.at[1])
+    middle_load.start()
+    greet([(lax.rem(place + step, RING), core) for step in range(1, RING)] + [partner])
+
+    def remote(source, target, send, recv, peer):
         return pltpu.make_async_remote_copy(
             src_ref=source,
             dst_ref=target,
-            send_sem=core_send.at[sem],
-            recv_sem=core_recv.at[sem],
-            device_id=(place, 1 - core),
+            send_sem=send,
+            recv_sem=recv,
+            device_id=peer,
             device_id_type=MESH,
         )
 
-    def half(part, size):
-        return pl.ds(pl.multiple_of(part * size, 128), size)
+    def cot_copy(step, peer):
+        return remote(
+            home_ref.at[peer], cot_far.at[place], cot_send.at[step], cot_recv.at[step], (peer, core)
+        )
+
+    def core_copy(source, target, sem):
+        return remote(source, target, core_send.at[sem], core_recv.at[sem], partner)
 
     def pair_copy(turn_x, turn_y, depth):
-        x, y, z = lax.rem(place, 2), lax.rem(place // 2, 2), place // 4
         owner = lax.rem(z + depth, 4) * 4 + flip(y, turn_y) * 2 + flip(x, turn_x)
         return core_copy(
-            pair_own.at[owner], pair_far.at[owner], 4 + turn_x * 8 + turn_y * 4 + depth
+            pair_own.at[owner], pair_far.at[owner], 6 + turn_x * 8 + turn_y * 4 + depth
         )
 
     sides = [
         core_copy(ffn_ref.at[:, half(1 - core, half_width)], ffn_far, 0),
         core_copy(mixed_ref.at[half(1 - core, half_width), :], mixed_far, 1),
-        core_copy(hidden_ref.at[:, half(1 - core, half_hidden)], hidden_far, 2),
-        core_copy(side_own, side_far, 3),
+        core_copy(side_own, side_far, 2),
+        core_copy(hidden_hbm.at[:, half(1 - core, half_hidden)], hidden_far, 3),
     ]
-    for copy in sides[:3]:
+    order = []
+    for depth in (2, 1, 3, 0):
+        order += [(1, 1, depth), (1, 0, depth), (0, 1, depth)]
+    order += [(0, 0, depth) for depth in (2, 1, 3, 0)]
+    for copy in sides:
         copy.start()
-
-    def put_side(which):
-        def put(column, value):
-            side_own[which, column : column + 128, :] = value
-
-        return put
-
-    turn_into(cot_ref, put_side(0))
-    turn_into(middle_ref, put_side(1))
-    sides[3].start()
-
-    def put_pair(base):
-        def put(column, value):
-            done = 0
-            while done < 128:
-                owner, row = divmod(column + done, wide)
-                count = min(128 - done, wide - row)
-                pair_own[owner, base + row : base + row + count, :] = value[done : done + count]
-                done += count
-
-        return put
-
-    turn_into(gate_ref, put_pair(0))
-    turn_into(up_ref, put_pair(wide))
-    order = []
-    for depth in (1, 2, 3, 0):
-        order += [(1, 1, depth), (1, 0, depth), (0, 1, depth)]
-    order += [(0, 0, depth) for depth in (1, 2, 3, 0)]
-    for turn_x, turn_y, depth in order:
+    pair_copy(*order[0]).start()
+    for step in range(1, RING):
+        cot_copy(step, lax.rem(place + step, RING)).start()
+    for turn_x, turn_y, depth in order[1:]:
         pair_copy(turn_x, turn_y, depth).start()
+    normed_copy = core_copy(normed_ref.at[:, half(1 - core, half_width)], normed_far, 4)
+    normed_copy.start()
+    cot_far[place] = home_ref[place]
 
     def compute(chain, owner):
         lanes = pl.ds(chain * 256, 256)
@@ -687,13 +713,9 @@
         values = [(0, both_pair)]
         rows = pl.ds(pl.multiple_of(owner * narrow, 16), narrow)
         begin, chunks = (0, 5) if chain == 0 else (5, 4)
-        cols = pl.ds(pl.multiple_of(core * half_hidden + begin * 256, 128), chunks * 256)
-        down = jnp.dot(side_own[0, rows, :], hidden_ref[:, cols], preferred_element_type=F32)
-        down += jnp.dot(
-            side_far[0, rows, :],
-            hidden_far[:, begin * 256 : (begin + chunks) * 256],
-            preferred_element_type=F32,
-        )
+        cols = slice(begin * 256, (begin + chunks) * 256)
+        down = jnp.dot(side_own[0, rows, :], hidden_own[:, cols], preferred_element_type=F32)
+        down += jnp.dot(side_far[0, rows, :], hidden_far[:, cols], preferred_element_type=F32)
         row = 2 * wide
         for chunk in range(chunks):
             values.append((row, down[:, chunk * 256 : chunk * 256 + 256]))
@@ -720,6 +742,7 @@
         Spread(0, compute, sent_a, (came_a0, came_a1, came_a2), send_sems, recv_sems),
         Spread(1, compute, sent_b, (came_b0, came_b1, came_b2), send_sems, recv_sems),
     )
+    own_hidden.wait()
     for copy in sides:
         copy.wait_recv()
 
@@ -734,162 +757,360 @@
         for chain in chains:
             chain.stage_one(0, depth)
 
-    def event(number):
-        @pl.when(lax.rem(number, 2) == 1)
-        def _():
-            for chain in chains:
-                chain.stage_two(lax.rem((number + 1) // 2, 4))
-
-        @pl.when((lax.rem(number, 2) == 1) & (number >= 3))
-        def _():
-            depth = (number - 1) // 2
-            pair_copy(0, 0, depth).wait_recv()
-            for chain in chains:
-                chain.stage_three(depth)
-
-        @pl.when((lax.rem(number, 2) == 1) & (number <= 5))
-        def _():
-            far(lax.rem(number // 2 + 2, 4))
-
-        @pl.when((lax.rem(number, 2) == 0) & (number <= 5))
-        def _():
-            near(lax.rem(number // 2 + 2, 4))
-
+    def onward(depth):
+        for chain in chains:
+            chain.stage_two(depth)
+
+    def deeper(depth):
+        pair_copy(0, 0, depth).wait_recv()
+        for chain in chains:
+            chain.stage_three(depth)
+
+    near(2)
+    far(2)
     near(1)
-    far(1)
-    near(2)
-
-    key_value[0] = jnp.zeros(key_value.shape[1:], BF16)
-
-    def prepare(j, nothing):
-        packed = qkv_ref[j, HEAD_DIM : 3 * HEAD_DIM, :].astype(F32)
-        key_value[j + 1] = packed.T.astype(BF16)
-        grad_acc[j + 1] = jnp.zeros(grad_acc.shape[1:], F32)
-        return nothing
-
-    grad_acc[0] = jnp.zeros(grad_acc.shape[1:], F32)
-    lax.fori_loop(0, blocks, prepare, 0)
 
     def back_copy(step, peer):
-        return pltpu.make_async_remote_copy(
-            src_ref=back_own.at[peer],
-            dst_ref=back_out.at[place],
-            send_sem=back_send.at[step],
-            recv_sem=back_recv.at[step],
-            device_id=(peer, core),
-            device_id_type=MESH,
-        )
-
-    def flush(j):
-        turned = grad_acc[j + 1].T.astype(BF16)
-        back_own[j, HEAD_DIM : 3 * HEAD_DIM, :] = turned
-
-        @pl.when(j != place)
-        def _():
-            back_copy(lax.rem(j - place + RING, RING), j).start()
-
-    def per_query(i):
-        @pl.when(i != place)
-        def _():
-            step = lax.rem(place - i + RING, RING)
-            cot_copy(step, lax.rem(place + step, RING)).wait_recv()
-
-        empty = jnp.zeros((HEAD_DIM, BLOCK), BF16)
-        query = qkv_ref[i, 0:HEAD_DIM, :] * jnp.asarray(scale, BF16)
-        query_t = jnp.concatenate([query, empty], axis=0)
-        cot = cot_far[i]
-        cot_t = jnp.concatenate([empty, cot], axis=0)
-        query_nat = transposed(query_t)
-        cot_nat = transposed(cot_t)
-        start = start_ref[i]
-        inverse = inv_ref[i]
-        delta = jnp.sum(cot.astype(F32) * part_ref[i].astype(F32), axis=0, keepdims=True)
-        query_place = i * BLOCK + lax.broadcasted_iota(jnp.int32, (1, BLOCK), 1)
-
-        def step(diagonal, j):
-            block = key_value[j + 1]
-            scores = jnp.dot(block, query_t, preferred_element_type=F32)
-            grad_probs = jnp.dot(block, cot_t, preferred_element_type=F32)
-            key_place = j * BLOCK + lax.broadcasted_iota(jnp.int32, scores.shape, 0)
-            ok = key_place >= start
-            if diagonal:
-                ok = ok & (key_place <= query_place)
-            probs = jnp.where(ok, jnp.exp(scores) * inverse, 0.0)
-            grad_scores = (probs * (grad_probs - delta)).astype(BF16)
-            update = jnp.dot(grad_scores, query_nat, preferred_element_type=F32)
-            update += jnp.dot(probs.astype(BF16), cot_nat, preferred_element_type=F32)
-            grad_acc[j + 1] += update
-            return jnp.dot(
-                qkv_ref[jnp.maximum(j, 0), HEAD_DIM : 2 * HEAD_DIM, :],
-                grad_scores,
-                preferred_element_type=F32,
+        return remote(
+            back_own.at[peer],
+            back_far.at[place],
+            back_send.at[step],
+            back_recv.at[step],
+            (peer, core),
+        )
+
+    def attention(scaled, natural, delta_ref, query_acc, key_nat, value_nat, pair_acc):
+        def prepare(i):
+            @pl.when(i != place)
+            def _():
+                step = lax.rem(place - i + RING, RING)
+                cot_copy(step, lax.rem(place + step, RING)).wait_recv()
+
+            query = qkv_ref[i, 0:HEAD_DIM, :] * jnp.asarray(scale, BF16)
+            cot = cot_far[i]
+            scaled[i] = query
+            natural[i] = transposed(jnp.concatenate([query, cot], axis=0))
+            delta_ref[i] = jnp.sum(
+                cot.astype(F32) * part_ref[i].astype(F32), axis=0, keepdims=True
             )
-
-        pairs = (jnp.minimum(i, 8) + 1) // 2
-
-        def two(index, acc):
-            j = i - 2 * pairs + 2 * index
-            return acc + step(False, j) + step(False, j + 1)
-
-        acc = lax.fori_loop(0, pairs, two, step(True, i))
-        back_own[i, 0:HEAD_DIM, :] = (acc * scale).astype(BF16)
-
-        @pl.when(i >= 8)
-        def _():
-            flush(i - 8)
-
-    def rest(j, nothing):
-        flush(j)
-        return nothing
-
-    def per_step(i, nothing):
-        @pl.when(i < blocks)
-        def _():
-            per_query(i)
-
-        @pl.when(i == blocks - 1)
-        def _():
-            lax.fori_loop(blocks - 8, blocks, rest, 0)
-
-        @pl.when((i >= 6) & (lax.rem(i, 3) == 0))
-        def _():
-            event(i // 3 - 1)
-
-        return nothing
-
-    lax.fori_loop(0, 25, per_step, 0)
-    back_out[place] = back_own[place]
+            query_acc[i] = jnp.zeros(query_acc.shape[1:], F32)
+
+        def prepare_one(i, nothing):
+            prepare(i)
+            return nothing
+
+        def per_key(j, nothing):
+            @pl.when(j + 8 < blocks)
+            def _():
+                prepare(j + 8)
+
+            key_nat[...] = transposed(qkv_ref[j, HEAD_DIM : 2 * HEAD_DIM, :])
+            value_nat[...] = transposed(qkv_ref[j, 2 * HEAD_DIM : 3 * HEAD_DIM, :])
+            key_place = j * BLOCK + lax.broadcasted_iota(jnp.int32, (BLOCK, BLOCK), 0)
+
+            def step(diagonal, i):
+                inside = jnp.minimum(i, blocks - 1)
+                start = start_ref[inside] + (i // blocks) * (blocks * BLOCK)
+                scores = jnp.dot(key_nat[...], scaled[inside], preferred_element_type=F32)
+                grad_probs = jnp.dot(value_nat[...], cot_far[inside], preferred_element_type=F32)
+                ok = key_place >= start
+                if diagonal:
+                    query_place = i * BLOCK + lax.broadcasted_iota(jnp.int32, (1, BLOCK), 1)
+                    ok = ok & (key_place <= query_place)
+                probs = jnp.where(ok, jnp.exp(scores) * inv_ref[inside], 0.0)
+                grad_scores = (probs * (grad_probs - delta_ref[inside])).astype(BF16)
+                both_low = jnp.concatenate([grad_scores, probs.astype(BF16)], axis=0)
+                query_acc[i] += jnp.dot(
+                    qkv_ref[j, HEAD_DIM : 2 * HEAD_DIM, :],
+                    grad_scores,
+                    preferred_element_type=F32,
+                )
+                return jnp.dot(both_low, natural[inside], preferred_element_type=F32)
+
+            pair_acc[...] = step(True, j)
+            count = (jnp.minimum(8, blocks - 1 - j) + 1) // 2
+
+            def two(index, carry):
+                i = j + 1 + 2 * index
+                pair_acc[...] += step(False, i) + step(False, i + 1)
+                return carry
+
+            lax.fori_loop(0, count, two, 0)
+            back_own[j, 0:HEAD_DIM, :] = (query_acc[j] * scale).astype(BF16)
+            first = lax.broadcasted_iota(jnp.int32, (BLOCK, 2 * HEAD_DIM), 1) < HEAD_DIM
+            merged = jnp.where(first, pair_acc[0:BLOCK, :], pair_acc[BLOCK:, :])
+            back_own[j, HEAD_DIM : 3 * HEAD_DIM, :] = merged.T.astype(BF16)
+
+            @pl.when(j != place)
+            def _():
+                back_copy(lax.rem(j - place + RING, RING), j).start()
+
+            @pl.when(j == 4)
+            def _():
+                onward(2)
+                far(1)
+
+            @pl.when(j == 9)
+            def _():
+                near(3)
+
+            return nothing
+
+        lax.fori_loop(0, 8, prepare_one, 0)
+        lax.fori_loop(0, blocks, per_key, 0)
+        back_far[place] = back_own[place]
+
+    pl.run_scoped(
+        attention,
+        pltpu.VMEM((blocks, HEAD_DIM, BLOCK), BF16),
+        pltpu.VMEM((blocks, BLOCK, 2 * HEAD_DIM), BF16),
+        pltpu.VMEM((blocks, 1, BLOCK), F32),
+        pltpu.VMEM((blocks + 1, HEAD_DIM, BLOCK), F32),
+        pltpu.VMEM((BLOCK, HEAD_DIM), BF16),
+        pltpu.VMEM((BLOCK, HEAD_DIM), BF16),
+        pltpu.VMEM((2 * BLOCK, 2 * HEAD_DIM), F32),
+    )
+
+    turned_copy = core_copy(turned_own, turned_far, 5)
+
+    def tail_compute(chain, owner):
+        lanes = slice(chain * 256, chain * 256 + 256)
+        own_lanes = pl.ds(pl.multiple_of(core * half_width + chain * 256, 128), 256)
+        values, row = [], 0
+        for size, base in ((heads, 2 * pairs), (pairs, 0), (pairs, pairs)):
+            count = size * HEAD_DIM // RING
+            rows = pl.ds(pl.multiple_of(base * HEAD_DIM + owner * count, 16), count)
+            value = jnp.dot(
+                turned_own[rows, :], normed_ref[:, own_lanes], preferred_element_type=F32
+            )
+            value += jnp.dot(turned_far[rows, :], normed_far[:, lanes], preferred_element_type=F32)
+            values.append((row, value))
+            row += count
+        return values
+
+    def tail_finish(chain, row, value):
+        grads_out[row : row + value.shape[0], chain * 256 : chain * 256 + 256] = value
+
+    tails = (
+        Spread(
+            0,
+            tail_compute,
+            tail_sent_a,
+            (tail_came_a0, tail_came_a1, tail_came_a2),
+            tail_send,
+            tail_recv,
+        ),
+        Spread(
+            1,
+            tail_compute,
+            tail_sent_b,
+            (tail_came_b0, tail_came_b1, tail_came_b2),
+            tail_send,
+            tail_recv,
+        ),
+    )
+
+    near_x = (place + 1 - 2 * x, core)
+    near_y = (place + 2 - 4 * y, core)
+
+    def finish_all(natural, summed, query_ref, key_ref, tokens_ref):
+        loads = [
+            pltpu.make_async_copy(query_hbm, query_ref, load_sem.at[2]),
+            pltpu.make_async_copy(key_hbm, key_ref, load_sem.at[3]),
+            pltpu.make_async_copy(tokens_hbm, tokens_ref, load_sem.at[4]),
+        ]
+        for copy in loads:
+            copy.start()
+        cosine, sine = cosine_ref[...], sine_ref[...]
+
+        def head_rows(index):
+            return pl.ds(pl.multiple_of(index * HEAD_DIM, HEAD_DIM), HEAD_DIM)
+
+        def query_head(head, total):
+            upstream = turn_back(back_far[head, 0:HEAD_DIM, :].astype(F32), cosine, sine)
+            back, terms = column_norm_back(query_ref[head], query_gain_ref[...], upstream)
+            turned_own[head_rows(2 * pairs + head), :] = back.astype(BF16)
+            return total + terms
+
+        def key_head(pair, total):
+            upstream = jnp.zeros((2 * HEAD_DIM, BLOCK), F32)
+            for member in range(group):
+                upstream += back_far[group * pair + member, HEAD_DIM : 3 * HEAD_DIM, :].astype(F32)
+            back, terms = column_norm_back(
+                key_ref[pair],
+                key_gain_ref[...],
+                turn_back(upstream[:HEAD_DIM], cosine, sine),
+            )
+            turned_own[head_rows(pair), :] = back.astype(BF16)
+            turned_own[head_rows(pairs + pair), :] = upstream[HEAD_DIM:].astype(BF16)
+            return total + terms
+
+        def weight_load(part, column):
+            slot = (sent_a, sent_b)[part]
+            return pltpu.make_async_copy(
+                weights_hbm.at[pl.ds(part * 512, 512), pl.ds(pl.multiple_of(column * 256, 256), 256)],
+                slot.at[column, pl.ds(0, 512), :],
+                weight_sem.at[part, column],
+            )
+
+        onward(1)
+        deeper(2)
+        far(3)
+        near(0)
+
+        def arrive(step, nothing):
+            back_copy(step, lax.rem(place + step, RING)).wait_recv()
+            return nothing
+
+        lax.fori_loop(1, RING, arrive, 0)
+        for copy in loads:
+            copy.wait()
+        nothing = jnp.zeros((HEAD_DIM, BLOCK), F32)
+        query_terms = lax.fori_loop(0, heads, query_head, nothing)
+        key_terms = lax.fori_loop(0, pairs, key_head, nothing)
+        turned_copy.start()
+        onward(3)
+        deeper(1)
+        far(0)
+        for row in range(0, turned_own.shape[0], 128):
+            natural[:, row : row + 128] = turned_own[row : row + 128, :].astype(F32).T.astype(BF16)
+        normed_copy.wait_recv()
+        turned_copy.wait_recv()
+
+        def tail_one(index, carry):
+            for chain in tails:
+                chain.stage_one(1 - index // 4, lax.rem(index + 1, 4))
+            return carry
+
+        lax.fori_loop(0, 8, tail_one, 0)
+        onward(0)
+
+        def tail_two(index, carry):
+            for chain in tails:
+                chain.stage_two(lax.rem(index + 1, 4))
+            return carry
+
+        lax.fori_loop(0, 4, tail_two, 0)
+        deeper(3)
+        for chain in chains:
+            chain.drain_first()
+        for part in range(2):
+            for column in range(8):
+                weight_load(part, column).start()
+
+        for part, slots in enumerate((sent_a, sent_b)):
+            total = None
+            for column in range(8):
+                weight_load(part, column).wait()
+                term = dot_dims(
+                    natural[:, column * 256 : column * 256 + 256], slots[column, 0:512, :], 1, 1
+                )
+                total = term if total is None else total + term
+            summed[:, part * 512 : part * 512 + 512] = total
+        middle_load.wait()
+
+        def token_rows(index, total):
+            rows = pl.ds(pl.multiple_of(index * 32, 32), 32)
+            values, upstream = tokens_ref[rows, :].astype(F32), summed[rows, :]
+            inverse = lax.rsqrt(jnp.mean(values * values, axis=-1, keepdims=True) + EPSILON)
+            scaled = upstream * attn_gain_ref[...]
+            weight = jnp.sum(scaled * values, axis=-1, keepdims=True) / values.shape[1]
+            tokens_out[rows, :] += inverse * scaled - values * inverse**3 * weight
+            return total + jnp.sum(upstream * values * inverse, axis=0, keepdims=True)
+
+        terms = lax.fori_loop(
+            0, BLOCK // 32, token_rows, jnp.zeros((1, tokens_ref.shape[1]), F32)
+        )
+        gain_own[0] = jnp.zeros(gain_own.shape[1:], F32)
+        gain_own[0, 0:1, :] = terms
+        gain_own[0, 1:2, :] = ffn_terms_ref[...]
+        gain_own[0, 2:3, 0:HEAD_DIM] = jnp.sum(query_terms.T, axis=0, keepdims=True)
+        gain_own[0, 3:4, 0:HEAD_DIM] = jnp.sum(key_terms.T, axis=0, keepdims=True)
+
+    width = normed_ref.shape[1]
+    pl.run_scoped(
+        finish_all,
+        pltpu.VMEM((BLOCK, turned_own.shape[0]), BF16),
+        pltpu.VMEM((BLOCK, width), F32),
+        pltpu.VMEM((heads, HEAD_DIM, BLOCK), F32),
+        pltpu.VMEM((pairs, HEAD_DIM, BLOCK), F32),
+        pltpu.VMEM((BLOCK, width), BF16),
+    )
+
+    gain_copies = []
+
+    def gain_copy(source, target, sem, peer):
+        copy = remote(source, target, gain_send.at[sem], gain_recv.at[sem], peer)
+        copy.start()
+        gain_copies.append(copy)
+
+    gain_copy(gain_own.at[0], gain_came.at[0], 0, near_x)
+
+    def tail_three(depth, carry):
+        for chain in tails:
+            chain.stage_three(depth)
+        return carry
+
+    lax.fori_loop(1, 4, tail_three, 0)
+    gain_copies[0].wait_recv()
+    gain_own[1] = gain_own[0] + gain_came[0]
+    gain_copy(gain_own.at[1], gain_came.at[1], 1, near_y)
     pair_copy(0, 0, 0).wait_recv()
-    for chain in chains:
-        chain.close(finish)
+    chains[0].close(finish)
+    gain_copies[1].wait_recv()
+    gain_own[2] = gain_own[1] + gain_came[1]
+    gain_copy(gain_own.at[2], gain_came.at[2], 2, partner)
+    chains[1].close(finish)
+    gain_copies[2].wait_recv()
+    gain_own[3] = gain_own[2] + gain_came[2]
+    gain_deep[z] = gain_own[3]
+    for step in range(1, 4):
+        deep = (lax.rem(place + 4 * step, RING), core)
+        gain_copy(gain_own.at[3], gain_deep.at[z], 2 + step, deep)
+    for chain in tails:
+        chain.close(tail_finish)
+    for copy in gain_copies[3:]:
+        copy.wait_recv()
+    gains_out[...] = (gain_deep[0] + gain_deep[1]) + (gain_deep[2] + gain_deep[3])
 
     def settle(step, nothing):
         peer = lax.rem(place + step, RING)
-        back_copy(step, peer).wait()
+        back_copy(step, peer).wait_send()
         cot_copy(step, peer).wait_send()
         return nothing
 
     lax.fori_loop(1, RING, settle, 0)
-    for copy in sides:
+    for copy in sides + [normed_copy, turned_copy] + gain_copies:
         copy.wait_send()
     for turn_x, turn_y, depth in order:
         pair_copy(turn_x, turn_y, depth).wait_send()
     for chain in chains:
-        chain.drain()
-
-
-def back_call(call_id, *inputs):
-    gate_back, qkv = inputs[0], inputs[8]
-    rows, hidden_width = gate_back.shape
-    width = inputs[3].shape[1]
+        chain.drain_last()
+    for chain in tails:
+        chain.drain_first()
+        chain.drain_last()
+
+
+def back_call(call_id, inputs, loads):
+    pair, hidden, side, ffn_low, qkv = (inputs[k] for k in (0, 1, 2, 3, 6))
+    rows, hidden_width = hidden.shape
+    width = ffn_low.shape[1]
     blocks = qkv.shape[0]
     wide, narrow = hidden_width // RING, width // RING
-    chain_rows = (2 * wide + 6 * narrow, 2 * wide + 5 * narrow)
-    buffers = [
-        pltpu.VMEM((slots, chain_rows[chain], 256), BF16)
-        for chain in range(2)
-        for slots in (8, 8, 4, 3)
-    ]
+    total = (HEADS + 2 * KV_HEADS) * HEAD_DIM
+
+    def buffers(sizes):
+        return [
+            pltpu.VMEM((slots, sizes[chain], 256), BF16)
+            for chain in range(2)
+            for slots in (8, 8, 4, 3)
+        ]
+
+    dma = pltpu.SemaphoreType.DMA
+    specs = [VMEM_SPEC] * (len(inputs) + len(loads))
+    specs[1] = HBM_SPEC
+    for index in range(len(inputs), len(specs)):
+        specs[index] = HBM_SPEC
     return pl.pallas_call(
         back_kernel,
         out_shape=(
@@ -897,302 +1118,41 @@
             jax.ShapeDtypeStruct((wide, width // 2), F32),
             jax.ShapeDtypeStruct((narrow, hidden_width // 2), F32),
             jax.ShapeDtypeStruct((narrow, width // 2), F32),
-            jax.ShapeDtypeStruct(qkv.shape, BF16),
+            jax.ShapeDtypeStruct((total // RING, width // 2), F32),
+            jax.ShapeDtypeStruct((rows, width), F32),
+            jax.ShapeDtypeStruct((4, width), F32),
         ),
-        in_specs=[VMEM_SPEC] * len(inputs),
-        out_specs=(VMEM_SPEC,) * 5,
+        in_specs=specs,
+        out_specs=(VMEM_SPEC,) * 7,
         scratch_shapes=[
-            pltpu.VMEM((RING, 2 * wide, rows), BF16),
-            pltpu.VMEM((RING, 2 * wide, rows), BF16),
-            pltpu.VMEM((2, width, rows), BF16),
-            pltpu.VMEM((2, width, rows), BF16),
+            pltpu.VMEM(pair.shape, BF16),
+            pltpu.VMEM(side.shape, BF16),
+            pltpu.VMEM((rows, hidden_width // 2), BF16),
             pltpu.VMEM((rows, hidden_width // 2), BF16),
             pltpu.VMEM((rows, width // 2), BF16),
             pltpu.VMEM((width // 2, rows), BF16),
+            pltpu.VMEM((rows, width // 2), BF16),
             pltpu.VMEM((blocks, HEAD_DIM, BLOCK), BF16),
             pltpu.VMEM(qkv.shape, BF16),
-            pltpu.VMEM((blocks + 1, BLOCK, 2 * HEAD_DIM), BF16),
-            pltpu.VMEM((blocks + 1, BLOCK, 2 * HEAD_DIM), F32),
+            pltpu.VMEM(qkv.shape, BF16),
+            pltpu.VMEM((total, rows), BF16),
+            pltpu.VMEM((total, rows), BF16),
+            pltpu.VMEM((4, 4, width), F32),
+            pltpu.VMEM((3, 4, width), F32),
+            pltpu.VMEM((4, 4, width), F32),
         ]
-        + buffers
-        + [
-            pltpu.SemaphoreType.DMA((2, 15)),
-            pltpu.SemaphoreType.DMA((2, 15)),
-            pltpu.SemaphoreType.DMA((RING,)),
-            pltpu.SemaphoreType.DMA((RING,)),
-            pltpu.SemaphoreType.DMA((RING,)),
-            pltpu.SemaphoreType.DMA((RING,)),
-            pltpu.SemaphoreType.DMA((20,)),
-            pltpu.SemaphoreType.DMA((20,)),
-        ],
+        + buffers((2 * wide + 6 * narrow, 2 * wide + 5 * narrow))
+        + buffers((total // RING, total // RING))
+        + [dma((2, 15))] * 4
+        + [dma((RING,))] * 4
+        + [dma((22,))] * 2
+        + [dma((6,))] * 2
+        + [dma((5,)), dma((2, 8))],
         compiler_params=pltpu.CompilerParams(
             collective_id=call_id, has_side_effects=True, vmem_limit_bytes=63 << 20
         ),
         name="backward_spread",
-    )(*inputs)
-
-
-def turn_back(values, cosine, sine):
-    half = HEAD_DIM // 2
-    first, second = values[:half], values[half:]
-    return jnp.concatenate(
-        [first * cosine + second * sine, second * cosine - first * sine], axis=0
-    )
-
-
-def column_norm_back(values, gain, upstream):
-    inverse = lax.rsqrt(jnp.mean(values * values, axis=0, keepdims=True) + EPSILON)
-    scaled = upstream * gain
-    total = jnp.sum(scaled * values, axis=0, keepdims=True) / values.shape[0]
-    return inverse * scaled - values * inverse**3 * total, upstream * values * inverse
-
-
-def tail_kernel(
-    back_ref,
-    query_ref,
-    key_ref,
-    cosine_ref,
-    sine_ref,
-    query_gain_ref,
-    key_gain_ref,
-    weights_ref,
-    normed_ref,
-    tokens_ref,
-    attn_gain_ref,
-    middle_ref,
-    ffn_terms_ref,
-    tokens_out,
-    grads_out,
-    gains_out,
-    turned_own,
-    turned_far,
-    normed_far,
-    natural,
-    summed,
-    gain_own,
-    gain_came,
-    gain_deep,
-    sent_a,
-    came_a0,
-    came_a1,
-    came_a2,
-    sent_b,
-    came_b0,
-    came_b1,
-    came_b2,
-    send_sems,
-    recv_sems,
-    core_send,
-    core_recv,
-    gain_send,
-    gain_recv,
-):
-    place, core = lax.axis_index("ctx"), lax.axis_index("fsdp")
-    x, y, z = lax.rem(place, 2), lax.rem(place // 2, 2), place // 4
-    near_x = (place + 1 - 2 * x, core)
-    near_y = (place + 2 - 4 * y, core)
-    partner = (place, 1 - core)
-    deep = [(lax.rem(place + 4 * step, RING), core) for step in range(1, 4)]
-    greet([near_x, near_y, partner] + deep)
-    half_width = normed_far.shape[1]
-    heads, pairs = query_ref.shape[0], key_ref.shape[0]
-    group = heads // pairs
-
-    def core_copy(source, target, sem):
-        return pltpu.make_async_remote_copy(
-            src_ref=source,
-            dst_ref=target,
-            send_sem=core_send.at[sem],
-            recv_sem=core_recv.at[sem],
-            device_id=partner,
-            device_id_type=MESH,
-        )
-
-    other = pl.ds(pl.multiple_of((1 - core) * half_width, 128), half_width)
-    sides = [
-        core_copy(normed_ref.at[:, other], normed_far, 0),
-        core_copy(turned_own, turned_far, 1),
-    ]
-    sides[0].start()
-    cosine, sine = cosine_ref[...], sine_ref[...]
-
-    def query_head(head, total):
-        upstream = turn_back(back_ref[head, 0:HEAD_DIM, :].astype(F32), cosine, sine)
-        back, terms = column_norm_back(query_ref[head], query_gain_ref[...], upstream)
-        rows = pl.ds(pl.multiple_of(head * HEAD_DIM, HEAD_DIM), HEAD_DIM)
-        turned_own[rows, :] = back.astype(BF16)
-        return total + terms
-
-    def key_head(pair, total):
-        upstream = jnp.zeros((2 * HEAD_DIM, back_ref.shape[2]), F32)
-        for member in range(group):
-            upstream += back_ref[group * pair + member, HEAD_DIM : 3 * HEAD_DIM, :].astype(F32)
-        back, terms = column_norm_back(
-            key_ref[pair],
-            key_gain_ref[...],
-            turn_back(upstream[:HEAD_DIM], cosine, sine),
-        )
-        base = heads * HEAD_DIM
-        rows = pl.ds(pl.multiple_of(base + pair * HEAD_DIM, HEAD_DIM), HEAD_DIM)
-        turned_own[rows, :] = back.astype(BF16)
-        base += pairs * HEAD_DIM
-        rows = pl.ds(pl.multiple_of(base + pair * HEAD_DIM, HEAD_DIM), HEAD_DIM)
-        turned_own[rows, :] = upstream[HEAD_DIM:].astype(BF16)
-        return total + terms
-
-    nothing = jnp.zeros((HEAD_DIM, back_ref.shape[2]), F32)
-    query_terms = lax.fori_loop(0, heads, query_head, nothing)
-    key_terms = lax.fori_loop(0, pairs, key_head, nothing)
-    sides[1].start()
-
-    def compute(chain, owner):
-        lanes = slice(chain * 256, chain * 256 + 256)
-        own_lanes = pl.ds(pl.multiple_of(core * half_width + chain * 256, 128), 256)
-        values, row, base = [], 0, 0
-        for size in (heads, pairs, pairs):
-            count = size * HEAD_DIM // RING
-            rows = pl.ds(pl.multiple_of(base + owner * count, 16), count)
-            value = jnp.dot(turned_own[rows, :], normed_ref[:, own_lanes], preferred_element_type=F32)
-            value += jnp.dot(turned_far[rows, :], normed_far[:, lanes], preferred_element_type=F32)
-            values.append((row, value))
-            row += count
-            base += size * HEAD_DIM
-        return values
-
-    def finish(chain, row, value):
-        grads_out[row : row + value.shape[0], chain * 256 : chain * 256 + 256] = value
-
-    chains = (
-        Spread(0, compute, sent_a, (came_a0, came_a1, came_a2), send_sems, recv_sems),
-        Spread(1, compute, sent_b, (came_b0, came_b1, came_b2), send_sems, recv_sems),
-    )
-    for copy in sides:
-        copy.wait_recv()
-
-    def one(index, carry):
-        for chain in chains:
-            chain.stage_one(1 - index // 4, lax.rem(index + 1, 4))
-        return carry
-
-    lax.fori_loop(0, 8, one, 0)
-
-    natural[...] = jnp.zeros(natural.shape, BF16)
-    for row in range(0, turned_own.shape[0], 128):
-        natural[:, row : row + 128] = turned_own[row : row + 128, :].astype(F32).T.astype(BF16)
-
-    def two(index, carry):
-        for chain in chains:
-            chain.stage_two(lax.rem(index + 1, 4))
-        return carry
-
-    lax.fori_loop(0, 4, two, 0)
-
-    cut = 2 * pairs * HEAD_DIM
-    upstream = dot_dims(natural[:, : heads * HEAD_DIM], weights_ref[:, cut:], 1, 1)
-    upstream += dot_dims(natural[:, heads * HEAD_DIM :], weights_ref[:, :cut], 1, 1)
-    summed[...] = upstream
-
-    def three(depth, carry):
-        for chain in chains:
-            chain.stage_three(depth)
-        return carry
-
-    lax.fori_loop(1, 4, three, 0)
-
-    def token_rows(index, total):
-        rows = pl.ds(pl.multiple_of(index * 32, 32), 32)
-        values, upstream = tokens_ref[rows, :].astype(F32), summed[rows, :]
-        inverse = lax.rsqrt(jnp.mean(values * values, axis=-1, keepdims=True) + EPSILON)
-        scaled = upstream * attn_gain_ref[...]
-        weight = jnp.sum(scaled * values, axis=-1, keepdims=True) / values.shape[1]
-        tokens_out[rows, :] = (
-            middle_ref[rows, :] + inverse * scaled - values * inverse**3 * weight
-        )
-        return total + jnp.sum(upstream * values * inverse, axis=0, keepdims=True)
-
-    terms = lax.fori_loop(
-        0, tokens_ref.shape[0] // 32, token_rows, jnp.zeros((1, tokens_ref.shape[1]), F32)
-    )
-    gain_own[0] = jnp.zeros(gain_own.shape[1:], F32)
-    gain_own[0, 0:1, :] = terms
-    gain_own[0, 1:2, :] = ffn_terms_ref[...]
-    gain_own[0, 2:3, 0:HEAD_DIM] = jnp.sum(query_terms.T, axis=0, keepdims=True)
-    gain_own[0, 3:4, 0:HEAD_DIM] = jnp.sum(key_terms.T, axis=0, keepdims=True)
-
-    def gain_copy(source, target, sem, peer):
-        return pltpu.make_async_remote_copy(
-            src_ref=source,
-            dst_ref=target,
-            send_sem=gain_send.at[sem],
-            recv_sem=gain_recv.at[sem],
-            device_id=peer,
-            device_id_type=MESH,
-        )
-
-    gain_copies = []
-    for stage, peer in enumerate((near_x, near_y, partner)):
-        copy = gain_copy(gain_own.at[stage], gain_came.at[stage], stage, peer)
-        copy.start()
-        gain_copies.append(copy)
-        copy.wait_recv()
-        gain_own[stage + 1] = gain_own[stage] + gain_came[stage]
-    gain_deep[z] = gain_own[3]
-    for step in range(1, 4):
-        copy = gain_copy(gain_own.at[3], gain_deep.at[z], 2 + step, deep[step - 1])
-        copy.start()
-        gain_copies.append(copy)
-
-    for chain in chains:
-        chain.close(finish)
-    for copy in gain_copies[3:]:
-        copy.wait_recv()
-    gains_out[...] = (gain_deep[0] + gain_deep[1]) + (gain_deep[2] + gain_deep[3])
-    for copy in sides + gain_copies:
-        copy.wait_send()
-    for chain in chains:
-        chain.drain()
-
-
-def tail_call(call_id, *inputs):
-    rows, width = inputs[8].shape
-    total = (HEADS + 2 * KV_HEADS) * HEAD_DIM
-    block_rows = total // RING
-    buffers = [
-        pltpu.VMEM((slots, block_rows, 256), BF16) for chain in range(2) for slots in (8, 8, 4, 3)
-    ]
-    return pl.pallas_call(
-        tail_kernel,
-        out_shape=(
-            jax.ShapeDtypeStruct((rows, width), F32),
-            jax.ShapeDtypeStruct((block_rows, width // 2), F32),
-            jax.ShapeDtypeStruct((4, width), F32),
-        ),
-        in_specs=[VMEM_SPEC] * len(inputs),
-        out_specs=(VMEM_SPEC,) * 3,
-        scratch_shapes=[
-            pltpu.VMEM((total, rows), BF16),
-            pltpu.VMEM((total, rows), BF16),
-            pltpu.VMEM((rows, width // 2), BF16),
-            pltpu.VMEM((rows, total), BF16),
-            pltpu.VMEM((rows, width), F32),
-            pltpu.VMEM((4, 4, width), F32),
-            pltpu.VMEM((3, 4, width), F32),
-            pltpu.VMEM((4, 4, width), F32),
-        ]
-        + buffers
-        + [
-            pltpu.SemaphoreType.DMA((2, 15)),
-            pltpu.SemaphoreType.DMA((2, 15)),
-            pltpu.SemaphoreType.DMA((2,)),
-            pltpu.SemaphoreType.DMA((2,)),
-            pltpu.SemaphoreType.DMA((6,)),
-            pltpu.SemaphoreType.DMA((6,)),
-        ],
-        compiler_params=pltpu.CompilerParams(
-            collective_id=call_id, has_side_effects=True, vmem_limit_bytes=60 << 20
-        ),
-        name="backward_tail",
-    )(*inputs)
+    )(*inputs, *loads)
 
 
 def angle_parts(positions):
@@ -1397,6 +1357,149 @@
     )(*inputs)
 
 
+def ffn_kernel(
+    tokens_ref,
+    mixed_ref,
+    w_out_ref,
+    gain_ref,
+    cot_ref,
+    gate_ref,
+    up_ref,
+    down_ref,
+    pair_out,
+    hidden_out,
+    output_out,
+    ffn_out,
+    side_out,
+    mixed_back_out,
+    grad_middle_out,
+    terms_out,
+    middle,
+    result,
+    upstream,
+    middle_low,
+):
+    step = pl.program_id(0)
+    rows, width = tokens_ref.shape
+    strip = 32
+
+    def strips(work):
+        def one(index, carry):
+            return work(pl.ds(pl.multiple_of(index * strip, strip), strip), carry)
+
+        return one
+
+    @pl.when(step == 0)
+    def _():
+        mixed = mixed_ref[...].astype(F32).T.astype(BF16)
+        middle[...] = tokens_ref[...].astype(F32) + jnp.dot(
+            mixed, w_out_ref[...], preferred_element_type=F32
+        )
+
+        def norm(window, carry):
+            values = middle[window, :]
+            inverse = lax.rsqrt(jnp.mean(values * values, axis=-1, keepdims=True) + EPSILON)
+            ffn_out[window, :] = (values * inverse * gain_ref[...]).astype(BF16)
+            result[window, :] = values
+            return carry
+
+        lax.fori_loop(0, rows // strip, strips(norm), 0)
+        upstream[...] = jnp.zeros(upstream.shape, F32)
+        side_out[0] = cot_ref[...].astype(F32).T.astype(BF16)
+
+    gate_pre = jnp.dot(ffn_out[...], gate_ref[...], preferred_element_type=F32)
+    up_pre = jnp.dot(ffn_out[...], up_ref[...], preferred_element_type=F32)
+    grad_hidden = dot_dims(cot_ref[...], down_ref[...], 1, 1)
+    gate_sig = jax.nn.sigmoid(gate_pre)
+    gate_act = gate_pre * gate_sig
+    hidden_out[...] = (gate_act * up_pre).astype(BF16)
+    gate_back = (grad_hidden * up_pre * (gate_sig * (1.0 + gate_pre * (1.0 - gate_sig)))).astype(
+        BF16
+    )
+    up_back = (grad_hidden * gate_act).astype(BF16)
+    result[...] += jnp.dot(hidden_out[...], down_ref[...], preferred_element_type=F32)
+    upstream[...] += dot_dims(gate_back, gate_ref[...], 1, 1) + dot_dims(
+        up_back, up_ref[...], 1, 1
+    )
+    wide = pair_out.shape[1] // 2
+    for base, back in ((0, gate_back), (wide, up_back)):
+        turned = back.astype(F32).T.astype(BF16)
+        for owner in range(pair_out.shape[0]):
+            pair_out[owner, base : base + wide, :] = turned[owner * wide : (owner + 1) * wide]
+
+    @pl.when(step == pl.num_programs(0) - 1)
+    def _():
+        output_out[...] = result[...].astype(BF16)
+
+        def back(window, total):
+            values, grads = middle[window, :], upstream[window, :]
+            inverse = lax.rsqrt(jnp.mean(values * values, axis=-1, keepdims=True) + EPSILON)
+            scaled = grads * gain_ref[...]
+            weight = jnp.sum(scaled * values, axis=-1, keepdims=True) / width
+            grad_middle = cot_ref[window, :].astype(F32) + (
+                inverse * scaled - values * inverse**3 * weight
+            )
+            grad_middle_out[window, :] = grad_middle
+            middle_low[window, :] = grad_middle.astype(BF16)
+            return total + jnp.sum(grads * values * inverse, axis=0, keepdims=True)
+
+        terms_out[...] = lax.fori_loop(
+            0, rows // strip, strips(back), jnp.zeros((1, width), F32)
+        )
+        mixed_back_out[...] = dot_dims(w_out_ref[...], middle_low[...], 1, 1).astype(BF16)
+        side_out[1] = middle_low[...].astype(F32).T.astype(BF16)
+
+
+def ffn_call(tokens, mixed_t, w_out, gain, cot, gate, up, down):
+    rows, width = tokens.shape
+    hidden_width = gate.shape[1]
+    steps = 4
+    chunk = hidden_width // steps
+    owners = RING // steps
+    wide = hidden_width // RING
+
+    def whole(*shape):
+        return pl.BlockSpec(shape, lambda i: (0,) * len(shape))
+
+    return pl.pallas_call(
+        ffn_kernel,
+        grid=(steps,),
+        out_shape=(
+            jax.ShapeDtypeStruct((RING, 2 * wide, rows), BF16),
+            jax.ShapeDtypeStruct((rows, hidden_width), BF16),
+            jax.ShapeDtypeStruct((rows, width), BF16),
+            jax.ShapeDtypeStruct((rows, width), BF16),
+            jax.ShapeDtypeStruct((2, width, rows), BF16),
+            jax.ShapeDtypeStruct((width, rows), BF16),
+            jax.ShapeDtypeStruct((rows, width), F32),
+            jax.ShapeDtypeStruct((1, width), F32),
+        ),
+        in_specs=[
+            whole(rows, width),
+            whole(width, rows),
+            whole(width, width),
+            whole(1, width),
+            whole(rows, width),
+            pl.BlockSpec((width, chunk), lambda i: (0, i)),
+            pl.BlockSpec((width, chunk), lambda i: (0, i)),
+            pl.BlockSpec((chunk, width), lambda i: (i, 0)),
+        ],
+        out_specs=(
+            pl.BlockSpec((owners, 2 * wide, rows), lambda i: (i, 0, 0)),
+            pl.BlockSpec((rows, chunk), lambda i: (0, i)),
+            whole(rows, width),
+            whole(rows, width),
+            whole(2, width, rows),
+            whole(width, rows),
+            whole(rows, width),
+            whole(1, width),
+        ),
+        scratch_shapes=[pltpu.VMEM((rows, width), F32)] * 3 + [pltpu.VMEM((rows, width), BF16)],
+        compiler_params=pltpu.CompilerParams(vmem_limit_bytes=56 << 20),
+        name="ffn_both_ways",
+    )(tokens, mixed_t, w_out, gain, cot, gate, up, down)
+
+
 def both(block, axis):
     return lax.all_gather(block, "fsdp", axis=axis, tiled=True)
 
@@ -1420,7 +1523,6 @@
 ):
     place, core = lax.axis_index("ctx"), lax.axis_index("fsdp")
     rows, width = tokens.shape[1], tokens.shape[2]
-    resid_in = tokens[0].astype(F32)
     pos_local = doc_pos[0]
     o_full, gate_full = both(w_out, 0), both(w_gate, 0)
     up_full, down_full = both(w_up, 0), both(w_down, 0)
@@ -1445,61 +1547,44 @@
     mixed_far, inverse_total = attend(first, clear, qkv, starts)
     mixed_t = exchange(mixed_far, 2).reshape(HEADS * HEAD_DIM, rows)
 
-    middle = resid_in + dot_dims(mixed_t, o_full, 0, 0)
-    ffn_low = rms_norm(middle, ffn_gain).astype(BF16)
-    gate_pre = jnp.dot(ffn_low, gate_full, preferred_element_type=F32)
-    up_pre = jnp.dot(ffn_low, up_full, preferred_element_type=F32)
-    gate_sig = jax.nn.sigmoid(gate_pre)
-    gate_act = gate_pre * gate_sig
-    hidden_low = (gate_act * up_pre).astype(BF16)
-    result = middle + jnp.dot(hidden_low, down_full, preferred_element_type=F32)
-    output = result.astype(BF16)[None]
     cot_low = d_output[0]
-    cotangent = cot_low.astype(F32)
-    grad_hidden = against(cot_low, down_full)
-    gate_back = (grad_hidden * up_pre * (gate_sig * (1.0 + gate_pre * (1.0 - gate_sig)))).astype(
-        BF16
-    )
-    up_back = (grad_hidden * gate_act).astype(BF16)
-    grad_ffn_in = against(gate_back, gate_full) + against(up_back, up_full)
-    middle_part, ffn_terms = rms_back(middle, ffn_gain, grad_ffn_in)
-    grad_middle = cotangent + middle_part
-    middle_low = grad_middle.astype(BF16)
-    grad_mixed = dot_dims(o_full, middle_low, 1, 1).astype(BF16)
-
-    gate_t, up_t, down_t, out_t, back_home = back_call(
+    (
+        pair,
+        hidden_low,
+        output,
+        ffn_low,
+        side,
+        grad_mixed,
+        grad_middle,
+        ffn_terms,
+    ) = ffn_call(
+        tokens[0], mixed_t, o_full, ffn_gain[None, :], cot_low, gate_full, up_full, down_full
+    )
+    gate_t, up_t, down_t, out_t, qkv_grads, d_tokens, gain_totals = back_call(
         3,
-        gate_back,
-        up_back,
-        hidden_low,
-        cot_low,
-        middle_low,
-        ffn_low,
-        mixed_t,
-        grad_mixed.reshape(HEADS, HEAD_DIM, rows),
-        qkv,
-        starts,
-        mixed_far,
-        inverse_total,
-    )
-    d_tokens, qkv_grads, gain_totals = tail_call(
-        4,
-        back_home,
-        query_raw,
-        key_raw,
-        cosine,
-        sine,
-        query_gain[:, None],
-        key_gain[:, None],
-        kvq_full,
-        normed_low,
-        tokens[0],
-        attn_gain[None, :],
-        grad_middle,
-        jnp.sum(ffn_terms, axis=0, keepdims=True),
+        (
+            pair,
+            hidden_low,
+            side,
+            ffn_low,
+            mixed_t,
+            grad_mixed.reshape(HEADS, HEAD_DIM, rows),
+            qkv,
+            starts,
+            mixed_far,
+            inverse_total,
+            cosine,
+            sine,
+            query_gain[:, None],
+            key_gain[:, None],
+            normed_low,
+            attn_gain[None, :],
+            ffn_terms,
+        ),
+        (tokens[0], query_raw, key_raw, kvq_full, grad_middle),
     )
     return (
-        output,
+        output[None],
         d_tokens[None],
         gain_totals[0],
         qkv_grads[:64].T,

time: 409 us -> 356 us (0.87)
  matrix products: 49.3 us -> 0 us
    dot_general x8 -> x0, matrix products: 49.3 us -> none  [the longest x3 22.5 us: against(): lax.dot_general(left_mat, right_mat, (((1,), (1,)), ((), ())), preferred_...]
    pallas_call x1, Pallas kernels: 52.3 us -> 29.1 us  [ffn_call(): pl.pallas_call(ffn_kernel, grid=(steps,), out_shape=(jax.ShapeDtypeStruct...]
    pallas_call x1, Pallas kernels: 173 us -> 192 us  [back_call(): pl.pallas_call(back_kernel, out_shape=(jax.ShapeDtypeStruct((wide, width...]
    unnamed x69 -> x39, local copies, waits for them, and re-layouts: 7.57 us -> 11.2 us
  transfers between devices with their start and end apart: 4 -> 4, of which waited for: 0 -> 0; matrix products, arithmetic and copies ran while one was open for 5% -> 0% of each run, Pallas kernels for 24% -> 27%
where the time goes in v4:
time: 356 us; the launch traced here: 352 us
  Pallas kernels  317 us (89%)
  local copies, waits for them, and re-layouts  17.1 us (5%)
  between operations  14.1 us (4%)
    pallas_call x1, Pallas kernels, back_call(): pl.pallas_call(back_kernel, out_shape=(jax.ShapeDtypeStruct((wide, width...  192 us
    pallas_call x1, Pallas kernels, front_call(): pl.pallas_call(front_kernel, out_shape=(jax.ShapeDtypeStruct((RING, 3 * H...  50.2 us
    pallas_call x1, Pallas kernels, ffn_call(): pl.pallas_call(ffn_kernel, grid=(steps,), out_shape=(jax.ShapeDtypeStruct...  29.1 us
    pallas_call x1, Pallas kernels, attend(): pl.pallas_call(attend_kernel, out_shape=(jax.ShapeDtypeStruct((blocks, HE...  28.4 us
    pallas_call x1, Pallas kernels, exchange(): pl.pallas_call(exchange_kernel, out_shape=jax.ShapeDtypeStruct(blocks.sha...  17.3 us
    unnamed x39, local copies, waits for them, and re-layouts  11.2 us
  transfers between devices with their start and end apart: 4, of which 0 were waited for; matrix products, arithmetic and copies ran while one was open for 0% of the time, Pallas kernels for 27%

profile of v4, /device:TPU:15, one launch (start us, length us, event | category | flops | bytes accessed | tf_op | source)
XLA Modules:
  0.0 352.2 jit_solution(17898634495527273813)
XLA Ops:
  7.2 0.0 all-gather.5.cloned.1.call-start
  7.2 0.7 all-gather.5.cloned.1.call-update
  7.9 0.0 all-gather.7.cloned.1.call-start
  8.0 0.7 all-gather.7.cloned.1.call-update
  8.7 0.0 all-gather.9.cloned.1.call-start
  8.8 0.7 all-gather.9.cloned.1.call-update
  9.5 0.0 all-gather.11.cloned.1.call-start
  9.5 0.5 all-gather.11.cloned.1.call-update
  10.1 0.1 copy.31.query_gain_ref
  10.2 0.1 copy.32.key_gain_ref
  10.3 0.2 multiply_sine_fusion
  10.6 50.2 %front_heads.1 = (bf16[16,192,256]{2,1,0:T(8,128)(2,1)}, s32[16,1,256]{2,1,0:T(1,128)S(1)}, f32[16,64,256]{2,1,0:T(8,128)S(1)}, f32[8,64,256]{2,1,0:T(8,128)S(1)...) custom-call(bf16[256,1024]{1,0:T(8,128)(2,1)S(1)} %bitcast.29, f32[1,1024]{1,0:T(1,128)S(1)} %bitcast.31, ...), custom_call_target="tpu_custom_call" | custom-call | tf_op jit(solution)/shard_map/front_heads/pallas_call | solution.py:1331
  60.8 1.0 copy-done.1
  61.8 0.8 copy-done.5
  62.6 0.8 copy-done.6
  63.4 0.7 add_reduce_fusion
  64.1 0.5 and_select_fusion.1
  64.7 28.4 %attend_forward.1 = (bf16[16,64,256]{2,1,0:T(8,128)(2,1)}, f32[16,1,256]{2,1,0:T(1,128)}) custom-call(s32[16]{0:T(128)} %get-tuple-element.71.first_ref, s32[16]{0:T(128)} %get-tuple-element.72.clear_ref, bf16[16,192,256]{2,1,0:T(8,128)(2,1)} %get-tuple-element.37.qkv_ref, s32[16,1,256]{2,1,0:T(1,128)} %copy-done.11), custom_call_target="tpu_custom_call" | custom-call | tf_op jit(solution)/shard_map/attend_forward/pallas_call | solution.py:438
  93.1 17.3 %exchange_heads.1 = bf16[16,64,256]{2,1,0:T(8,128)(2,1)} custom-call(bf16[16,64,256]{2,1,0:T(8,128)(2,1)} %get-tuple-element.38.src.part_ref), custom_call_target="tpu_custom_call" | custom-call | tf_op jit(solution)/shard_map/exchange_heads/pallas_call | solution.py:364
  110.3 0.0 all-gather.5.cloned.1.call-done.w_out_ref
  110.4 0.0 all-gather.7.cloned.1.call-done.gate_ref
  110.4 29.1 %ffn_both_ways.1 = (bf16[16,576,256]{2,1,0:T(8,128)(2,1)}, bf16[256,4608]{1,0:T(8,128)(2,1)}, bf16[256,1024]{1,0:T(8,128)(2,1)}, bf16[256,1024]{1,0:T(8,128)(2,1...) custom-call(bf16[256,1024]{1,0:T(8,128)(2,1)} %bitcast.27, ...), custom_call_target="tpu_custom_call" | custom-call | tf_op jit(solution)/shard_map/ffn_both_ways/pallas_call | solution.py:1464
  139.6 191.7 %backward_spread.1 = (f32[288,512]{1,0:T(8,128)}, f32[288,512]{1,0:T(8,128)}, f32[64,2304]{1,0:T(8,128)}, f32[64,512]{1,0:T(8,128)}, f32[128,512]{1,0:T(8,128)}, /*index=5*/f32[256,1024]{1,0:T(8,128)}, f32[4,1024]{1,0:T(4,128)}) custom-call(bf16[16,576,256]{2,1,0:T(8,128)(2,1)} %get-tuple-element.40.pair_own, ...), custom_call_target="tpu_custom_call" | custom-call | tf_op jit(solution)/shard_map/backward_spread/pallas_call | solution.py:1114
  331.3 1.3 slice_bitcast_fusion.3
  332.6 1.4 fusion
  334.0 1.6 slice_bitcast_fusion
  335.6 1.5 slice_bitcast_fusion.1
  337.1 2.3 copy.40
  339.4 1.6 copy.41
  341.0 1.9 copy.42
  342.9 1.9 copy.43
  344.8 0.8 copy.44
  (35 shorter events, 0.1 us)
Async XLA Ops:
  7.2 103.2 %all-gather.5.cloned.1.call-start = ((), (), s32[]{:S(2)}) async-start(), calls=%async_computation | async-start | bytes 3145728 | tf_op jit(solution)/shard_map/all_gather | solution.py:1504
  7.9 102.5 %all-gather.7.cloned.1.call-start = ((), (), s32[]{:S(2)}) async-start(), calls=%async_computation.1 | async-start | bytes 14155776 | tf_op jit(solution)/shard_map/all_gather | solution.py:1504
  8.7 1.4 copy-start.15
  8.7 1.5 copy-start.16
  8.7 1.6 copy-start.14
  8.7 1.8 copy-start
  8.7 1.8 copy-start.2
  8.7 1.8 copy-start.3
  8.7 1.8 copy-start.4
  8.7 1.8 copy-start.12
  8.7 101.7 %all-gather.9.cloned.1.call-start = ((), (), s32[]{:S(2)}) async-start(), calls=%async_computation.2 | async-start | bytes 14155776 | tf_op jit(solution)/shard_map/all_gather | solution.py:1504
  9.5 100.9 %all-gather.11.cloned.1.call-start = ((), (), s32[]{:S(2)}) async-start(), calls=%async_computation.3 | async-start | bytes 14155776 | tf_op jit(solution)/shard_map/all_gather | solution.py:1504
  10.2 129.4 %copy-start.7 = (f32[64,1]{1,0:T(8,128)}, f32[64,1]{1,0:T(8,128)S(1)}, u32[]{:S(2)}) copy-start(f32[64,1]{1,0:T(8,128)S(1)} %copy.31.query_gain_ref) | copy-start | bytes 772
  10.3 129.3 %copy-start.8 = (f32[64,1]{1,0:T(8,128)}, f32[64,1]{1,0:T(8,128)S(1)}, u32[]{:S(2)}) copy-start(f32[64,1]{1,0:T(8,128)S(1)} %copy.32.key_gain_ref) | copy-start | bytes 772
  10.5 129.1 %copy-start.9 = (f32[32,256]{1,0:T(8,128)}, f32[32,256]{1,0:T(8,128)S(1)}, u32[]{:S(2)}) copy-start(f32[32,256]{1,0:T(8,128)S(1)} %get-tuple-element.67.sine_ref) | copy-start | bytes 98308
  10.5 129.1 %copy-start.10 = (f32[32,256]{1,0:T(8,128)}, f32[32,256]{1,0:T(8,128)S(1)}, u32[]{:S(2)}) copy-start(f32[32,256]{1,0:T(8,128)S(1)} %get-tuple-element.68.cosine_ref) | copy-start | bytes 98308
  60.8 1.0 copy-start.1
  61.8 0.8 copy-start.5
  62.6 0.8 copy-start.6
  63.4 1.3 copy-start.11
  331.3 13.5 %copy-start.13 = (f32[64,2304]{1,0:T(8,128)S(1)}, f32[64,2304]{1,0:T(8,128)}, u32[]{:S(2)}) copy-start(f32[64,2304]{1,0:T(8,128)} %get-tuple-element.58) | copy-start | bytes 1769476
Sparse Core Ops, SparseCore 0:
  9.6 12.3 all-gather.4
  23.5 23.0 all-gather.6
  48.2 23.0 all-gather.8
  72.7 23.2 all-gather.10

commit v5 on v4

--- a/solution.py
+++ b/solution.py
@@ -320,6 +320,7 @@
 MESH = pl.DeviceIdType.MESH
 BLOCK = 256
 RING = 16
+HALF = 8
 VMEM_SPEC = pl.BlockSpec(memory_space=pltpu.VMEM)
 HBM_SPEC = pl.BlockSpec(memory_space=pltpu.HBM)
 SMEM_SPEC = pl.BlockSpec(memory_space=pltpu.SMEM)
@@ -333,119 +334,8 @@
     )
 
 
-def exchange_kernel(src, dst, own_sem, send_sem, recv_sem):
-    place, core = lax.axis_index("ctx"), lax.axis_index("fsdp")
-    barrier = pltpu.get_barrier_semaphore()
-    for step in range(1, RING):
-        peer = lax.rem(place + step, RING)
-        pl.semaphore_signal(barrier, inc=1, device_id=(peer, core), device_id_type=MESH)
-    own = pltpu.make_async_copy(src.at[place], dst.at[place], own_sem)
-    own.start()
-    pl.semaphore_wait(barrier, RING - 1)
-    copies = []
-    for step in range(1, RING):
-        peer = lax.rem(place + step, RING)
-        copy = pltpu.make_async_remote_copy(
-            src_ref=src.at[peer],
-            dst_ref=dst.at[place],
-            send_sem=send_sem.at[step],
-            recv_sem=recv_sem.at[step],
-            device_id=(peer, core),
-            device_id_type=MESH,
-        )
-        copy.start()
-        copies.append(copy)
-    own.wait()
-    for copy in copies:
-        copy.wait()
-
-
-def exchange(blocks, call_id):
-    return pl.pallas_call(
-        exchange_kernel,
-        out_shape=jax.ShapeDtypeStruct(blocks.shape, blocks.dtype),
-        in_specs=[VMEM_SPEC],
-        out_specs=VMEM_SPEC,
-        scratch_shapes=[
-            pltpu.SemaphoreType.DMA,
-            pltpu.SemaphoreType.DMA((RING,)),
-            pltpu.SemaphoreType.DMA((RING,)),
-        ],
-        compiler_params=pltpu.CompilerParams(collective_id=call_id, has_side_effects=True),
-        name="exchange_heads",
-    )(blocks)
-
-
 def transposed(block):
     return block.astype(F32).T.astype(BF16)
-
-
-def block_probs(key_nat, query_t, first_key, start, query_place, diagonal, masked):
-    scores = jnp.dot(key_nat, query_t, preferred_element_type=F32)
-    probs = jnp.exp(scores)
-    if masked:
-        key_place = first_key + lax.broadcasted_iota(jnp.int32, probs.shape, 0)
-        ok = key_place >= start
-        if diagonal:
-            ok = ok & (key_place <= query_place)
-        probs = jnp.where(ok, probs, 0.0)
-    return probs
-
-
-def attend_kernel(first_ref, clear_ref, qkv_ref, start_ref, mixed_ref, inv_ref, key_nat):
-    blocks = qkv_ref.shape[0]
-
-    def turn(j, carry):
-        key_nat[j] = transposed(qkv_ref[j, HEAD_DIM : 2 * HEAD_DIM, :])
-        return carry
-
-    lax.fori_loop(0, blocks, turn, 0)
-
-    def per_query(i, nothing):
-        query_t = qkv_ref[i, 0:HEAD_DIM, :] * jnp.asarray(HEAD_DIM**-0.5, BF16)
-        start = start_ref[i]
-        query_place = i * BLOCK + lax.broadcasted_iota(jnp.int32, (1, BLOCK), 1)
-
-        def step(diagonal, masked, j, carry):
-            total, acc = carry
-            probs = block_probs(
-                key_nat[j], query_t, j * BLOCK, start, query_place, diagonal, masked
-            )
-            total = total + jnp.sum(probs, axis=0, keepdims=True)
-            acc = acc + jnp.dot(
-                qkv_ref[j, 2 * HEAD_DIM : 3 * HEAD_DIM, :],
-                probs.astype(BF16),
-                preferred_element_type=F32,
-            )
-            return total, acc
-
-        carry = (jnp.zeros((1, BLOCK), F32), jnp.zeros((HEAD_DIM, BLOCK), F32))
-        carry = lax.fori_loop(
-            first_ref[i], clear_ref[i], functools.partial(step, False, True), carry
-        )
-        carry = lax.fori_loop(clear_ref[i], i, functools.partial(step, False, False), carry)
-        total, acc = step(True, True, i, carry)
-        inverse = 1.0 / total
-        mixed_ref[i] = (acc * inverse).astype(BF16)
-        inv_ref[i] = inverse
-        return nothing
-
-    lax.fori_loop(0, blocks, per_query, 0)
-
-
-def attend(first, clear, qkv, start):
-    blocks = qkv.shape[0]
-    return pl.pallas_call(
-        attend_kernel,
-        out_shape=(
-            jax.ShapeDtypeStruct((blocks, HEAD_DIM, BLOCK), BF16),
-            jax.ShapeDtypeStruct((blocks, 1, BLOCK), F32),
-        ),
-        in_specs=[SMEM_SPEC, SMEM_SPEC, VMEM_SPEC, VMEM_SPEC],
-        out_specs=(VMEM_SPEC, VMEM_SPEC),
-        scratch_shapes=[pltpu.VMEM((blocks, BLOCK, HEAD_DIM), BF16)],
-        name="attend_forward",
-    )(first, clear, qkv, start)
 
 
 def flip(bit, turned):
@@ -528,11 +418,9 @@
                 value = value + self.came[2][depth, window, :].astype(F32)
             finish(self.chain, row, value)
 
-    def drain_first(self):
+    def drain(self):
         for slot in range(8):
             self.copy(0, slot).wait_send()
-
-    def drain_last(self):
         for depth in range(4):
             self.copy(1, depth).wait_send()
         for depth in range(1, 4):
@@ -572,10 +460,7 @@
     start_ref,
     part_ref,
     inv_ref,
-    cosine_ref,
-    sine_ref,
-    query_gain_ref,
-    key_gain_ref,
+    table_ref,
     normed_ref,
     attn_gain_ref,
     ffn_terms_ref,
@@ -601,11 +486,13 @@
     cot_far,
     back_own,
     back_far,
+    extra_own,
+    extra_far,
     turned_own,
     turned_far,
     gain_own,
     gain_came,
-    gain_deep,
+    gain_all,
     sent_a,
     came_a0,
     came_a1,
@@ -634,18 +521,19 @@
     core_recv,
     gain_send,
     gain_recv,
+    extra_send,
+    extra_recv,
     load_sem,
-    weight_sem,
 ):
     place, core = lax.axis_index("ctx"), lax.axis_index("fsdp")
+    part, member = place // HALF, lax.rem(place, HALF)
+    base = part * HALF - 1
     x, y, z = lax.rem(place, 2), lax.rem(place // 2, 2), place // 4
-    blocks = qkv_ref.shape[0]
     wide = pair_own.shape[1] // 2
     narrow = side_own.shape[1] // RING
     half_hidden = hidden_far.shape[1]
     half_width = ffn_far.shape[1]
     heads, pairs = query_hbm.shape[0], key_hbm.shape[0]
-    group = heads // pairs
     scale = HEAD_DIM**-0.5
     partner = (place, 1 - core)
 
@@ -670,9 +558,16 @@
             device_id_type=MESH,
         )
 
-    def cot_copy(step, peer):
+    def mate(step):
+        return (part * HALF + lax.rem(member + step, HALF), core)
+
+    def cot_copy(step):
         return remote(
-            home_ref.at[peer], cot_far.at[place], cot_send.at[step], cot_recv.at[step], (peer, core)
+            home_ref.at[lax.rem(member + step, HALF)],
+            cot_far.at[member],
+            cot_send.at[step],
+            cot_recv.at[step],
+            mate(step),
         )
 
     def core_copy(source, target, sem):
@@ -697,13 +592,13 @@
     for copy in sides:
         copy.start()
     pair_copy(*order[0]).start()
-    for step in range(1, RING):
-        cot_copy(step, lax.rem(place + step, RING)).start()
+    for step in range(1, HALF):
+        cot_copy(step).start()
     for turn_x, turn_y, depth in order[1:]:
         pair_copy(turn_x, turn_y, depth).start()
     normed_copy = core_copy(normed_ref.at[:, half(1 - core, half_width)], normed_far, 4)
     normed_copy.start()
-    cot_far[place] = home_ref[place]
+    cot_far[member] = home_ref[member]
 
     def compute(chain, owner):
         lanes = pl.ds(chain * 256, 256)
@@ -770,102 +665,128 @@
     far(2)
     near(1)
 
-    def back_copy(step, peer):
+    def back_copy(step):
         return remote(
-            back_own.at[peer],
-            back_far.at[place],
+            back_own.at[lax.rem(member + step, HALF)],
+            back_far.at[member],
             back_send.at[step],
             back_recv.at[step],
-            (peer, core),
-        )
-
-    def attention(scaled, natural, delta_ref, query_acc, key_nat, value_nat, pair_acc):
-        def prepare(i):
-            @pl.when(i != place)
+            mate(step),
+        )
+
+    def extra_copy(group):
+        return remote(
+            extra_own,
+            extra_far.at[group],
+            extra_send.at[group],
+            extra_recv.at[group],
+            (HALF - 1, core),
+        )
+
+    def attention(
+        scaled, cots, natural, delta_ref, query_acc, key_nat, value_nat, pair_acc
+    ):
+        def widen(ref, i, row):
+            return jnp.concatenate(
+                [ref[i, row : row + HEAD_DIM, :], ref[i, row + HEAD_DIM : row + 2 * HEAD_DIM, :]],
+                axis=1,
+            )
+
+        def prepare(i, nothing):
+            @pl.when(i != member)
             def _():
-                step = lax.rem(place - i + RING, RING)
-                cot_copy(step, lax.rem(place + step, RING)).wait_recv()
-
-            query = qkv_ref[i, 0:HEAD_DIM, :] * jnp.asarray(scale, BF16)
-            cot = cot_far[i]
+                cot_copy(lax.rem(member - i + HALF, HALF)).wait_recv()
+
+            query = widen(qkv_ref, i + 1, 0) * jnp.asarray(scale, BF16)
+            cot = widen(cot_far, i, 0)
             scaled[i] = query
+            cots[i] = cot
             natural[i] = transposed(jnp.concatenate([query, cot], axis=0))
             delta_ref[i] = jnp.sum(
-                cot.astype(F32) * part_ref[i].astype(F32), axis=0, keepdims=True
+                cot.astype(F32) * widen(part_ref, i, 0).astype(F32), axis=0, keepdims=True
             )
             query_acc[i] = jnp.zeros(query_acc.shape[1:], F32)
-
-        def prepare_one(i, nothing):
-            prepare(i)
             return nothing
 
         def per_key(j, nothing):
-            @pl.when(j + 8 < blocks)
-            def _():
-                prepare(j + 8)
-
-            key_nat[...] = transposed(qkv_ref[j, HEAD_DIM : 2 * HEAD_DIM, :])
-            value_nat[...] = transposed(qkv_ref[j, 2 * HEAD_DIM : 3 * HEAD_DIM, :])
-            key_place = j * BLOCK + lax.broadcasted_iota(jnp.int32, (BLOCK, BLOCK), 0)
+            key_t = qkv_ref[j, 2 * HEAD_DIM : 3 * HEAD_DIM, :]
+            key_nat[...] = transposed(key_t)
+            value_nat[...] = transposed(qkv_ref[j, 3 * HEAD_DIM : 4 * HEAD_DIM, :])
+            shape = (BLOCK, 2 * BLOCK)
+            key_place = (base + j) * BLOCK + lax.broadcasted_iota(jnp.int32, shape, 0)
 
             def step(diagonal, i):
-                inside = jnp.minimum(i, blocks - 1)
-                start = start_ref[inside] + (i // blocks) * (blocks * BLOCK)
-                scores = jnp.dot(key_nat[...], scaled[inside], preferred_element_type=F32)
-                grad_probs = jnp.dot(value_nat[...], cot_far[inside], preferred_element_type=F32)
+                start = jnp.concatenate([start_ref[i - 1]] * 2, axis=1)
+                scores = jnp.dot(key_nat[...], scaled[i - 1], preferred_element_type=F32)
+                grad_probs = jnp.dot(value_nat[...], cots[i - 1], preferred_element_type=F32)
                 ok = key_place >= start
                 if diagonal:
-                    query_place = i * BLOCK + lax.broadcasted_iota(jnp.int32, (1, BLOCK), 1)
-                    ok = ok & (key_place <= query_place)
-                probs = jnp.where(ok, jnp.exp(scores) * inv_ref[inside], 0.0)
-                grad_scores = (probs * (grad_probs - delta_ref[inside])).astype(BF16)
+                    places = (base + i) * BLOCK + lax.broadcasted_iota(jnp.int32, (1, BLOCK), 1)
+                    ok = ok & (key_place <= jnp.concatenate([places] * 2, axis=1))
+                probs = jnp.where(ok, jnp.exp(scores) * inv_ref[i - 1], 0.0)
+                grad_scores = (probs * (grad_probs - delta_ref[i - 1])).astype(BF16)
                 both_low = jnp.concatenate([grad_scores, probs.astype(BF16)], axis=0)
-                query_acc[i] += jnp.dot(
-                    qkv_ref[j, HEAD_DIM : 2 * HEAD_DIM, :],
+                query_acc[i - 1] += jnp.dot(
+                    qkv_ref[j, 2 * HEAD_DIM : 3 * HEAD_DIM, :],
                     grad_scores,
                     preferred_element_type=F32,
                 )
-                return jnp.dot(both_low, natural[inside], preferred_element_type=F32)
-
-            pair_acc[...] = step(True, j)
-            count = (jnp.minimum(8, blocks - 1 - j) + 1) // 2
-
-            def two(index, carry):
-                i = j + 1 + 2 * index
-                pair_acc[...] += step(False, i) + step(False, i + 1)
+                return jnp.dot(both_low, natural[i - 1], preferred_element_type=F32)
+
+            @pl.when(j == 0)
+            def _():
+                pair_acc[...] = jnp.zeros(pair_acc.shape, F32)
+
+            @pl.when(j > 0)
+            def _():
+                pair_acc[...] = step(True, j)
+
+            def one(i, carry):
+                pair_acc[...] += step(False, i)
                 return carry
 
-            lax.fori_loop(0, count, two, 0)
-            back_own[j, 0:HEAD_DIM, :] = (query_acc[j] * scale).astype(BF16)
+            lax.fori_loop(j + 1, HALF + 1, one, 0)
             first = lax.broadcasted_iota(jnp.int32, (BLOCK, 2 * HEAD_DIM), 1) < HEAD_DIM
-            merged = jnp.where(first, pair_acc[0:BLOCK, :], pair_acc[BLOCK:, :])
-            back_own[j, HEAD_DIM : 3 * HEAD_DIM, :] = merged.T.astype(BF16)
-
-            @pl.when(j != place)
+            merged = jnp.where(first, pair_acc[0:BLOCK, :], pair_acc[BLOCK:, :]).T.astype(BF16)
+
+            @pl.when(j == 0)
             def _():
-                back_copy(lax.rem(j - place + RING, RING), j).start()
+                extra_own[...] = merged
+                extra_copy(member).start()
+
+            @pl.when(j > 0)
+            def _():
+                query_grad = (query_acc[j - 1] * scale).astype(BF16)
+                back_own[j - 1, 0:HEAD_DIM, :] = query_grad[:, :BLOCK]
+                back_own[j - 1, HEAD_DIM : 2 * HEAD_DIM, :] = query_grad[:, BLOCK:]
+                back_own[j - 1, 2 * HEAD_DIM : 4 * HEAD_DIM, :] = merged
+
+            @pl.when((j > 0) & (j - 1 != member))
+            def _():
+                back_copy(lax.rem(j - 1 - member + HALF, HALF)).start()
 
             @pl.when(j == 4)
             def _():
                 onward(2)
                 far(1)
 
-            @pl.when(j == 9)
+            @pl.when(j == HALF)
             def _():
                 near(3)
 
             return nothing
 
-        lax.fori_loop(0, 8, prepare_one, 0)
-        lax.fori_loop(0, blocks, per_key, 0)
-        back_far[place] = back_own[place]
+        lax.fori_loop(0, HALF, prepare, 0)
+        lax.fori_loop(1 - part, HALF + 1, per_key, 0)
+        back_far[member] = back_own[member]
 
     pl.run_scoped(
         attention,
-        pltpu.VMEM((blocks, HEAD_DIM, BLOCK), BF16),
-        pltpu.VMEM((blocks, BLOCK, 2 * HEAD_DIM), BF16),
-        pltpu.VMEM((blocks, 1, BLOCK), F32),
-        pltpu.VMEM((blocks + 1, HEAD_DIM, BLOCK), F32),
+        pltpu.VMEM((HALF, HEAD_DIM, 2 * BLOCK), BF16),
+        pltpu.VMEM((HALF, HEAD_DIM, 2 * BLOCK), BF16),
+        pltpu.VMEM((HALF, 2 * BLOCK, 2 * HEAD_DIM), BF16),
+        pltpu.VMEM((HALF, 1, 2 * BLOCK), F32),
+        pltpu.VMEM((HALF, HEAD_DIM, 2 * BLOCK), F32),
         pltpu.VMEM((BLOCK, HEAD_DIM), BF16),
         pltpu.VMEM((BLOCK, HEAD_DIM), BF16),
         pltpu.VMEM((2 * BLOCK, 2 * HEAD_DIM), F32),
@@ -910,70 +831,74 @@
         ),
     )
 
-    near_x = (place + 1 - 2 * x, core)
-    near_y = (place + 2 - 4 * y, core)
-
-    def finish_all(natural, summed, query_ref, key_ref, tokens_ref):
+    def finish_all(natural, summed, query_ref, key_ref, tokens_ref, weights_ref):
         loads = [
             pltpu.make_async_copy(query_hbm, query_ref, load_sem.at[2]),
             pltpu.make_async_copy(key_hbm, key_ref, load_sem.at[3]),
             pltpu.make_async_copy(tokens_hbm, tokens_ref, load_sem.at[4]),
+            pltpu.make_async_copy(weights_hbm, weights_ref, load_sem.at[5]),
         ]
         for copy in loads:
             copy.start()
-        cosine, sine = cosine_ref[...], sine_ref[...]
+        half_dim = HEAD_DIM // 2
+        cosine, sine = table_ref[0:half_dim, :], table_ref[half_dim:HEAD_DIM, :]
+        query_gain = table_ref[HEAD_DIM : 2 * HEAD_DIM, :]
+        key_gain = table_ref[2 * HEAD_DIM : 3 * HEAD_DIM, :]
 
         def head_rows(index):
             return pl.ds(pl.multiple_of(index * HEAD_DIM, HEAD_DIM), HEAD_DIM)
 
         def query_head(head, total):
-            upstream = turn_back(back_far[head, 0:HEAD_DIM, :].astype(F32), cosine, sine)
-            back, terms = column_norm_back(query_ref[head], query_gain_ref[...], upstream)
+            low = pl.multiple_of(lax.rem(head, 2) * HEAD_DIM, HEAD_DIM)
+            upstream = turn_back(
+                back_far[head // 2, pl.ds(low, HEAD_DIM), :].astype(F32), cosine, sine
+            )
+            back, terms = column_norm_back(query_ref[head], query_gain, upstream)
             turned_own[head_rows(2 * pairs + head), :] = back.astype(BF16)
             return total + terms
 
         def key_head(pair, total):
-            upstream = jnp.zeros((2 * HEAD_DIM, BLOCK), F32)
-            for member in range(group):
-                upstream += back_far[group * pair + member, HEAD_DIM : 3 * HEAD_DIM, :].astype(F32)
+            upstream = back_far[pair, 2 * HEAD_DIM : 4 * HEAD_DIM, :].astype(F32)
+            upstream += extra_far[pair].astype(F32)
             back, terms = column_norm_back(
                 key_ref[pair],
-                key_gain_ref[...],
+                key_gain,
                 turn_back(upstream[:HEAD_DIM], cosine, sine),
             )
             turned_own[head_rows(pair), :] = back.astype(BF16)
             turned_own[head_rows(pairs + pair), :] = upstream[HEAD_DIM:].astype(BF16)
             return total + terms
 
-        def weight_load(part, column):
-            slot = (sent_a, sent_b)[part]
-            return pltpu.make_async_copy(
-                weights_hbm.at[pl.ds(part * 512, 512), pl.ds(pl.multiple_of(column * 256, 256), 256)],
-                slot.at[column, pl.ds(0, 512), :],
-                weight_sem.at[part, column],
-            )
-
         onward(1)
-        deeper(2)
         far(3)
-        near(0)
 
         def arrive(step, nothing):
-            back_copy(step, lax.rem(place + step, RING)).wait_recv()
+            back_copy(step).wait_recv()
             return nothing
 
-        lax.fori_loop(1, RING, arrive, 0)
+        lax.fori_loop(1, HALF, arrive, 0)
+
+        def extra_arrive(group, nothing):
+            extra_copy(group).wait_recv()
+            return nothing
+
+        @pl.when(place == HALF - 1)
+        def _():
+            lax.fori_loop(0, HALF, extra_arrive, 0)
+
+        @pl.when(place != HALF - 1)
+        def _():
+            extra_far[...] = jnp.zeros(extra_far.shape, BF16)
+
         for copy in loads:
             copy.wait()
         nothing = jnp.zeros((HEAD_DIM, BLOCK), F32)
         query_terms = lax.fori_loop(0, heads, query_head, nothing)
         key_terms = lax.fori_loop(0, pairs, key_head, nothing)
         turned_copy.start()
-        onward(3)
-        deeper(1)
-        far(0)
         for row in range(0, turned_own.shape[0], 128):
             natural[:, row : row + 128] = turned_own[row : row + 128, :].astype(F32).T.astype(BF16)
+        deeper(2)
         normed_copy.wait_recv()
         turned_copy.wait_recv()
 
@@ -983,30 +908,8 @@
             return carry
 
         lax.fori_loop(0, 8, tail_one, 0)
-        onward(0)
-
-        def tail_two(index, carry):
-            for chain in tails:
-                chain.stage_two(lax.rem(index + 1, 4))
-            return carry
-
-        lax.fori_loop(0, 4, tail_two, 0)
-        deeper(3)
-        for chain in chains:
-            chain.drain_first()
-        for part in range(2):
-            for column in range(8):
-                weight_load(part, column).start()
-
-        for part, slots in enumerate((sent_a, sent_b)):
-            total = None
-            for column in range(8):
-                weight_load(part, column).wait()
-                term = dot_dims(
-                    natural[:, column * 256 : column * 256 + 256], slots[column, 0:512, :], 1, 1
-                )
-                total = term if total is None else total + term
-            summed[:, part * 512 : part * 512 + 512] = total
+        near(0)
+        summed[...] = dot_dims(natural[...], weights_ref[...], 1, 1)
         middle_load.wait()
 
         def token_rows(index, total):
@@ -1021,11 +924,11 @@
         terms = lax.fori_loop(
             0, BLOCK // 32, token_rows, jnp.zeros((1, tokens_ref.shape[1]), F32)
         )
-        gain_own[0] = jnp.zeros(gain_own.shape[1:], F32)
-        gain_own[0, 0:1, :] = terms
-        gain_own[0, 1:2, :] = ffn_terms_ref[...]
-        gain_own[0, 2:3, 0:HEAD_DIM] = jnp.sum(query_terms.T, axis=0, keepdims=True)
-        gain_own[0, 3:4, 0:HEAD_DIM] = jnp.sum(key_terms.T, axis=0, keepdims=True)
+        gain_own[...] = jnp.zeros(gain_own.shape, F32)
+        gain_own[0:1, :] = terms
+        gain_own[1:2, :] = ffn_terms_ref[...]
+        gain_own[2:3, 0:HEAD_DIM] = jnp.sum(query_terms.T, axis=0, keepdims=True)
+        gain_own[3:4, 0:HEAD_DIM] = jnp.sum(key_terms.T, axis=0, keepdims=True)
 
     width = normed_ref.shape[1]
     pl.run_scoped(
@@ -1035,67 +938,81 @@
         pltpu.VMEM((heads, HEAD_DIM, BLOCK), F32),
         pltpu.VMEM((pairs, HEAD_DIM, BLOCK), F32),
         pltpu.VMEM((BLOCK, width), BF16),
-    )
-
-    gain_copies = []
-
-    def gain_copy(source, target, sem, peer):
-        copy = remote(source, target, gain_send.at[sem], gain_recv.at[sem], peer)
-        copy.start()
-        gain_copies.append(copy)
-
-    gain_copy(gain_own.at[0], gain_came.at[0], 0, near_x)
+        pltpu.VMEM(weights_hbm.shape, BF16),
+    )
+
+    def tail_two(index, carry):
+        for chain in tails:
+            chain.stage_two(lax.rem(index + 1, 4))
+        return carry
 
     def tail_three(depth, carry):
         for chain in tails:
             chain.stage_three(depth)
         return carry
 
+    gain_swap = core_copy(gain_own, gain_came, 22)
+    gain_swap.start()
+
+    def gain_copy(step):
+        peer = (lax.rem(place + step, RING), core)
+        return remote(
+            gain_all.at[place], gain_all.at[place], gain_send.at[step], gain_recv.at[step], peer
+        )
+
+    def gain_start(step, carry):
+        gain_copy(step).start()
+        return carry
+
+    def gain_arrive(step, carry):
+        gain_copy(step).wait()
+        return carry
+
+    onward(3)
+    deeper(1)
+    far(0)
+    gain_swap.wait()
+    gain_all[place] = gain_own[...] + gain_came[...]
+    lax.fori_loop(1, RING, gain_start, 0)
+    lax.fori_loop(0, 4, tail_two, 0)
+    onward(0)
+    deeper(3)
     lax.fori_loop(1, 4, tail_three, 0)
-    gain_copies[0].wait_recv()
-    gain_own[1] = gain_own[0] + gain_came[0]
-    gain_copy(gain_own.at[1], gain_came.at[1], 1, near_y)
     pair_copy(0, 0, 0).wait_recv()
-    chains[0].close(finish)
-    gain_copies[1].wait_recv()
-    gain_own[2] = gain_own[1] + gain_came[1]
-    gain_copy(gain_own.at[2], gain_came.at[2], 2, partner)
-    chains[1].close(finish)
-    gain_copies[2].wait_recv()
-    gain_own[3] = gain_own[2] + gain_came[2]
-    gain_deep[z] = gain_own[3]
-    for step in range(1, 4):
-        deep = (lax.rem(place + 4 * step, RING), core)
-        gain_copy(gain_own.at[3], gain_deep.at[z], 2 + step, deep)
+    for chain in chains:
+        chain.close(finish)
     for chain in tails:
         chain.close(tail_finish)
-    for copy in gain_copies[3:]:
-        copy.wait_recv()
-    gains_out[...] = (gain_deep[0] + gain_deep[1]) + (gain_deep[2] + gain_deep[3])
+    lax.fori_loop(1, RING, gain_arrive, 0)
+
+    def gain_sum(index, total):
+        return total + gain_all[index]
+
+    gains_out[...] = lax.fori_loop(1, RING, gain_sum, gain_all[0])
 
     def settle(step, nothing):
-        peer = lax.rem(place + step, RING)
-        back_copy(step, peer).wait_send()
-        cot_copy(step, peer).wait_send()
+        back_copy(step).wait_send()
+        cot_copy(step).wait_send()
         return nothing
 
-    lax.fori_loop(1, RING, settle, 0)
-    for copy in sides + [normed_copy, turned_copy] + gain_copies:
+    lax.fori_loop(1, HALF, settle, 0)
+
+    @pl.when(part == 1)
+    def _():
+        extra_copy(member).wait_send()
+
+    for copy in sides + [normed_copy, turned_copy]:
         copy.wait_send()
     for turn_x, turn_y, depth in order:
         pair_copy(turn_x, turn_y, depth).wait_send()
-    for chain in chains:
-        chain.drain_last()
-    for chain in tails:
-        chain.drain_first()
-        chain.drain_last()
+    for chain in chains + tails:
+        chain.drain()
 
 
 def back_call(call_id, inputs, loads):
-    pair, hidden, side, ffn_low, qkv = (inputs[k] for k in (0, 1, 2, 3, 6))
+    pair, hidden, side, ffn_low = inputs[:4]
     rows, hidden_width = hidden.shape
     width = ffn_low.shape[1]
-    blocks = qkv.shape[0]
     wide, narrow = hidden_width // RING, width // RING
     total = (HEADS + 2 * KV_HEADS) * HEAD_DIM
 
@@ -1132,22 +1049,25 @@
             pltpu.VMEM((rows, width // 2), BF16),
             pltpu.VMEM((width // 2, rows), BF16),
             pltpu.VMEM((rows, width // 2), BF16),
-            pltpu.VMEM((blocks, HEAD_DIM, BLOCK), BF16),
-            pltpu.VMEM(qkv.shape, BF16),
-            pltpu.VMEM(qkv.shape, BF16),
+            pltpu.VMEM((HALF, 2 * HEAD_DIM, rows), BF16),
+            pltpu.VMEM((HALF, 4 * HEAD_DIM, rows), BF16),
+            pltpu.VMEM((HALF, 4 * HEAD_DIM, rows), BF16),
+            pltpu.VMEM((2 * HEAD_DIM, rows), BF16),
+            pltpu.VMEM((HALF, 2 * HEAD_DIM, rows), BF16),
             pltpu.VMEM((total, rows), BF16),
             pltpu.VMEM((total, rows), BF16),
-            pltpu.VMEM((4, 4, width), F32),
-            pltpu.VMEM((3, 4, width), F32),
-            pltpu.VMEM((4, 4, width), F32),
+            pltpu.VMEM((4, width), F32),
+            pltpu.VMEM((4, width), F32),
+            pltpu.VMEM((RING, 4, width), F32),
         ]
         + buffers((2 * wide + 6 * narrow, 2 * wide + 5 * narrow))
         + buffers((total // RING, total // RING))
         + [dma((2, 15))] * 4
-        + [dma((RING,))] * 4
-        + [dma((22,))] * 2
-        + [dma((6,))] * 2
-        + [dma((5,)), dma((2, 8))],
+        + [dma((HALF,))] * 4
+        + [dma((23,))] * 2
+        + [dma((RING,))] * 2
+        + [dma((HALF,))] * 2
+        + [dma((6,))],
         compiler_params=pltpu.CompilerParams(
             collective_id=call_id, has_side_effects=True, vmem_limit_bytes=63 << 20
         ),
@@ -1155,81 +1075,125 @@
     )(*inputs, *loads)
 
 
-def angle_parts(positions):
+def head_table(positions, query_gain, key_gain):
     half = HEAD_DIM // 2
     inverse_freq = THETA ** (-(2.0 / HEAD_DIM) * jnp.arange(half, dtype=F32))
     angles = inverse_freq[:, None] * positions.astype(F32)[None, :]
-    return jnp.cos(angles), jnp.sin(angles)
+    shape = (HEAD_DIM, positions.shape[0])
+    return jnp.concatenate(
+        [
+            jnp.cos(angles),
+            jnp.sin(angles),
+            jnp.broadcast_to(query_gain[:, None], shape),
+            jnp.broadcast_to(key_gain[:, None], shape),
+        ],
+        axis=0,
+    )
 
 
 def front_kernel(
-    tokens_ref,
     gain_ref,
-    w_query_ref,
-    w_key_ref,
-    w_value_ref,
-    query_gain_ref,
-    key_gain_ref,
-    cosine_ref,
-    sine_ref,
+    table_ref,
     own_start_ref,
+    tokens_hbm,
+    w_query_hbm,
+    w_key_hbm,
+    w_value_hbm,
+    w_out_hbm,
+    w_gate_hbm,
+    w_up_hbm,
+    w_down_hbm,
     qkv_out,
     starts_out,
+    normed_out,
+    part_out,
+    mixed_out,
+    inv_out,
+    out_full,
+    query_hbm,
+    key_hbm,
+    weights_hbm,
+    gate_far,
+    up_far,
+    down_far,
+    home,
+    key_nat,
+    tokens_ref,
     query_out,
     key_out,
-    normed_out,
     weights_out,
-    home,
+    keep_sem,
     own_sem,
     send_sem,
     recv_sem,
     start_send,
     start_recv,
+    mixed_send,
+    mixed_recv,
+    extra_send,
+    extra_recv,
     core_send,
     core_recv,
 ):
     place, core = lax.axis_index("ctx"), lax.axis_index("fsdp")
+    part, member = place // HALF, lax.rem(place, HALF)
     rows = tokens_ref.shape[0]
-    depth = w_query_ref.shape[0]
+    depth = w_query_hbm.shape[0]
     partner = (place, 1 - core)
+    tokens_load = pltpu.make_async_copy(tokens_hbm, tokens_ref, keep_sem.at[0])
+    tokens_load.start()
     greet([partner] + [(lax.rem(place + step, RING), core) for step in range(1, RING)])
 
-    def own_rows(part):
-        return pl.ds(pl.multiple_of(part * depth, 128), depth)
-
-    copies, locals_, column = [], [], 0
-    for index, source in enumerate((w_key_ref, w_value_ref, w_query_ref)):
-        window = pl.ds(column, source.shape[1])
-        target = weights_out.at[own_rows(core), window]
-        copy = pltpu.make_async_remote_copy(
+    def remote(source, target, send, recv, peer):
+        return pltpu.make_async_remote_copy(
             src_ref=source,
             dst_ref=target,
-            send_sem=core_send.at[index],
-            recv_sem=core_recv.at[index],
-            device_id=partner,
+            send_sem=send,
+            recv_sem=recv,
+            device_id=peer,
             device_id_type=MESH,
         )
+
+    def mate(step):
+        return (part * HALF + lax.rem(member + step, HALF), core)
+
+    copies, near_copies = [], []
+
+    def share(source, target, near_target=None):
+        index = len(copies)
+        copy = remote(source, target, core_send.at[index], core_recv.at[index], partner)
         copy.start()
         copies.append(copy)
-        near = pltpu.make_async_copy(source, target, own_sem.at[index])
-        near.start()
-        locals_.append(near)
+        if near_target is not None:
+            near = pltpu.make_async_copy(source, near_target, own_sem.at[index])
+            near.start()
+            near_copies.append(near)
+
+    column = 0
+    own_depth = pl.ds(pl.multiple_of(core * depth, 128), depth)
+    for source in (w_key_hbm, w_value_hbm, w_query_hbm):
+        window = pl.ds(column, source.shape[1])
+        target = weights_out.at[own_depth, window]
+        share(source, target, target)
         column += source.shape[1]
 
+    target = out_full.at[own_depth, :]
+    share(w_out_hbm, target, target)
+    for source, target in ((w_gate_hbm, gate_far), (w_up_hbm, up_far), (w_down_hbm, down_far)):
+        share(source, target)
+
     def start_copy(step):
-        peer = lax.rem(place + step, RING)
-        return pltpu.make_async_remote_copy(
-            src_ref=own_start_ref,
-            dst_ref=starts_out.at[place],
-            send_sem=start_send.at[step],
-            recv_sem=start_recv.at[step],
-            device_id=(peer, core),
-            device_id_type=MESH,
-        )
-
-    for step in range(1, RING):
+        return remote(
+            own_start_ref,
+            starts_out.at[member],
+            start_send.at[step],
+            start_recv.at[step],
+            mate(step),
+        )
+
+    for step in range(1, HALF):
         start_copy(step).start()
-    starts_out[place] = own_start_ref[...]
+    starts_out[member] = own_start_ref[...]
 
     def norm_rows(index, nothing):
         window = pl.ds(pl.multiple_of(index * 32, 32), 32)
@@ -1238,9 +1202,12 @@
         normed_out[window, :] = (values * inverse * gain_ref[...]).astype(BF16)
         return nothing
 
+    tokens_load.wait()
     lax.fori_loop(0, rows // 32, norm_rows, 0)
-    cosine, sine = cosine_ref[...], sine_ref[...]
     half = HEAD_DIM // 2
+    cosine, sine = table_ref[0:half, :], table_ref[half:HEAD_DIM, :]
+    query_gain = table_ref[HEAD_DIM : 2 * HEAD_DIM, :]
+    key_gain = table_ref[2 * HEAD_DIM : 3 * HEAD_DIM, :]
 
     def project(column, count):
         window = pl.ds(column, count)
@@ -1255,117 +1222,239 @@
             [first * cosine - second * sine, second * cosine + first * sine], axis=0
         ).astype(BF16)
 
-    group = HEADS // KV_HEADS
     kv_width = KV_HEADS * HEAD_DIM
     copies[0].wait_recv()
-    locals_[0].wait()
+    near_copies[0].wait()
 
     def key_chunk(index, nothing):
         products = project(pl.multiple_of(index * 256, 256), 256)
-        for member in range(4):
-            raw = products[member * HEAD_DIM : (member + 1) * HEAD_DIM]
-            pair = index * 4 + member
-            key_out[pair] = raw
-            key = turned(raw, key_gain_ref[...])
-            for twin in range(group):
-                home[group * pair + twin, HEAD_DIM : 2 * HEAD_DIM, :] = key
+        for offset in range(4):
+            raw = products[offset * HEAD_DIM : (offset + 1) * HEAD_DIM]
+            group = index * 4 + offset
+            key_out[group] = raw
+            home[group, 2 * HEAD_DIM : 3 * HEAD_DIM, :] = turned(raw, key_gain)
         return nothing
 
     lax.fori_loop(0, KV_HEADS // 4, key_chunk, 0)
     copies[1].wait_recv()
-    locals_[1].wait()
+    near_copies[1].wait()
 
     def value_chunk(index, nothing):
         products = project(pl.multiple_of(kv_width + index * 256, 256), 256)
-        for member in range(4):
-            value = products[member * HEAD_DIM : (member + 1) * HEAD_DIM].astype(BF16)
-            for twin in range(group):
-                home[group * (index * 4 + member) + twin, 2 * HEAD_DIM : 3 * HEAD_DIM, :] = value
+        for offset in range(4):
+            value = products[offset * HEAD_DIM : (offset + 1) * HEAD_DIM].astype(BF16)
+            home[index * 4 + offset, 3 * HEAD_DIM : 4 * HEAD_DIM, :] = value
         return nothing
 
     lax.fori_loop(0, KV_HEADS // 4, value_chunk, 0)
+
+    def extra_copy(group):
+        window = pl.ds(2 * HEAD_DIM, 2 * HEAD_DIM)
+        return remote(
+            home.at[group, window],
+            qkv_out.at[0, window],
+            extra_send.at[group],
+            extra_recv.at[group],
+            (HALF + group, core),
+        )
+
+    def extra_start(group, nothing):
+        extra_copy(group).start()
+        return nothing
+
+    @pl.when(place == HALF - 1)
+    def _():
+        lax.fori_loop(0, HALF, extra_start, 0)
+
     copies[2].wait_recv()
-    locals_[2].wait()
+    near_copies[2].wait()
 
     def block_copy(step):
-        peer = lax.rem(place + step, RING)
-        return pltpu.make_async_remote_copy(
-            src_ref=home.at[peer],
-            dst_ref=qkv_out.at[place],
-            send_sem=send_sem.at[step],
-            recv_sem=recv_sem.at[step],
-            device_id=(peer, core),
-            device_id_type=MESH,
+        peer = mate(step)
+        return remote(
+            home.at[lax.rem(member + step, HALF)],
+            qkv_out.at[1 + member],
+            send_sem.at[step],
+            recv_sem.at[step],
+            peer,
         )
 
     def query_chunk(index, nothing):
         products = project(pl.multiple_of(2 * kv_width + index * 256, 256), 256)
-        for member in range(4):
-            raw = products[member * HEAD_DIM : (member + 1) * HEAD_DIM]
-            head = index * 4 + member
-            query_out[head] = raw
-            home[head, 0:HEAD_DIM, :] = turned(raw, query_gain_ref[...])
-
-            @pl.when(head != place)
+        for offset in range(4):
+            raw = products[offset * HEAD_DIM : (offset + 1) * HEAD_DIM]
+            query_out[index * 4 + offset] = raw
+            low = (offset % 2) * HEAD_DIM
+            home[index * 2 + offset // 2, low : low + HEAD_DIM, :] = turned(
+                raw, query_gain
+            )
+        for offset in range(2):
+            group = index * 2 + offset
+
+            @pl.when(group != member)
             def _():
-                block_copy(lax.rem(head - place + RING, RING)).start()
+                block_copy(lax.rem(group - member + HALF, HALF)).start()
 
         return nothing
 
     lax.fori_loop(0, HEADS // 4, query_chunk, 0)
-    qkv_out[place] = home[place]
+    keeps = [
+        pltpu.make_async_copy(source, target, keep_sem.at[1 + index])
+        for index, (source, target) in enumerate(
+            ((query_out, query_hbm), (key_out, key_hbm), (weights_out, weights_hbm))
+        )
+    ]
+    for keep in keeps:
+        keep.start()
+    qkv_out[1 + member] = home[member]
+    base = part * HALF - 1
+
+    @pl.when(part == 1)
+    def _():
+        extra_copy(member).wait_recv()
+        key_nat[0] = transposed(qkv_out[0, 2 * HEAD_DIM : 3 * HEAD_DIM, :])
+
+    def mixed_copy(step):
+        peer = mate(step)
+        return remote(
+            part_out.at[lax.rem(member + step, HALF)],
+            mixed_out.at[member],
+            mixed_send.at[step],
+            mixed_recv.at[step],
+            peer,
+        )
+
+    def per_query(i, nothing):
+        @pl.when(i - 1 != member)
+        def _():
+            step = lax.rem(member - i + 1 + HALF, HALF)
+            block_copy(step).wait_recv()
+            start_copy(step).wait_recv()
+
+        key_nat[i] = transposed(qkv_out[i, 2 * HEAD_DIM : 3 * HEAD_DIM, :])
+        query_t = jnp.concatenate(
+            [qkv_out[i, 0:HEAD_DIM, :], qkv_out[i, HEAD_DIM : 2 * HEAD_DIM, :]], axis=1
+        ) * jnp.asarray(HEAD_DIM**-0.5, BF16)
+        start = jnp.concatenate([starts_out[i - 1]] * 2, axis=1)
+        places = (base + i) * BLOCK + lax.broadcasted_iota(jnp.int32, (1, BLOCK), 1)
+        query_place = jnp.concatenate([places] * 2, axis=1)
+
+        def step(diagonal, j, carry):
+            total, acc = carry
+            scores = jnp.dot(key_nat[j], query_t, preferred_element_type=F32)
+            key_place = (base + j) * BLOCK + lax.broadcasted_iota(jnp.int32, scores.shape, 0)
+            ok = key_place >= start
+            if diagonal:
+                ok = ok & (key_place <= query_place)
+            probs = jnp.where(ok, jnp.exp(scores), 0.0)
+            total = total + jnp.sum(probs, axis=0, keepdims=True)
+            acc = acc + jnp.dot(
+                qkv_out[j, 3 * HEAD_DIM : 4 * HEAD_DIM, :],
+                probs.astype(BF16),
+                preferred_element_type=F32,
+            )
+            return total, acc
+
+        carry = (jnp.zeros((1, 2 * BLOCK), F32), jnp.zeros((HEAD_DIM, 2 * BLOCK), F32))
+        carry = lax.fori_loop(1 - part, i, functools.partial(step, False), carry)
+        total, acc = step(True, i, carry)
+        inverse = 1.0 / total
+        low = (acc * inverse).astype(BF16)
+        part_out[i - 1, 0:HEAD_DIM, :] = low[:, :BLOCK]
+        part_out[i - 1, HEAD_DIM:, :] = low[:, BLOCK:]
+        inv_out[i - 1] = inverse
+
+        @pl.when(i - 1 != member)
+        def _():
+            mixed_copy(lax.rem(i - 1 - member + HALF, HALF)).start()
+
+        return nothing
+
+    lax.fori_loop(1, HALF + 1, per_query, 0)
+    mixed_out[member] = part_out[member]
 
     def settle(step, nothing):
-        block_copy(step).wait()
-        start_copy(step).wait()
+        block_copy(step).wait_send()
+        start_copy(step).wait_send()
+        mixed_copy(step).wait()
         return nothing
 
-    lax.fori_loop(1, RING, settle, 0)
-    for copy in copies:
+    lax.fori_loop(1, HALF, settle, 0)
+
+    def extra_settle(group, nothing):
+        extra_copy(group).wait_send()
+        return nothing
+
+    @pl.when(place == HALF - 1)
+    def _():
+        lax.fori_loop(0, HALF, extra_settle, 0)
+
+    for copy in copies[:3]:
         copy.wait_send()
-
-
-def front_call(call_id, *inputs):
-    rows, width = inputs[0].shape
+    for copy in copies[3:]:
+        copy.wait()
+    for near in near_copies[3:] + keeps:
+        near.wait()
+
+
+def front_call(call_id, inputs, loads):
+    rows, width = loads[0].shape
+    half_depth, hidden_width = loads[5].shape
     total = (HEADS + 2 * KV_HEADS) * HEAD_DIM
+    dma = pltpu.SemaphoreType.DMA
+    query_raw = (HEADS, HEAD_DIM, rows)
+    key_raw = (KV_HEADS, HEAD_DIM, rows)
     return pl.pallas_call(
         front_kernel,
         out_shape=(
-            jax.ShapeDtypeStruct((RING, 3 * HEAD_DIM, rows), BF16),
-            jax.ShapeDtypeStruct((RING, 1, rows), jnp.int32),
-            jax.ShapeDtypeStruct((HEADS, HEAD_DIM, rows), F32),
-            jax.ShapeDtypeStruct((KV_HEADS, HEAD_DIM, rows), F32),
+            jax.ShapeDtypeStruct((HALF + 1, 4 * HEAD_DIM, rows), BF16),
+            jax.ShapeDtypeStruct((HALF, 1, rows), jnp.int32),
             jax.ShapeDtypeStruct((rows, width), BF16),
+            jax.ShapeDtypeStruct((HALF, 2 * HEAD_DIM, rows), BF16),
+            jax.ShapeDtypeStruct((HALF, 2 * HEAD_DIM, rows), BF16),
+            jax.ShapeDtypeStruct((HALF, 1, 2 * rows), F32),
+            jax.ShapeDtypeStruct((width, width), BF16),
+            jax.ShapeDtypeStruct(query_raw, F32),
+            jax.ShapeDtypeStruct(key_raw, F32),
             jax.ShapeDtypeStruct((width, total), BF16),
+            jax.ShapeDtypeStruct((half_depth, hidden_width), BF16),
+            jax.ShapeDtypeStruct((half_depth, hidden_width), BF16),
+            jax.ShapeDtypeStruct((hidden_width // 2, width), BF16),
         ),
-        in_specs=[VMEM_SPEC] * len(inputs),
-        out_specs=(VMEM_SPEC,) * 6,
+        in_specs=[VMEM_SPEC] * len(inputs) + [HBM_SPEC] * len(loads),
+        out_specs=(VMEM_SPEC,) * 7 + (HBM_SPEC,) * 6,
         scratch_shapes=[
-            pltpu.VMEM((RING, 3 * HEAD_DIM, rows), BF16),
-            pltpu.SemaphoreType.DMA((3,)),
-            pltpu.SemaphoreType.DMA((RING,)),
-            pltpu.SemaphoreType.DMA((RING,)),
-            pltpu.SemaphoreType.DMA((RING,)),
-            pltpu.SemaphoreType.DMA((RING,)),
-            pltpu.SemaphoreType.DMA((3,)),
-            pltpu.SemaphoreType.DMA((3,)),
-        ],
+            pltpu.VMEM((HALF, 4 * HEAD_DIM, rows), BF16),
+            pltpu.VMEM((HALF + 1, rows, HEAD_DIM), BF16),
+            pltpu.VMEM((rows, width), BF16),
+            pltpu.VMEM(query_raw, F32),
+            pltpu.VMEM(key_raw, F32),
+            pltpu.VMEM((width, total), BF16),
+            dma((4,)),
+            dma((4,)),
+        ]
+        + [dma((HALF,))] * 8
+        + [dma((7,))] * 2,
         compiler_params=pltpu.CompilerParams(
-            collective_id=call_id, has_side_effects=True, vmem_limit_bytes=48 << 20
+            collective_id=call_id, has_side_effects=True, vmem_limit_bytes=63 << 20
         ),
         name="front_heads",
-    )(*inputs)
+    )(*inputs, *loads)
 
 
 def ffn_kernel(
+    core_ref,
     tokens_ref,
     mixed_ref,
     w_out_ref,
     gain_ref,
     cot_ref,
-    gate_ref,
-    up_ref,
-    down_ref,
+    gate_own,
+    gate_far,
+    up_own,
+    up_far,
+    down_own,
+    down_far,
     pair_out,
     hidden_out,
     output_out,
@@ -1407,25 +1496,43 @@
         upstream[...] = jnp.zeros(upstream.shape, F32)
         side_out[0] = cot_ref[...].astype(F32).T.astype(BF16)
 
-    gate_pre = jnp.dot(ffn_out[...], gate_ref[...], preferred_element_type=F32)
-    up_pre = jnp.dot(ffn_out[...], up_ref[...], preferred_element_type=F32)
-    grad_hidden = dot_dims(cot_ref[...], down_ref[...], 1, 1)
-    gate_sig = jax.nn.sigmoid(gate_pre)
-    gate_act = gate_pre * gate_sig
-    hidden_out[...] = (gate_act * up_pre).astype(BF16)
-    gate_back = (grad_hidden * up_pre * (gate_sig * (1.0 + gate_pre * (1.0 - gate_sig)))).astype(
-        BF16
-    )
-    up_back = (grad_hidden * gate_act).astype(BF16)
-    result[...] += jnp.dot(hidden_out[...], down_ref[...], preferred_element_type=F32)
-    upstream[...] += dot_dims(gate_back, gate_ref[...], 1, 1) + dot_dims(
-        up_back, up_ref[...], 1, 1
-    )
-    wide = pair_out.shape[1] // 2
-    for base, back in ((0, gate_back), (wide, up_back)):
-        turned = back.astype(F32).T.astype(BF16)
-        for owner in range(pair_out.shape[0]):
-            pair_out[owner, base : base + wide, :] = turned[owner * wide : (owner + 1) * wide]
+    depth = gate_own.shape[0]
+    own = pl.ds(pl.multiple_of(core_ref[0] * depth, 128), depth)
+    far = pl.ds(pl.multiple_of((1 - core_ref[0]) * depth, 128), depth)
+
+    def strip_of_hidden(down_ref):
+        def ahead(near_ref, far_ref):
+            return jnp.dot(ffn_out[:, own], near_ref[...], preferred_element_type=F32) + jnp.dot(
+                ffn_out[:, far], far_ref[...], preferred_element_type=F32
+            )
+
+        gate_pre, up_pre = ahead(gate_own, gate_far), ahead(up_own, up_far)
+        grad_hidden = dot_dims(cot_ref[...], down_ref[...], 1, 1)
+        gate_sig = jax.nn.sigmoid(gate_pre)
+        gate_act = gate_pre * gate_sig
+        hidden_out[...] = (gate_act * up_pre).astype(BF16)
+        gate_back = (
+            grad_hidden * up_pre * (gate_sig * (1.0 + gate_pre * (1.0 - gate_sig)))
+        ).astype(BF16)
+        up_back = (grad_hidden * gate_act).astype(BF16)
+        result[...] += jnp.dot(hidden_out[...], down_ref[...], preferred_element_type=F32)
+        for window, gate_ref, up_ref in ((own, gate_own, up_own), (far, gate_far, up_far)):
+            upstream[:, window] += dot_dims(gate_back, gate_ref[...], 1, 1) + dot_dims(
+                up_back, up_ref[...], 1, 1
+            )
+        wide = pair_out.shape[1] // 2
+        for base, back in ((0, gate_back), (wide, up_back)):
+            turned = back.astype(F32).T.astype(BF16)
+            for owner in range(pair_out.shape[0]):
+                pair_out[owner, base : base + wide, :] = turned[owner * wide : (owner + 1) * wide]
+
+    @pl.when(step < 2)
+    def _():
+        strip_of_hidden(down_own)
+
+    @pl.when(step >= 2)
+    def _():
+        strip_of_hidden(down_far)
 
     @pl.when(step == pl.num_programs(0) - 1)
     def _():
@@ -1450,20 +1557,54 @@
         side_out[1] = middle_low[...].astype(F32).T.astype(BF16)
 
 
-def ffn_call(tokens, mixed_t, w_out, gain, cot, gate, up, down):
+def ffn_call(core, tokens, mixed_t, w_out, gain, cot, gate, up, down):
     rows, width = tokens.shape
-    hidden_width = gate.shape[1]
+    half_depth, hidden_width = gate[0].shape
     steps = 4
     chunk = hidden_width // steps
     owners = RING // steps
     wide = hidden_width // RING
 
     def whole(*shape):
-        return pl.BlockSpec(shape, lambda i: (0,) * len(shape))
-
+        return pl.BlockSpec(shape, lambda i, core_ref: (0,) * len(shape))
+
+    def turn(i, core_ref):
+        return lax.rem(i + 2 * core_ref[0], steps)
+
+    columns = pl.BlockSpec((half_depth, chunk), lambda i, core_ref: (0, turn(i, core_ref)))
     return pl.pallas_call(
         ffn_kernel,
-        grid=(steps,),
+        grid_spec=pltpu.PrefetchScalarGridSpec(
+            num_scalar_prefetch=1,
+            grid=(steps,),
+            in_specs=[
+                whole(rows, width),
+                whole(width, rows),
+                whole(width, width),
+                whole(1, width),
+                whole(rows, width),
+                columns,
+                columns,
+                columns,
+                columns,
+                pl.BlockSpec((chunk, width), lambda i, core_ref: (jnp.minimum(i, 1), 0)),
+                pl.BlockSpec((chunk, width), lambda i, core_ref: (jnp.maximum(i - 2, 0), 0)),
+            ],
+            out_specs=(
+                pl.BlockSpec(
+                    (owners, 2 * wide, rows), lambda i, core_ref: (turn(i, core_ref), 0, 0)
+                ),
+                pl.BlockSpec((rows, chunk), lambda i, core_ref: (0, turn(i, core_ref))),
+                whole(rows, width),
+                whole(rows, width),
+                whole(2, width, rows),
+                whole(width, rows),
+                whole(rows, width),
+                whole(1, width),
+            ),
+            scratch_shapes=[pltpu.VMEM((rows, width), F32)] * 3
+            + [pltpu.VMEM((rows, width), BF16)],
+        ),
         out_shape=(
             jax.ShapeDtypeStruct((RING, 2 * wide, rows), BF16),
             jax.ShapeDtypeStruct((rows, hidden_width), BF16),
@@ -1474,34 +1615,60 @@
             jax.ShapeDtypeStruct((rows, width), F32),
             jax.ShapeDtypeStruct((1, width), F32),
         ),
-        in_specs=[
-            whole(rows, width),
-            whole(width, rows),
-            whole(width, width),
-            whole(1, width),
-            whole(rows, width),
-            pl.BlockSpec((width, chunk), lambda i: (0, i)),
-            pl.BlockSpec((width, chunk), lambda i: (0, i)),
-            pl.BlockSpec((chunk, width), lambda i: (i, 0)),
-        ],
-        out_specs=(
-            pl.BlockSpec((owners, 2 * wide, rows), lambda i: (i, 0, 0)),
-            pl.BlockSpec((rows, chunk), lambda i: (0, i)),
-            whole(rows, width),
-            whole(rows, width),
-            whole(2, width, rows),
-            whole(width, rows),
-            whole(rows, width),
-            whole(1, width),
-        ),
-        scratch_shapes=[pltpu.VMEM((rows, width), F32)] * 3 + [pltpu.VMEM((rows, width), BF16)],
-        compiler_params=pltpu.CompilerParams(vmem_limit_bytes=56 << 20),
+        compiler_params=pltpu.CompilerParams(vmem_limit_bytes=63 << 20),
         name="ffn_both_ways",
-    )(tokens, mixed_t, w_out, gain, cot, gate, up, down)
-
-
-def both(block, axis):
-    return lax.all_gather(block, "fsdp", axis=axis, tiled=True)
+    )(core, tokens, mixed_t, w_out, gain, cot, *gate, *up, *down)
+
+
+def settle_kernel(*refs):
+    count = 6
+    sources, gains, rest = refs[:count], refs[count], refs[count + 1 :]
+    targets, gain_targets, rest = rest[: count + 2], rest[count + 2 : count + 6], rest[count + 6 :]
+    held, in_sem, out_sem = rest[:count], rest[count], rest[count + 1]
+    loads = [
+        pltpu.make_async_copy(source, hold, in_sem.at[index])
+        for index, (source, hold) in enumerate(zip(sources, held))
+    ]
+    for load in loads:
+        load.start()
+    stores, row = [], 0
+    for index, load in enumerate(loads):
+        load.wait()
+        if index < count - 1:
+            pieces = [(held[index], targets[index])]
+        else:
+            pieces = []
+            for target in targets[index:]:
+                pieces.append((held[index].at[pl.ds(row, target.shape[0])], target))
+                row += target.shape[0]
+        for piece, target in pieces:
+            store = pltpu.make_async_copy(piece, target, out_sem.at[len(stores)])
+            store.start()
+            stores.append(store)
+    for index, target in enumerate(gain_targets):
+        target[...] = gains[index : index + 1, 0 : target.shape[1]]
+    for store in stores:
+        store.wait()
+
+
+def settle_call(tokens, gate_t, up_t, down_t, out_t, qkv_t, gains):
+    sources = (tokens, gate_t, up_t, down_t, out_t, qkv_t)
+    lanes = qkv_t.shape[1]
+    query = HEADS * HEAD_DIM // RING
+    pair = KV_HEADS * HEAD_DIM // RING
+    shapes = [source.shape for source in sources[:-1]]
+    shapes += [(query, lanes), (pair, lanes), (pair, lanes)]
+    gain_shapes = [(1, gains.shape[1])] * 2 + [(1, HEAD_DIM)] * 2
+    return pl.pallas_call(
+        settle_kernel,
+        out_shape=tuple(jax.ShapeDtypeStruct(shape, F32) for shape in shapes + gain_shapes),
+        in_specs=[HBM_SPEC] * len(sources) + [VMEM_SPEC],
+        out_specs=(HBM_SPEC,) * len(shapes) + (VMEM_SPEC,) * 4,
+        scratch_shapes=[pltpu.VMEM(source.shape, F32) for source in sources]
+        + [pltpu.SemaphoreType.DMA((6,)), pltpu.SemaphoreType.DMA((8,))],
+        compiler_params=pltpu.CompilerParams(vmem_limit_bytes=63 << 20),
+        name="settle_results",
+    )(*sources, gains)
 
 
 def heads_body(
@@ -1521,32 +1688,31 @@
     w_down,
     d_output,
 ):
-    place, core = lax.axis_index("ctx"), lax.axis_index("fsdp")
-    rows, width = tokens.shape[1], tokens.shape[2]
+    place = lax.axis_index("ctx")
+    rows = tokens.shape[1]
     pos_local = doc_pos[0]
-    o_full, gate_full = both(w_out, 0), both(w_gate, 0)
-    up_full, down_full = both(w_up, 0), both(w_down, 0)
     own_starts = place * rows + jnp.arange(rows, dtype=jnp.int32) - pos_local
-    cosine, sine = angle_parts(pos_local)
-    qkv, starts, query_raw, key_raw, normed_low, kvq_full = front_call(
+    table = head_table(pos_local, query_gain, key_gain)
+    (
+        qkv,
+        starts,
+        normed_low,
+        mixed_far,
+        mixed_home,
+        inverse_total,
+        o_full,
+        query_raw,
+        key_raw,
+        kvq_full,
+        gate_far,
+        up_far,
+        down_far,
+    ) = front_call(
         1,
-        tokens[0],
-        attn_gain[None, :],
-        w_query,
-        w_key,
-        w_value,
-        query_gain[:, None],
-        key_gain[:, None],
-        cosine,
-        sine,
-        own_starts[None, :],
-    )
-    first = starts[:, 0, 0] // BLOCK
-    own_index = jnp.arange(RING, dtype=jnp.int32)
-    clear = jnp.minimum((starts[:, 0, -1] + BLOCK - 1) // BLOCK, own_index)
-    mixed_far, inverse_total = attend(first, clear, qkv, starts)
-    mixed_t = exchange(mixed_far, 2).reshape(HEADS * HEAD_DIM, rows)
-
+        (attn_gain[None, :], table, own_starts[None, :]),
+        (tokens[0], w_query, w_key, w_value, w_out, w_gate, w_up, w_down),
+    )
+    mixed_t = mixed_home.reshape(HEADS * HEAD_DIM, rows)
     cot_low = d_output[0]
     (
         pair,
@@ -1558,7 +1724,15 @@
         grad_middle,
         ffn_terms,
     ) = ffn_call(
-        tokens[0], mixed_t, o_full, ffn_gain[None, :], cot_low, gate_full, up_full, down_full
+        lax.axis_index("fsdp").astype(jnp.int32)[None],
+        tokens[0],
+        mixed_t,
+        o_full,
+        ffn_gain[None, :],
+        cot_low,
+        (w_gate, gate_far),
+        (w_up, up_far),
+        (w_down, down_far),
     )
     gate_t, up_t, down_t, out_t, qkv_grads, d_tokens, gain_totals = back_call(
         3,
@@ -1568,35 +1742,35 @@
             side,
             ffn_low,
             mixed_t,
-            grad_mixed.reshape(HEADS, HEAD_DIM, rows),
+            grad_mixed.reshape(HALF, 2 * HEAD_DIM, rows),
             qkv,
             starts,
             mixed_far,
             inverse_total,
-            cosine,
-            sine,
-            query_gain[:, None],
-            key_gain[:, None],
+            table,
             normed_low,
             attn_gain[None, :],
             ffn_terms,
         ),
         (tokens[0], query_raw, key_raw, kvq_full, grad_middle),
     )
+    d_tokens, gate, up, down, out, query, key, value, attn, ffn, query_gains, key_gains = (
+        settle_call(d_tokens, gate_t, up_t, down_t, out_t, qkv_grads, gain_totals)
+    )
     return (
         output[None],
         d_tokens[None],
-        gain_totals[0],
-        qkv_grads[:64].T,
-        qkv_grads[64:96].T,
-        qkv_grads[96:].T,
-        gain_totals[2, :HEAD_DIM],
-        gain_totals[3, :HEAD_DIM],
-        out_t.T,
-        gain_totals[1],
-        gate_t.T,
-        up_t.T,
-        down_t.T,
+        attn[0],
+        query.T,
+        key.T,
+        value.T,
+        query_gains[0],
+        key_gains[0],
+        out.T,
+        ffn[0],
+        gate.T,
+        up.T,
+        down.T,
     )
 
 

time: 356 us -> 274 us (0.77)
  Pallas kernels: 317 us -> 266 us
  local copies, waits for them, and re-layouts: 17.1 us -> 1.39 us
  between operations: 14.1 us -> 0.84 us
    pallas_call x4 -> x3, Pallas kernels: 125 us -> 84.8 us  [the longest x1 50.7 us: front_call(): pl.pallas_call(front_kernel, out_shape=(jax.ShapeDtypeStruct((HALF + 1, 4...]
    unnamed x39 -> x0, local copies, waits for them, and re-layouts: 11.2 us -> none
    pallas_call x1, Pallas kernels: 192 us -> 181 us  [back_call(): pl.pallas_call(back_kernel, out_shape=(jax.ShapeDtypeStruct((wide, width...]
  transfers between devices with their start and end apart: 4 -> 0, of which waited for: 0 -> 0; matrix products, arithmetic and copies ran while one was open for 0% -> 0% of each run, Pallas kernels for 27% -> 0%
where the time goes in v5:
time: 274 us; the launch traced here: 270 us
  Pallas kernels  266 us (97%)
    pallas_call x1, Pallas kernels, back_call(): pl.pallas_call(back_kernel, out_shape=(jax.ShapeDtypeStruct((wide, width...  181 us
    pallas_call x1, Pallas kernels, front_call(): pl.pallas_call(front_kernel, out_shape=(jax.ShapeDtypeStruct((HALF + 1, 4...  50.7 us
    pallas_call x1, Pallas kernels, ffn_call(): pl.pallas_call(ffn_kernel, grid_spec=pltpu.PrefetchScalarGridSpec(num_sca...  29.8 us

profile of v5, /device:TPU:15, one launch (start us, length us, event | category | flops | bytes accessed | tf_op | source)
XLA Modules:
  0.0 270.4 jit_solution(10268075685915396779)
XLA Ops:
  0.7 0.7 pad.2.clone
  1.4 0.7 pad.3.clone
  2.1 1.3 add_subtract_fusion
  3.4 0.2 multiply_cosine_fusion
  3.6 0.8 maximum_maximum_fusion.table_ref
  4.4 50.7 %front_heads.1 = (bf16[9,256,256]{2,1,0:T(8,128)(2,1)}, s32[8,1,256]{2,1,0:T(1,128)}, bf16[256,1024]{1,0:T(8,128)(2,1)}, bf16[8,128,256]{2,1,0:T(8,128)(2,1)}, b...) custom-call(f32[1,1024]{1,0:T(1,128)} %bitcast.28, ...), custom_call_target="tpu_custom_call" | custom-call | tf_op jit(solution)/shard_map/front_heads/pallas_call | solution.py:1407
  55.1 29.8 %ffn_both_ways.1 = (bf16[16,576,256]{2,1,0:T(8,128)(2,1)}, bf16[256,4608]{1,0:T(8,128)(2,1)}, bf16[256,1024]{1,0:T(8,128)(2,1)}, bf16[256,1024]{1,0:T(8,128)(2,1...) custom-call(s32[1]{0:T(128)} %bitcast.core_ref, ...), custom_call_target="tpu_custom_call" | custom-call | tf_op jit(solution)/shard_map/ffn_both_ways/pallas_call | solution.py:1575
  84.9 181.1 %backward_spread.1 = (f32[288,512]{1,0:T(8,128)}, f32[288,512]{1,0:T(8,128)}, f32[64,2304]{1,0:T(8,128)}, f32[64,512]{1,0:T(8,128)}, f32[128,512]{1,0:T(8,128)}, /*index=5*/f32[256,1024]{1,0:T(8,128)}, f32[4,1024]{1,0:T(4,128)}) custom-call(bf16[16,576,256]{2,1,0:T(8,128)(2,1)} %get-tuple-element.59.pair_own, ...), custom_call_target="tpu_custom_call" | custom-call | tf_op jit(solution)/shard_map/backward_spread/pallas_call | solution.py:1031
  265.9 4.3 %settle_results.1 = (f32[256,1024]{1,0:T(8,128)}, f32[288,512]{1,0:T(8,128)}, f32[288,512]{1,0:T(8,128)}, f32[64,2304]{1,0:T(8,128)}, f32[64,512]{1,0:T(8,128)},...) custom-call(f32[256,1024]{1,0:T(8,128)} %get-tuple-element.74.refs_0, ...), custom_call_target="tpu_custom_call" | custom-call | tf_op jit(solution)/shard_map/settle_results/pallas_call | solution.py:1662
  (1 shorter events, 0.0 us)

commit v6 on v5

--- a/solution.py
+++ b/solution.py
@@ -2,6 +2,7 @@
 
 import jax
 import jax.numpy as jnp
+import numpy as np
 from jax import lax
 from jax.experimental import pallas as pl
 from jax.experimental.pallas import tpu as pltpu
@@ -321,6 +322,8 @@
 BLOCK = 256
 RING = 16
 HALF = 8
+EDGE = 128
+DOWN_CHUNKS = ((0, 3), (3, 2), (5, 4))
 VMEM_SPEC = pl.BlockSpec(memory_space=pltpu.VMEM)
 HBM_SPEC = pl.BlockSpec(memory_space=pltpu.HBM)
 SMEM_SPEC = pl.BlockSpec(memory_space=pltpu.SMEM)
@@ -427,6 +430,87 @@
             self.copy(2, depth).wait_send()
 
 
+class DeepSpread:
+    def __init__(self, compute, sent, came, send_sems, recv_sems):
+        self.place, self.core = lax.axis_index("ctx"), lax.axis_index("fsdp")
+        self.x, self.y = lax.rem(self.place, 2), lax.rem(self.place // 2, 2)
+        self.compute, self.sent, self.came = compute, sent, came
+        self.send_sems, self.recv_sems = send_sems, recv_sems
+
+    def copy(self, stage, slot):
+        if stage == 0:
+            peer = lax.rem(self.place + 4 * slot, RING)
+            source, target, sem = self.sent.at[slot - 1], self.came[0].at[slot - 1], slot - 1
+        elif stage == 1:
+            peer = self.place + 1 - 2 * self.x
+            local = flip(self.y, slot) * 2 + 1 - self.x
+            source, target, sem = self.came[0].at[0, local], self.came[1].at[slot], 3 + slot
+        else:
+            peer = self.place + 2 - 4 * self.y
+            local = (1 - self.y) * 2 + self.x
+            source, target, sem = self.came[0].at[0, local], self.came[2].at[0], 5
+        return pltpu.make_async_remote_copy(
+            src_ref=source,
+            dst_ref=target,
+            send_sem=self.send_sems.at[sem],
+            recv_sem=self.recv_sems.at[sem],
+            device_id=(peer, self.core),
+            device_id_type=MESH,
+        )
+
+    def stage_one(self, slot):
+        first = lax.rem(self.place // 4 + slot, 4) * 4
+        value = self.compute(first, 4)
+        rows = value.shape[0] // 4
+        for local in range(4):
+            for chunk in range(value.shape[1] // 256):
+                self.sent[slot - 1, local, chunk * rows : (chunk + 1) * rows, :] = value[
+                    local * rows : (local + 1) * rows, chunk * 256 : (chunk + 1) * 256
+                ].astype(BF16)
+        self.copy(0, slot).start()
+
+    def arrived(self, local):
+        value = self.compute(self.place - lax.rem(self.place, 4) + local, 1)
+        rows = value.shape[0]
+        for chunk in range(value.shape[1] // 256):
+            window = slice(chunk * rows, (chunk + 1) * rows)
+            total = value[:, chunk * 256 : (chunk + 1) * 256]
+            for slot in range(3):
+                total = total + self.came[0][slot, local, window, :].astype(F32)
+            yield window, total
+
+    def stage_two(self):
+        for slot in range(1, 4):
+            self.copy(0, slot).wait_recv()
+        for slot in (1, 0):
+            local = flip(self.y, slot) * 2 + 1 - self.x
+            for window, total in self.arrived(local):
+                self.came[0][0, local, window, :] = total.astype(BF16)
+            self.copy(1, slot).start()
+
+    def stage_three(self):
+        self.copy(1, 1).wait_recv()
+        local = (1 - self.y) * 2 + self.x
+        for window, total in self.arrived(local):
+            total = total + self.came[1][1, window, :].astype(F32)
+            self.came[0][0, local, window, :] = total.astype(BF16)
+        self.copy(2, 0).start()
+
+    def close(self, finish):
+        self.copy(1, 0).wait_recv()
+        self.copy(2, 0).wait_recv()
+        for window, total in self.arrived(lax.rem(self.place, 4)):
+            total = total + self.came[1][0, window, :].astype(F32)
+            finish(window, total + self.came[2][0, window, :].astype(F32))
+
+    def drain(self):
+        for slot in range(1, 4):
+            self.copy(0, slot).wait_send()
+        for slot in range(2):
+            self.copy(1, slot).wait_send()
+        self.copy(2, 0).wait_send()
+
+
 def greet(peers):
     barrier = pltpu.get_barrier_semaphore()
     for peer in peers:
@@ -450,18 +534,18 @@
 
 
 def back_kernel(
-    pair_own,
+    pair_hbm,
     hidden_hbm,
-    side_own,
-    ffn_ref,
-    mixed_ref,
-    home_ref,
-    qkv_ref,
+    side_hbm,
+    ffn_hbm,
+    mixed_hbm,
+    home_hbm,
+    qkv_hbm,
     start_ref,
-    part_ref,
+    part_hbm,
     inv_ref,
     table_ref,
-    normed_ref,
+    normed_hbm,
     attn_gain_ref,
     ffn_terms_ref,
     tokens_hbm,
@@ -476,6 +560,14 @@
     grads_out,
     tokens_out,
     gains_out,
+    pair_own,
+    side_own,
+    ffn_ref,
+    mixed_ref,
+    home_ref,
+    qkv_ref,
+    part_ref,
+    normed_ref,
     pair_far,
     side_far,
     hidden_own,
@@ -501,6 +593,12 @@
     came_b0,
     came_b1,
     came_b2,
+    sent_c,
+    came_c0,
+    came_c1,
+    came_c2,
+    deep_send,
+    deep_recv,
     tail_sent_a,
     tail_came_a0,
     tail_came_a1,
@@ -524,6 +622,7 @@
     extra_send,
     extra_recv,
     load_sem,
+    stage_sem,
 ):
     place, core = lax.axis_index("ctx"), lax.axis_index("fsdp")
     part, member = place // HALF, lax.rem(place, HALF)
@@ -540,10 +639,29 @@
     def half(part, size):
         return pl.ds(pl.multiple_of(part * size, 128), size)
 
+    stages = [
+        pltpu.make_async_copy(source, target, stage_sem.at[index])
+        for index, (source, target) in enumerate(
+            (
+                (home_hbm, home_ref),
+                (pair_hbm, pair_own),
+                (side_hbm, side_own),
+                (ffn_hbm, ffn_ref),
+                (mixed_hbm, mixed_ref),
+                (qkv_hbm, qkv_ref),
+                (part_hbm, part_ref),
+                (normed_hbm, normed_ref),
+            )
+        )
+    ]
     own_hidden = pltpu.make_async_copy(
         hidden_hbm.at[:, half(core, half_hidden)], hidden_own, load_sem.at[0]
     )
+    for stage in stages[:5]:
+        stage.start()
     own_hidden.start()
+    for stage in stages[5:]:
+        stage.start()
     middle_load = pltpu.make_async_copy(middle_hbm, tokens_out, load_sem.at[1])
     middle_load.start()
     greet([(lax.rem(place + step, RING), core) for step in range(1, RING)] + [partner])
@@ -576,13 +694,13 @@
     def pair_copy(turn_x, turn_y, depth):
         owner = lax.rem(z + depth, 4) * 4 + flip(y, turn_y) * 2 + flip(x, turn_x)
         return core_copy(
-            pair_own.at[owner], pair_far.at[owner], 6 + turn_x * 8 + turn_y * 4 + depth
+            pair_hbm.at[owner], pair_far.at[owner], 6 + turn_x * 8 + turn_y * 4 + depth
         )
 
     sides = [
-        core_copy(ffn_ref.at[:, half(1 - core, half_width)], ffn_far, 0),
-        core_copy(mixed_ref.at[half(1 - core, half_width), :], mixed_far, 1),
-        core_copy(side_own, side_far, 2),
+        core_copy(ffn_hbm.at[:, half(1 - core, half_width)], ffn_far, 0),
+        core_copy(mixed_hbm.at[half(1 - core, half_width), :], mixed_far, 1),
+        core_copy(side_hbm, side_far, 2),
         core_copy(hidden_hbm.at[:, half(1 - core, half_hidden)], hidden_far, 3),
     ]
     order = []
@@ -592,13 +710,27 @@
     for copy in sides:
         copy.start()
     pair_copy(*order[0]).start()
+    stages[0].wait()
     for step in range(1, HALF):
         cot_copy(step).start()
     for turn_x, turn_y, depth in order[1:]:
         pair_copy(turn_x, turn_y, depth).start()
-    normed_copy = core_copy(normed_ref.at[:, half(1 - core, half_width)], normed_far, 4)
+    normed_copy = core_copy(normed_hbm.at[:, half(1 - core, half_width)], normed_far, 4)
     normed_copy.start()
     cot_far[member] = home_ref[member]
+
+    def down_product(rows, split):
+        cols = slice(split[0] * 256, (split[0] + split[1]) * 256)
+        down = jnp.dot(side_own[0, rows, :], hidden_own[:, cols], preferred_element_type=F32)
+        return down + jnp.dot(side_far[0, rows, :], hidden_far[:, cols], preferred_element_type=F32)
+
+    def deep_compute(owner, count):
+        rows = pl.ds(pl.multiple_of(owner * narrow, 16), count * narrow)
+        return down_product(rows, DOWN_CHUNKS[2])
+
+    def deep_finish(window, value):
+        chunk = DOWN_CHUNKS[2][0] + window.start // narrow
+        down_out[:, chunk * 256 : chunk * 256 + 256] = value
 
     def compute(chain, owner):
         lanes = pl.ds(chain * 256, 256)
@@ -607,10 +739,8 @@
         both_pair += jnp.dot(pair_far[owner], ffn_far[:, lanes], preferred_element_type=F32)
         values = [(0, both_pair)]
         rows = pl.ds(pl.multiple_of(owner * narrow, 16), narrow)
-        begin, chunks = (0, 5) if chain == 0 else (5, 4)
-        cols = slice(begin * 256, (begin + chunks) * 256)
-        down = jnp.dot(side_own[0, rows, :], hidden_own[:, cols], preferred_element_type=F32)
-        down += jnp.dot(side_far[0, rows, :], hidden_far[:, cols], preferred_element_type=F32)
+        chunks = DOWN_CHUNKS[chain][1]
+        down = down_product(rows, DOWN_CHUNKS[chain])
         row = 2 * wide
         for chunk in range(chunks):
             values.append((row, down[:, chunk * 256 : chunk * 256 + 256]))
@@ -627,10 +757,10 @@
             up_out[:, lanes] = value[wide:]
             return
         chunk = (row - 2 * wide) // narrow
-        if chunk == 5 - chain:
+        if chunk == DOWN_CHUNKS[chain][1]:
             out_out[:, lanes] = value
         else:
-            chunk += 5 * chain
+            chunk += DOWN_CHUNKS[chain][0]
             down_out[:, chunk * 256 : chunk * 256 + 256] = value
 
     chains = (
@@ -638,6 +768,8 @@
         Spread(1, compute, sent_b, (came_b0, came_b1, came_b2), send_sems, recv_sems),
     )
     own_hidden.wait()
+    for stage in stages[1:5]:
+        stage.wait()
     for copy in sides:
         copy.wait_recv()
 
@@ -661,9 +793,16 @@
         for chain in chains:
             chain.stage_three(depth)
 
+    along = DeepSpread(
+        deep_compute, sent_c, (came_c0, came_c1, came_c2), deep_send, deep_recv
+    )
     near(2)
+    for slot in (2, 1, 3):
+        along.stage_one(slot)
     far(2)
     near(1)
+    for stage in stages[5:]:
+        stage.wait()
 
     def back_copy(step):
         return remote(
@@ -745,7 +884,14 @@
                 pair_acc[...] += step(False, i)
                 return carry
 
-            lax.fori_loop(j + 1, HALF + 1, one, 0)
+            def two(index, carry):
+                i = j + 1 + 2 * index
+                pair_acc[...] += step(False, i) + step(False, i + 1)
+                return carry
+
+            count = (HALF - j) // 2
+            lax.fori_loop(0, count, two, 0)
+            lax.fori_loop(j + 1 + 2 * count, HALF + 1, one, 0)
             first = lax.broadcasted_iota(jnp.int32, (BLOCK, 2 * HEAD_DIM), 1) < HEAD_DIM
             merged = jnp.where(first, pair_acc[0:BLOCK, :], pair_acc[BLOCK:, :]).T.astype(BF16)
 
@@ -953,6 +1099,7 @@
 
     gain_swap = core_copy(gain_own, gain_came, 22)
     gain_swap.start()
+    along.stage_two()
 
     def gain_copy(step):
         peer = (lax.rem(place + step, RING), core)
@@ -975,10 +1122,12 @@
     gain_all[place] = gain_own[...] + gain_came[...]
     lax.fori_loop(1, RING, gain_start, 0)
     lax.fori_loop(0, 4, tail_two, 0)
+    along.stage_three()
     onward(0)
     deeper(3)
     lax.fori_loop(1, 4, tail_three, 0)
     pair_copy(0, 0, 0).wait_recv()
+    along.close(deep_finish)
     for chain in chains:
         chain.close(finish)
     for chain in tails:
@@ -1005,7 +1154,7 @@
         copy.wait_send()
     for turn_x, turn_y, depth in order:
         pair_copy(turn_x, turn_y, depth).wait_send()
-    for chain in chains + tails:
+    for chain in chains + tails + (along,):
         chain.drain()
 
 
@@ -1025,8 +1174,8 @@
 
     dma = pltpu.SemaphoreType.DMA
     specs = [VMEM_SPEC] * (len(inputs) + len(loads))
-    specs[1] = HBM_SPEC
-    for index in range(len(inputs), len(specs)):
+    staged = (0, 2, 3, 4, 5, 6, 8, 11)
+    for index in (1, *staged, *range(len(inputs), len(specs))):
         specs[index] = HBM_SPEC
     return pl.pallas_call(
         back_kernel,
@@ -1041,7 +1190,8 @@
         ),
         in_specs=specs,
         out_specs=(VMEM_SPEC,) * 7,
-        scratch_shapes=[
+        scratch_shapes=[pltpu.VMEM(inputs[index].shape, BF16) for index in staged]
+        + [
             pltpu.VMEM(pair.shape, BF16),
             pltpu.VMEM(side.shape, BF16),
             pltpu.VMEM((rows, hidden_width // 2), BF16),
@@ -1060,14 +1210,16 @@
             pltpu.VMEM((4, width), F32),
             pltpu.VMEM((RING, 4, width), F32),
         ]
-        + buffers((2 * wide + 6 * narrow, 2 * wide + 5 * narrow))
+        + buffers([2 * wide + (split[1] + 1) * narrow for split in DOWN_CHUNKS[:2]])
+        + [pltpu.VMEM((*lead, DOWN_CHUNKS[2][1] * narrow, 256), BF16) for lead in ((3, 4), (3, 4), (2,), (1,))]
+        + [dma((6,)), dma((6,))]
         + buffers((total // RING, total // RING))
         + [dma((2, 15))] * 4
         + [dma((HALF,))] * 4
         + [dma((23,))] * 2
         + [dma((RING,))] * 2
         + [dma((HALF,))] * 2
-        + [dma((6,))],
+        + [dma((6,)), dma((8,))],
         compiler_params=pltpu.CompilerParams(
             collective_id=call_id, has_side_effects=True, vmem_limit_bytes=63 << 20
         ),
@@ -1075,26 +1227,18 @@
     )(*inputs, *loads)
 
 
-def head_table(positions, query_gain, key_gain):
+def head_frequencies(rows):
     half = HEAD_DIM // 2
-    inverse_freq = THETA ** (-(2.0 / HEAD_DIM) * jnp.arange(half, dtype=F32))
-    angles = inverse_freq[:, None] * positions.astype(F32)[None, :]
-    shape = (HEAD_DIM, positions.shape[0])
-    return jnp.concatenate(
-        [
-            jnp.cos(angles),
-            jnp.sin(angles),
-            jnp.broadcast_to(query_gain[:, None], shape),
-            jnp.broadcast_to(key_gain[:, None], shape),
-        ],
-        axis=0,
-    )
+    frequencies = THETA ** (-(2.0 / HEAD_DIM) * np.arange(half, dtype=np.float32))
+    return jnp.asarray(np.repeat(frequencies.astype(np.float32)[:, None], rows, axis=1))
 
 
 def front_kernel(
     gain_ref,
-    table_ref,
-    own_start_ref,
+    place_ref,
+    query_gain_ref,
+    key_gain_ref,
+    frequency_ref,
     tokens_hbm,
     w_query_hbm,
     w_key_hbm,
@@ -1110,6 +1254,7 @@
     mixed_out,
     inv_out,
     out_full,
+    table_ref,
     query_hbm,
     key_hbm,
     weights_hbm,
@@ -1118,10 +1263,13 @@
     down_far,
     home,
     key_nat,
+    totals,
+    accs,
     tokens_ref,
     query_out,
     key_out,
     weights_out,
+    own_start_ref,
     keep_sem,
     own_sem,
     send_sem,
@@ -1130,6 +1278,8 @@
     start_recv,
     mixed_send,
     mixed_recv,
+    kv_send,
+    kv_recv,
     extra_send,
     extra_recv,
     core_send,
@@ -1142,6 +1292,16 @@
     partner = (place, 1 - core)
     tokens_load = pltpu.make_async_copy(tokens_hbm, tokens_ref, keep_sem.at[0])
     tokens_load.start()
+    places = place * rows + lax.broadcasted_iota(jnp.int32, (1, rows), 1)
+    own_start_ref[...] = places - place_ref[...]
+    angles = frequency_ref[...] * place_ref[...].astype(F32)
+    half = HEAD_DIM // 2
+    table_ref[0:half, :] = jnp.cos(angles)
+    table_ref[half:HEAD_DIM, :] = jnp.sin(angles)
+    for index, source in enumerate((query_gain_ref, key_gain_ref)):
+        table_ref[(index + 1) * HEAD_DIM : (index + 2) * HEAD_DIM, :] = jnp.broadcast_to(
+            source[...], (rows, HEAD_DIM)
+        ).T
     greet([partner] + [(lax.rem(place + step, RING), core) for step in range(1, RING)])
 
     def remote(source, target, send, recv, peer):
@@ -1204,7 +1364,6 @@
 
     tokens_load.wait()
     lax.fori_loop(0, rows // 32, norm_rows, 0)
-    half = HEAD_DIM // 2
     cosine, sine = table_ref[0:half, :], table_ref[half:HEAD_DIM, :]
     query_gain = table_ref[HEAD_DIM : 2 * HEAD_DIM, :]
     key_gain = table_ref[2 * HEAD_DIM : 3 * HEAD_DIM, :]
@@ -1248,11 +1407,25 @@
 
     lax.fori_loop(0, KV_HEADS // 4, value_chunk, 0)
 
+    window = pl.ds(2 * HEAD_DIM, 2 * HEAD_DIM)
+
+    def kv_copy(step):
+        return remote(
+            home.at[lax.rem(member + step, HALF), window],
+            qkv_out.at[1 + member, window],
+            kv_send.at[step],
+            kv_recv.at[step],
+            mate(step),
+        )
+
+    def kv_start(step, nothing):
+        kv_copy(HALF - step).start()
+        return nothing
+
     def extra_copy(group):
-        window = pl.ds(2 * HEAD_DIM, 2 * HEAD_DIM)
         return remote(
-            home.at[group, window],
-            qkv_out.at[0, window],
+            home.at[group, window, pl.ds(rows - EDGE, EDGE)],
+            qkv_out.at[0, window, pl.ds(rows - EDGE, EDGE)],
             extra_send.at[group],
             extra_recv.at[group],
             (HALF + group, core),
@@ -1266,20 +1439,22 @@
     def _():
         lax.fori_loop(0, HALF, extra_start, 0)
 
+    lax.fori_loop(1, HALF, kv_start, 0)
     copies[2].wait_recv()
     near_copies[2].wait()
 
     def block_copy(step):
         peer = mate(step)
         return remote(
-            home.at[lax.rem(member + step, HALF)],
-            qkv_out.at[1 + member],
+            home.at[lax.rem(member + step, HALF), pl.ds(0, 2 * HEAD_DIM)],
+            qkv_out.at[1 + member, pl.ds(0, 2 * HEAD_DIM)],
             send_sem.at[step],
             recv_sem.at[step],
             peer,
         )
 
-    def query_chunk(index, nothing):
+    def query_chunk(turn, nothing):
+        index = lax.rem(member // 2 - turn + 4, 4)
         products = project(pl.multiple_of(2 * kv_width + index * 256, 256), 256)
         for offset in range(4):
             raw = products[offset * HEAD_DIM : (offset + 1) * HEAD_DIM]
@@ -1309,11 +1484,6 @@
     qkv_out[1 + member] = home[member]
     base = part * HALF - 1
 
-    @pl.when(part == 1)
-    def _():
-        extra_copy(member).wait_recv()
-        key_nat[0] = transposed(qkv_out[0, 2 * HEAD_DIM : 3 * HEAD_DIM, :])
-
     def mixed_copy(step):
         peer = mate(step)
         return remote(
@@ -1324,42 +1494,75 @@
             peer,
         )
 
-    def per_query(i, nothing):
+    def query_of(i):
+        query_t = jnp.concatenate(
+            [qkv_out[i, 0:HEAD_DIM, :], qkv_out[i, HEAD_DIM : 2 * HEAD_DIM, :]], axis=1
+        ) * jnp.asarray(HEAD_DIM**-0.5, BF16)
+        return query_t, jnp.concatenate([starts_out[i - 1]] * 2, axis=1)
+
+    def meet(query_t, keys, values, ok, carry):
+        total, acc = carry
+        probs = jnp.exp(jnp.dot(keys, query_t, preferred_element_type=F32))
+        probs = jnp.where(ok(lax.broadcasted_iota(jnp.int32, probs.shape, 0)), probs, 0.0)
+        total = total + jnp.sum(probs, axis=0, keepdims=True)
+        return total, acc + jnp.dot(values, probs.astype(BF16), preferred_element_type=F32)
+
+    def inner(i):
         @pl.when(i - 1 != member)
         def _():
             step = lax.rem(member - i + 1 + HALF, HALF)
+            start_copy(step).wait_recv()
+            kv_copy(step).wait_recv()
             block_copy(step).wait_recv()
-            start_copy(step).wait_recv()
 
         key_nat[i] = transposed(qkv_out[i, 2 * HEAD_DIM : 3 * HEAD_DIM, :])
-        query_t = jnp.concatenate(
-            [qkv_out[i, 0:HEAD_DIM, :], qkv_out[i, HEAD_DIM : 2 * HEAD_DIM, :]], axis=1
-        ) * jnp.asarray(HEAD_DIM**-0.5, BF16)
-        start = jnp.concatenate([starts_out[i - 1]] * 2, axis=1)
+        query_t, start = query_of(i)
         places = (base + i) * BLOCK + lax.broadcasted_iota(jnp.int32, (1, BLOCK), 1)
         query_place = jnp.concatenate([places] * 2, axis=1)
 
         def step(diagonal, j, carry):
-            total, acc = carry
-            scores = jnp.dot(key_nat[j], query_t, preferred_element_type=F32)
-            key_place = (base + j) * BLOCK + lax.broadcasted_iota(jnp.int32, scores.shape, 0)
-            ok = key_place >= start
-            if diagonal:
-                ok = ok & (key_place <= query_place)
-            probs = jnp.where(ok, jnp.exp(scores), 0.0)
-            total = total + jnp.sum(probs, axis=0, keepdims=True)
-            acc = acc + jnp.dot(
-                qkv_out[j, 3 * HEAD_DIM : 4 * HEAD_DIM, :],
-                probs.astype(BF16),
-                preferred_element_type=F32,
+            def ok(offset):
+                key_place = (base + j) * BLOCK + offset
+                if diagonal:
+                    return (key_place >= start) & (key_place <= query_place)
+                return key_place >= start
+
+            values = qkv_out[j, 3 * HEAD_DIM : 4 * HEAD_DIM, :]
+            return meet(query_t, key_nat[j], values, ok, carry)
+
+        carry = (jnp.zeros((1, 2 * BLOCK), F32), jnp.zeros((HEAD_DIM, 2 * BLOCK), F32))
+        pairs = (i - 1) // 2
+
+        def two(index, carry):
+            return step(False, 2 * index + 2, step(False, 2 * index + 1, carry))
+
+        carry = lax.fori_loop(0, pairs, two, carry)
+        carry = lax.fori_loop(2 * pairs + 1, i, functools.partial(step, False), carry)
+        totals[i - 1], accs[i - 1] = step(True, i, carry)
+
+    def outer(i):
+        @pl.when((part == 1) & (i == 1))
+        def _():
+            extra_copy(member).wait_recv()
+            qkv_out[0, 2 * HEAD_DIM :, 0 : rows - EDGE] = jnp.zeros(
+                (2 * HEAD_DIM, rows - EDGE), BF16
             )
-            return total, acc
-
-        carry = (jnp.zeros((1, 2 * BLOCK), F32), jnp.zeros((HEAD_DIM, 2 * BLOCK), F32))
-        carry = lax.fori_loop(1 - part, i, functools.partial(step, False), carry)
-        total, acc = step(True, i, carry)
-        inverse = 1.0 / total
-        low = (acc * inverse).astype(BF16)
+            key_nat[0] = transposed(qkv_out[0, 2 * HEAD_DIM : 3 * HEAD_DIM, :])
+
+        @pl.when(part == 1)
+        def _():
+            query_t, start = query_of(i)
+
+            def ok(offset):
+                return HALF * BLOCK - EDGE + offset >= start
+
+            values = qkv_out[0, 3 * HEAD_DIM : 4 * HEAD_DIM, rows - EDGE :]
+            totals[i - 1], accs[i - 1] = meet(
+                query_t, key_nat[0, rows - EDGE :, :], values, ok, (totals[i - 1], accs[i - 1])
+            )
+
+        inverse = 1.0 / totals[i - 1]
+        low = (accs[i - 1] * inverse).astype(BF16)
         part_out[i - 1, 0:HEAD_DIM, :] = low[:, :BLOCK]
         part_out[i - 1, HEAD_DIM:, :] = low[:, BLOCK:]
         inv_out[i - 1] = inverse
@@ -1368,13 +1571,24 @@
         def _():
             mixed_copy(lax.rem(i - 1 - member + HALF, HALF)).start()
 
+    def per_query(i, nothing):
+        @pl.when(i <= HALF)
+        def _():
+            inner(i)
+
+        @pl.when(i > lag)
+        def _():
+            outer(i - lag)
+
         return nothing
 
-    lax.fori_loop(1, HALF + 1, per_query, 0)
+    lag = 3
+    lax.fori_loop(1, HALF + lag + 1, per_query, 0)
     mixed_out[member] = part_out[member]
 
     def settle(step, nothing):
         block_copy(step).wait_send()
+        kv_copy(step).wait_send()
         start_copy(step).wait_send()
         mixed_copy(step).wait()
         return nothing
@@ -1414,6 +1628,7 @@
             jax.ShapeDtypeStruct((HALF, 2 * HEAD_DIM, rows), BF16),
             jax.ShapeDtypeStruct((HALF, 1, 2 * rows), F32),
             jax.ShapeDtypeStruct((width, width), BF16),
+            jax.ShapeDtypeStruct((3 * HEAD_DIM, rows), F32),
             jax.ShapeDtypeStruct(query_raw, F32),
             jax.ShapeDtypeStruct(key_raw, F32),
             jax.ShapeDtypeStruct((width, total), BF16),
@@ -1422,18 +1637,21 @@
             jax.ShapeDtypeStruct((hidden_width // 2, width), BF16),
         ),
         in_specs=[VMEM_SPEC] * len(inputs) + [HBM_SPEC] * len(loads),
-        out_specs=(VMEM_SPEC,) * 7 + (HBM_SPEC,) * 6,
+        out_specs=(VMEM_SPEC,) * 8 + (HBM_SPEC,) * 6,
         scratch_shapes=[
             pltpu.VMEM((HALF, 4 * HEAD_DIM, rows), BF16),
             pltpu.VMEM((HALF + 1, rows, HEAD_DIM), BF16),
+            pltpu.VMEM((HALF, 1, 2 * rows), F32),
+            pltpu.VMEM((HALF, HEAD_DIM, 2 * rows), F32),
             pltpu.VMEM((rows, width), BF16),
             pltpu.VMEM(query_raw, F32),
             pltpu.VMEM(key_raw, F32),
             pltpu.VMEM((width, total), BF16),
+            pltpu.VMEM((1, rows), jnp.int32),
             dma((4,)),
             dma((4,)),
         ]
-        + [dma((HALF,))] * 8
+        + [dma((HALF,))] * 10
         + [dma((7,))] * 2,
         compiler_params=pltpu.CompilerParams(
             collective_id=call_id, has_side_effects=True, vmem_limit_bytes=63 << 20
@@ -1688,11 +1906,7 @@
     w_down,
     d_output,
 ):
-    place = lax.axis_index("ctx")
     rows = tokens.shape[1]
-    pos_local = doc_pos[0]
-    own_starts = place * rows + jnp.arange(rows, dtype=jnp.int32) - pos_local
-    table = head_table(pos_local, query_gain, key_gain)
     (
         qkv,
         starts,
@@ -1701,6 +1915,7 @@
         mixed_home,
         inverse_total,
         o_full,
+        table,
         query_raw,
         key_raw,
         kvq_full,
@@ -1709,7 +1924,13 @@
         down_far,
     ) = front_call(
         1,
-        (attn_gain[None, :], table, own_starts[None, :]),
+        (
+            attn_gain[None, :],
+            doc_pos,
+            query_gain[None, :],
+            key_gain[None, :],
+            head_frequencies(rows),
+        ),
         (tokens[0], w_query, w_key, w_value, w_out, w_gate, w_up, w_down),
     )
     mixed_t = mixed_home.reshape(HEADS * HEAD_DIM, rows)

time: 274 us -> 249 us (0.909)
  Pallas kernels: 266 us -> 247 us
    pallas_call x1, Pallas kernels: 181 us -> 165 us  [back_call(): pl.pallas_call(back_kernel, out_shape=(jax.ShapeDtypeStruct((wide, width...]
    pallas_call x1, Pallas kernels: 50.7 us -> 47.4 us  [front_call(): pl.pallas_call(front_kernel, out_shape=(jax.ShapeDtypeStruct((HALF + 1, 4...]
where the time goes in v6:
time: 249 us; the launch traced here: 247 us
  Pallas kernels  247 us (99%)
    pallas_call x1, Pallas kernels, back_call(): pl.pallas_call(back_kernel, out_shape=(jax.ShapeDtypeStruct((wide, width...  165 us
    pallas_call x1, Pallas kernels, front_call(): pl.pallas_call(front_kernel, out_shape=(jax.ShapeDtypeStruct((HALF + 1, 4...  47.4 us
    pallas_call x1, Pallas kernels, ffn_call(): pl.pallas_call(ffn_kernel, grid_spec=pltpu.PrefetchScalarGridSpec(num_sca...  29.7 us

profile of v6, /device:TPU:15, one launch (start us, length us, event | category | flops | bytes accessed | tf_op | source)
XLA Modules:
  0.0 247.4 jit_solution(49517548979638735)
XLA Ops:
  0.7 47.4 %front_heads.1 = (bf16[9,256,256]{2,1,0:T(8,128)(2,1)}, s32[8,1,256]{2,1,0:T(1,128)}, bf16[256,1024]{1,0:T(8,128)(2,1)}, bf16[8,128,256]{2,1,0:T(8,128)(2,1)}, b...) custom-call(f32[1,1024]{1,0:T(1,128)} %bitcast.29, ...), custom_call_target="tpu_custom_call" | custom-call | tf_op jit(solution)/shard_map/front_heads/pallas_call | solution.py:1621
  48.0 29.7 %ffn_both_ways.1 = (bf16[16,576,256]{2,1,0:T(8,128)(2,1)}, bf16[256,4608]{1,0:T(8,128)(2,1)}, bf16[256,1024]{1,0:T(8,128)(2,1)}, bf16[256,1024]{1,0:T(8,128)(2,1...) custom-call(s32[1]{0:T(128)} %bitcast.core_ref, ...), custom_call_target="tpu_custom_call" | custom-call | tf_op jit(solution)/shard_map/ffn_both_ways/pallas_call | solution.py:1793
  77.8 165.1 %backward_spread.1 = (f32[288,512]{1,0:T(8,128)}, f32[288,512]{1,0:T(8,128)}, f32[64,2304]{1,0:T(8,128)}, f32[64,512]{1,0:T(8,128)}, f32[128,512]{1,0:T(8,128)}, /*index=5*/f32[256,1024]{1,0:T(8,128)}, f32[4,1024]{1,0:T(4,128)}) custom-call(bf16[16,576,256]{2,1,0:T(8,128)(2,1)} %get-tuple-element.60.pair_hbm, ...), custom_call_target="tpu_custom_call" | custom-call | tf_op jit(solution)/shard_map/backward_spread/pallas_call | solution.py:1180
  242.9 4.3 %settle_results.1 = (f32[256,1024]{1,0:T(8,128)}, f32[288,512]{1,0:T(8,128)}, f32[288,512]{1,0:T(8,128)}, f32[64,2304]{1,0:T(8,128)}, f32[64,512]{1,0:T(8,128)},...) custom-call(f32[256,1024]{1,0:T(8,128)} %get-tuple-element.76.refs_0, ...), custom_call_target="tpu_custom_call" | custom-call | tf_op jit(solution)/shard_map/settle_results/pallas_call | solution.py:1880

commit v7 on v6

--- a/solution.py
+++ b/solution.py
@@ -323,7 +323,8 @@
 RING = 16
 HALF = 8
 EDGE = 128
-DOWN_CHUNKS = ((0, 3), (3, 2), (5, 4))
+DOWN_CHUNKS = ((0, 3), (3, 3), (6, 3))
+EARLY = (2,)
 VMEM_SPEC = pl.BlockSpec(memory_space=pltpu.VMEM)
 HBM_SPEC = pl.BlockSpec(memory_space=pltpu.HBM)
 SMEM_SPEC = pl.BlockSpec(memory_space=pltpu.SMEM)
@@ -345,13 +346,21 @@
     return bit + turned - 2 * bit * turned
 
 
+def block_owner(chain, place, other, slot):
+    x, y, z = lax.rem(place, 2), lax.rem(place // 2, 2), place // 4
+    turned, depth = slot // 4, lax.rem(lax.rem(slot, 4) + z, 4)
+    first, second = flip((x, y)[chain], other), flip((y, x)[chain], turned)
+    return depth * 4 + (second * 2 + first if chain == 0 else first * 2 + second)
+
+
 class Spread:
-    def __init__(self, chain, compute, sent, came, send_sems, recv_sems):
+    def __init__(self, chain, compute, base, sent, came, hold, skip, send_sems, recv_sems):
         place, self.core = lax.axis_index("ctx"), lax.axis_index("fsdp")
         x, y, self.z = lax.rem(place, 2), lax.rem(place // 2, 2), place // 4
-        self.chain = chain
+        self.chain, self.base = chain, base
         self.first, self.second = (x, y) if chain == 0 else (y, x)
         self.compute, self.sent, self.came = compute, sent, came
+        self.hold, self.skip = hold, skip
         self.send_sems, self.recv_sems = send_sems, recv_sems
 
     def at(self, first, second, depth):
@@ -360,6 +369,9 @@
 
     def deep(self, depth):
         return lax.rem(self.z + depth, 4)
+
+    def owner(self, slot):
+        return self.at(self.first, flip(self.second, slot // 4), self.deep(lax.rem(slot, 4)))
 
     def copy(self, stage, slot):
         if stage == 0:
@@ -367,10 +379,10 @@
             source, target, sem = self.sent.at[slot], self.came[0].at[slot], slot
         elif stage == 1:
             peer = self.at(self.first, 1 - self.second, self.z)
-            source, target, sem = self.came[0].at[4 + slot], self.came[1].at[slot], 8 + slot
+            source, target, sem = self.hold.at[4 + slot - self.skip], self.came[1].at[slot], 8 + slot
         else:
             peer = self.at(self.first, self.second, self.deep(slot))
-            source, target, sem = self.came[0].at[slot], self.came[2].at[slot - 1], 11 + slot
+            source, target, sem = self.hold.at[slot - self.skip], self.came[2].at[slot - 1], 11 + slot
         return pltpu.make_async_remote_copy(
             src_ref=source,
             dst_ref=target,
@@ -383,28 +395,30 @@
     def stage_one(self, turned, depth):
         slot = turned * 4 + depth
         owner = self.at(1 - self.first, flip(self.second, turned), self.deep(depth))
-        for row, value in self.compute(self.chain, owner):
+        for row, value in self.compute(self.chain, owner, None):
+            row -= self.base
             self.sent[slot, row : row + value.shape[0], :] = value.astype(BF16)
         self.copy(0, slot).start()
 
+    def sums(self, slot):
+        for row, value in self.compute(self.chain, self.owner(slot), slot):
+            if row >= self.base:
+                low = row - self.base
+                value = value + self.came[0][slot, low : low + value.shape[0], :].astype(F32)
+            yield slice(row, row + value.shape[0]), value
+
     def stage_two(self, depth):
         self.copy(0, 4 + depth).wait_recv()
-        owner = self.at(self.first, 1 - self.second, self.deep(depth))
-        for row, value in self.compute(self.chain, owner):
-            window = slice(row, row + value.shape[0])
-            value = value + self.came[0][4 + depth, window, :].astype(F32)
-            self.came[0][4 + depth, window, :] = value.astype(BF16)
+        for window, value in self.sums(4 + depth):
+            self.hold[4 + depth - self.skip, window, :] = value.astype(BF16)
         self.copy(1, depth).start()
 
     def stage_three(self, depth):
         self.copy(0, depth).wait_recv()
         self.copy(1, depth).wait_recv()
-        owner = self.at(self.first, self.second, self.deep(depth))
-        for row, value in self.compute(self.chain, owner):
-            window = slice(row, row + value.shape[0])
-            value = value + self.came[0][depth, window, :].astype(F32)
+        for window, value in self.sums(depth):
             value = value + self.came[1][depth, window, :].astype(F32)
-            self.came[0][depth, window, :] = value.astype(BF16)
+            self.hold[depth - self.skip, window, :] = value.astype(BF16)
         self.copy(2, depth).start()
 
     def close(self, finish):
@@ -412,14 +426,11 @@
         self.copy(1, 0).wait_recv()
         for depth in range(1, 4):
             self.copy(2, depth).wait_recv()
-        owner = self.at(self.first, self.second, self.z)
-        for row, value in self.compute(self.chain, owner):
-            window = slice(row, row + value.shape[0])
-            value = value + self.came[0][0, window, :].astype(F32)
+        for window, value in self.sums(0):
             value = value + self.came[1][0, window, :].astype(F32)
             for depth in range(3):
                 value = value + self.came[2][depth, window, :].astype(F32)
-            finish(self.chain, row, value)
+            finish(self.chain, window.start, value)
 
     def drain(self):
         for slot in range(8):
@@ -553,6 +564,8 @@
     key_hbm,
     weights_hbm,
     middle_hbm,
+    swap_hbm,
+    near_hbm,
     gate_out,
     up_out,
     down_out,
@@ -560,7 +573,6 @@
     grads_out,
     tokens_out,
     gains_out,
-    pair_own,
     side_own,
     ffn_ref,
     mixed_ref,
@@ -568,7 +580,8 @@
     qkv_ref,
     part_ref,
     normed_ref,
-    pair_far,
+    rows_of,
+    ffn_near,
     side_far,
     hidden_own,
     hidden_far,
@@ -587,10 +600,12 @@
     gain_all,
     sent_a,
     came_a0,
+    hold_a,
     came_a1,
     came_a2,
     sent_b,
     came_b0,
+    hold_b,
     came_b1,
     came_b2,
     sent_c,
@@ -623,12 +638,20 @@
     extra_recv,
     load_sem,
     stage_sem,
+    rows_sem,
+    mate_send,
+    mate_recv,
+    relay_send,
+    relay_recv,
+    swap_send,
+    swap_recv,
+    near_sem,
 ):
     place, core = lax.axis_index("ctx"), lax.axis_index("fsdp")
     part, member = place // HALF, lax.rem(place, HALF)
     base = part * HALF - 1
     x, y, z = lax.rem(place, 2), lax.rem(place // 2, 2), place // 4
-    wide = pair_own.shape[1] // 2
+    wide = rows_of.shape[3]
     narrow = side_own.shape[1] // RING
     half_hidden = hidden_far.shape[1]
     half_width = ffn_far.shape[1]
@@ -644,7 +667,6 @@
         for index, (source, target) in enumerate(
             (
                 (home_hbm, home_ref),
-                (pair_hbm, pair_own),
                 (side_hbm, side_own),
                 (ffn_hbm, ffn_ref),
                 (mixed_hbm, mixed_ref),
@@ -657,13 +679,14 @@
     own_hidden = pltpu.make_async_copy(
         hidden_hbm.at[:, half(core, half_hidden)], hidden_own, load_sem.at[0]
     )
-    for stage in stages[:5]:
+    for stage in stages[:4]:
         stage.start()
     own_hidden.start()
-    for stage in stages[5:]:
+    for stage in stages[4:]:
         stage.start()
     middle_load = pltpu.make_async_copy(middle_hbm, tokens_out, load_sem.at[1])
     middle_load.start()
+    near = (place + 1 - 2 * x, place + 2 - 4 * y)
     greet([(lax.rem(place + step, RING), core) for step in range(1, RING)] + [partner])
 
     def remote(source, target, send, recv, peer):
@@ -691,30 +714,89 @@
     def core_copy(source, target, sem):
         return remote(source, target, core_send.at[sem], core_recv.at[sem], partner)
 
-    def pair_copy(turn_x, turn_y, depth):
-        owner = lax.rem(z + depth, 4) * 4 + flip(y, turn_y) * 2 + flip(x, turn_x)
-        return core_copy(
-            pair_hbm.at[owner], pair_far.at[owner], 6 + turn_x * 8 + turn_y * 4 + depth
-        )
-
+    def back_rows(chain, owner):
+        return pair_hbm.at[owner, pl.ds(chain * wide, wide)]
+
+    def owner_of(chain, slot):
+        return block_owner(chain, place, 0, slot)
+
+    def own_loads(chain, slot):
+        loads = [
+            pltpu.make_async_copy(
+                back_rows(chain, owner_of(chain, slot)),
+                rows_of.at[0, chain, slot],
+                rows_sem.at[0, chain, slot],
+            )
+        ]
+        if slot % 4 in EARLY:
+            loads.append(
+                pltpu.make_async_copy(
+                    swap_hbm.at[chain, slot],
+                    rows_of.at[2, chain, slot],
+                    rows_sem.at[1, chain, slot],
+                )
+            )
+        return loads
+
+    def swap_copy(chain, slot):
+        return remote(
+            back_rows(chain, block_owner(chain, place, 1, slot)),
+            rows_of.at[2, chain, slot],
+            swap_send.at[chain, slot],
+            swap_recv.at[chain, slot],
+            (near[chain], core),
+        )
+
+    def swap(depth):
+        for slot in (4 + depth, depth):
+            for chain in range(2):
+                swap_copy(chain, slot).start()
+
+    def relay(depth):
+        for slot in (4 + depth, depth):
+            for chain in range(2):
+                swap_copy(chain, slot).wait_recv()
+                relay_copy(chain, slot).start()
+
+    def mate_copy(chain, slot):
+        return remote(
+            back_rows(chain, owner_of(chain, slot)),
+            rows_of.at[1, chain, slot],
+            mate_send.at[chain, slot],
+            mate_recv.at[chain, slot],
+            partner,
+        )
+
+    def relay_copy(chain, slot):
+        return remote(
+            swap_hbm.at[chain, slot] if slot % 4 in EARLY else rows_of.at[2, chain, slot],
+            rows_of.at[3, chain, slot],
+            relay_send.at[chain, slot],
+            relay_recv.at[chain, slot],
+            partner,
+        )
+
+    near_load = pltpu.make_async_copy(near_hbm, ffn_near, near_sem)
     sides = [
         core_copy(ffn_hbm.at[:, half(1 - core, half_width)], ffn_far, 0),
         core_copy(mixed_hbm.at[half(1 - core, half_width), :], mixed_far, 1),
         core_copy(side_hbm, side_far, 2),
         core_copy(hidden_hbm.at[:, half(1 - core, half_hidden)], hidden_far, 3),
     ]
-    order = []
-    for depth in (2, 1, 3, 0):
-        order += [(1, 1, depth), (1, 0, depth), (0, 1, depth)]
-    order += [(0, 0, depth) for depth in (2, 1, 3, 0)]
-    for copy in sides:
-        copy.start()
-    pair_copy(*order[0]).start()
     stages[0].wait()
     for step in range(1, HALF):
         cot_copy(step).start()
-    for turn_x, turn_y, depth in order[1:]:
-        pair_copy(turn_x, turn_y, depth).start()
+    for copy in sides:
+        copy.start()
+    near_load.start()
+    for depth in (2, 1, 3, 0):
+        for slot in (4 + depth, depth):
+            for chain in range(2):
+                for load in own_loads(chain, slot):
+                    load.start()
+                mate_copy(chain, slot).start()
+                if depth in EARLY:
+                    relay_copy(chain, slot).start()
     normed_copy = core_copy(normed_hbm.at[:, half(1 - core, half_width)], normed_far, 4)
     normed_copy.start()
     cot_far[member] = home_ref[member]
@@ -732,13 +814,30 @@
         chunk = DOWN_CHUNKS[2][0] + window.start // narrow
         down_out[:, chunk * 256 : chunk * 256 + 256] = value
 
-    def compute(chain, owner):
+    def compute(chain, owner, slot):
         lanes = pl.ds(chain * 256, 256)
         own_lanes = pl.ds(pl.multiple_of(core * half_width + chain * 256, 128), 256)
-        both_pair = jnp.dot(pair_own[owner], ffn_ref[:, own_lanes], preferred_element_type=F32)
-        both_pair += jnp.dot(pair_far[owner], ffn_far[:, lanes], preferred_element_type=F32)
-        values = [(0, both_pair)]
         rows = pl.ds(pl.multiple_of(owner * narrow, 16), narrow)
+        values = []
+        if slot is not None:
+            for load in own_loads(chain, slot):
+                load.wait()
+            mate_copy(chain, slot).wait_recv()
+            relay_copy(chain, slot).wait_recv()
+            wide_sum = jnp.dot(
+                rows_of[0, chain, slot],
+                ffn_ref[:, half(core, half_width)],
+                preferred_element_type=F32,
+            )
+            for source, columns in (
+                (1, ffn_far[...]),
+                (2, ffn_near[chain, 0]),
+                (3, ffn_near[chain, 1]),
+            ):
+                wide_sum += jnp.dot(
+                    rows_of[source, chain, slot], columns, preferred_element_type=F32
+                )
+            values += [(0, wide_sum[:, :256]), (wide, wide_sum[:, 256:])]
         chunks = DOWN_CHUNKS[chain][1]
         down = down_product(rows, DOWN_CHUNKS[chain])
         row = 2 * wide
@@ -752,9 +851,9 @@
 
     def finish(chain, row, value):
         lanes = slice(chain * 256, chain * 256 + 256)
-        if row == 0:
-            gate_out[:, lanes] = value[:wide]
-            up_out[:, lanes] = value[wide:]
+        if row < 2 * wide:
+            target, low = (gate_out, up_out)[chain], row // wide * 256
+            target[:, low : low + 256] = value
             return
         chunk = (row - 2 * wide) // narrow
         if chunk == DOWN_CHUNKS[chain][1]:
@@ -764,23 +863,40 @@
             down_out[:, chunk * 256 : chunk * 256 + 256] = value
 
     chains = (
-        Spread(0, compute, sent_a, (came_a0, came_a1, came_a2), send_sems, recv_sems),
-        Spread(1, compute, sent_b, (came_b0, came_b1, came_b2), send_sems, recv_sems),
+        Spread(
+            0,
+            compute,
+            2 * wide,
+            sent_a,
+            (came_a0, came_a1, came_a2),
+            hold_a,
+            1,
+            send_sems,
+            recv_sems,
+        ),
+        Spread(
+            1,
+            compute,
+            2 * wide,
+            sent_b,
+            (came_b0, came_b1, came_b2),
+            hold_b,
+            1,
+            send_sems,
+            recv_sems,
+        ),
     )
     own_hidden.wait()
-    for stage in stages[1:5]:
+    for stage in stages[1:4]:
         stage.wait()
     for copy in sides:
         copy.wait_recv()
 
-    def near(depth):
-        pair_copy(1, 1, depth).wait_recv()
+    def near_side(depth):
         for chain in chains:
             chain.stage_one(1, depth)
 
-    def far(depth):
-        pair_copy(1, 0, depth).wait_recv()
-        pair_copy(0, 1, depth).wait_recv()
+    def far_side(depth):
         for chain in chains:
             chain.stage_one(0, depth)
 
@@ -789,19 +905,20 @@
             chain.stage_two(depth)
 
     def deeper(depth):
-        pair_copy(0, 0, depth).wait_recv()
         for chain in chains:
             chain.stage_three(depth)
 
     along = DeepSpread(
         deep_compute, sent_c, (came_c0, came_c1, came_c2), deep_send, deep_recv
     )
-    near(2)
+    near_side(2)
     for slot in (2, 1, 3):
         along.stage_one(slot)
-    far(2)
-    near(1)
-    for stage in stages[5:]:
+    far_side(2)
+    near_side(1)
+    swap(1)
+    near_load.wait()
+    for stage in stages[4:]:
         stage.wait()
 
     def back_copy(step):
@@ -911,14 +1028,26 @@
             def _():
                 back_copy(lax.rem(j - 1 - member + HALF, HALF)).start()
 
+            @pl.when(j == 1)
+            def _():
+                onward(2)
+                far_side(1)
+                swap(3)
+
+            @pl.when(j == 2)
+            def _():
+                near_side(3)
+                far_side(3)
+                swap(0)
+
             @pl.when(j == 4)
             def _():
-                onward(2)
-                far(1)
-
-            @pl.when(j == HALF)
+                relay(1)
+                onward(1)
+
+            @pl.when(j == 6)
             def _():
-                near(3)
+                deeper(2)
 
             return nothing
 
@@ -940,7 +1069,7 @@
 
     turned_copy = core_copy(turned_own, turned_far, 5)
 
-    def tail_compute(chain, owner):
+    def tail_compute(chain, owner, slot):
         lanes = slice(chain * 256, chain * 256 + 256)
         own_lanes = pl.ds(pl.multiple_of(core * half_width + chain * 256, 128), 256)
         values, row = [], 0
@@ -962,16 +1091,22 @@
         Spread(
             0,
             tail_compute,
+            0,
             tail_sent_a,
             (tail_came_a0, tail_came_a1, tail_came_a2),
+            tail_came_a0,
+            0,
             tail_send,
             tail_recv,
         ),
         Spread(
             1,
             tail_compute,
+            0,
             tail_sent_b,
             (tail_came_b0, tail_came_b1, tail_came_b2),
+            tail_came_b0,
+            0,
             tail_send,
             tail_recv,
         ),
@@ -1015,8 +1150,12 @@
             turned_own[head_rows(pairs + pair), :] = upstream[HEAD_DIM:].astype(BF16)
             return total + terms
 
-        onward(1)
-        far(3)
+
+        relay(3)
+        near_side(0)
+        deeper(1)
+        far_side(0)
+        onward(3)
 
         def arrive(step, nothing):
             back_copy(step).wait_recv()
@@ -1044,7 +1183,6 @@
         turned_copy.start()
         for row in range(0, turned_own.shape[0], 128):
             natural[:, row : row + 128] = turned_own[row : row + 128, :].astype(F32).T.astype(BF16)
-        deeper(2)
         normed_copy.wait_recv()
         turned_copy.wait_recv()
 
@@ -1054,7 +1192,9 @@
             return carry
 
         lax.fori_loop(0, 8, tail_one, 0)
-        near(0)
+        relay(0)
+        onward(0)
+        deeper(3)
         summed[...] = dot_dims(natural[...], weights_ref[...], 1, 1)
         middle_load.wait()
 
@@ -1115,18 +1255,12 @@
         gain_copy(step).wait()
         return carry
 
-    onward(3)
-    deeper(1)
-    far(0)
     gain_swap.wait()
     gain_all[place] = gain_own[...] + gain_came[...]
     lax.fori_loop(1, RING, gain_start, 0)
     lax.fori_loop(0, 4, tail_two, 0)
     along.stage_three()
-    onward(0)
-    deeper(3)
     lax.fori_loop(1, 4, tail_three, 0)
-    pair_copy(0, 0, 0).wait_recv()
     along.close(deep_finish)
     for chain in chains:
         chain.close(finish)
@@ -1152,14 +1286,18 @@
 
     for copy in sides + [normed_copy, turned_copy]:
         copy.wait_send()
-    for turn_x, turn_y, depth in order:
-        pair_copy(turn_x, turn_y, depth).wait_send()
+    for slot in range(8):
+        for chain in range(2):
+            mate_copy(chain, slot).wait_send()
+            relay_copy(chain, slot).wait_send()
+            if slot % 4 not in EARLY:
+                swap_copy(chain, slot).wait_send()
     for chain in chains + tails + (along,):
         chain.drain()
 
 
 def back_call(call_id, inputs, loads):
-    pair, hidden, side, ffn_low = inputs[:4]
+    hidden, side, ffn_low = inputs[1:4]
     rows, hidden_width = hidden.shape
     width = ffn_low.shape[1]
     wide, narrow = hidden_width // RING, width // RING
@@ -1172,10 +1310,15 @@
             for slots in (8, 8, 4, 3)
         ]
 
+    def chain_buffers(split):
+        rest = (split[1] + 1) * narrow
+        shapes = ((8, rest), (8, rest), (7, 2 * wide + rest), (4, 2 * wide + rest), (3, 2 * wide + rest))
+        return [pltpu.VMEM((*shape, 256), BF16) for shape in shapes]
+
     dma = pltpu.SemaphoreType.DMA
     specs = [VMEM_SPEC] * (len(inputs) + len(loads))
-    staged = (0, 2, 3, 4, 5, 6, 8, 11)
-    for index in (1, *staged, *range(len(inputs), len(specs))):
+    staged = (2, 3, 4, 5, 6, 8, 11)
+    for index in (0, 1, *staged, *range(len(inputs), len(specs))):
         specs[index] = HBM_SPEC
     return pl.pallas_call(
         back_kernel,
@@ -1192,7 +1335,8 @@
         out_specs=(VMEM_SPEC,) * 7,
         scratch_shapes=[pltpu.VMEM(inputs[index].shape, BF16) for index in staged]
         + [
-            pltpu.VMEM(pair.shape, BF16),
+            pltpu.VMEM((4, 2, 8, wide, rows), BF16),
+            pltpu.VMEM((2, 2, rows, width // 2), BF16),
             pltpu.VMEM(side.shape, BF16),
             pltpu.VMEM((rows, hidden_width // 2), BF16),
             pltpu.VMEM((rows, hidden_width // 2), BF16),
@@ -1210,7 +1354,8 @@
             pltpu.VMEM((4, width), F32),
             pltpu.VMEM((RING, 4, width), F32),
         ]
-        + buffers([2 * wide + (split[1] + 1) * narrow for split in DOWN_CHUNKS[:2]])
+        + chain_buffers(DOWN_CHUNKS[0])
+        + chain_buffers(DOWN_CHUNKS[1])
         + [pltpu.VMEM((*lead, DOWN_CHUNKS[2][1] * narrow, 256), BF16) for lead in ((3, 4), (3, 4), (2,), (1,))]
         + [dma((6,)), dma((6,))]
         + buffers((total // RING, total // RING))
@@ -1219,7 +1364,10 @@
         + [dma((23,))] * 2
         + [dma((RING,))] * 2
         + [dma((HALF,))] * 2
-        + [dma((6,)), dma((8,))],
+        + [dma((6,)), dma((7,))]
+        + [dma((2, 2, 8))]
+        + [dma((2, 8))] * 6
+        + [dma],
         compiler_params=pltpu.CompilerParams(
             collective_id=call_id, has_side_effects=True, vmem_limit_bytes=63 << 20
         ),
@@ -1661,7 +1809,6 @@
 
 
 def ffn_kernel(
-    core_ref,
     tokens_ref,
     mixed_ref,
     w_out_ref,
@@ -1681,12 +1828,56 @@
     mixed_back_out,
     grad_middle_out,
     terms_out,
+    swap_out,
+    near_out,
     middle,
     result,
     upstream,
     middle_low,
+    swap_send,
+    swap_recv,
+    near_send,
+    near_recv,
 ):
     step = pl.program_id(0)
+    place, core = lax.axis_index("ctx"), lax.axis_index("fsdp")
+    x, y, z = lax.rem(place, 2), lax.rem(place // 2, 2), place // 4
+    near = (place + 1 - 2 * x, place + 2 - 4 * y)
+    wide = pair_out.shape[1] // 2
+    half_width = gate_own.shape[0]
+    strip_owners = pair_out.shape[0] // 4
+    plane = lax.rem(z + 6 - step, 4)
+
+    def remote(source, target, send, recv, peer):
+        return pltpu.make_async_remote_copy(
+            src_ref=source,
+            dst_ref=target,
+            send_sem=send,
+            recv_sem=recv,
+            device_id=peer,
+            device_id_type=MESH,
+        )
+
+    def near_copy(chain, other):
+        target = core if other == 0 else 1 - core
+        lanes = pl.ds(pl.multiple_of(target * half_width, 128), half_width)
+        return remote(
+            ffn_out.at[:, lanes],
+            near_out.at[chain, other],
+            near_send.at[chain, other],
+            near_recv.at[chain, other],
+            (near[chain], target),
+        )
+
+    def swap_copy(chain, slot):
+        return remote(
+            pair_out.at[block_owner(chain, place, 1, slot), pl.ds(chain * wide, wide)],
+            swap_out.at[chain, slot],
+            swap_send.at[chain, slot],
+            swap_recv.at[chain, slot],
+            (near[chain], core),
+        )
+
     rows, width = tokens_ref.shape
     strip = 32
 
@@ -1711,12 +1902,15 @@
             return carry
 
         lax.fori_loop(0, rows // strip, strips(norm), 0)
+        greet([(peer, target) for peer in near for target in (core, 1 - core)])
+        for chain in range(2):
+            for other in range(2):
+                near_copy(chain, other).start()
         upstream[...] = jnp.zeros(upstream.shape, F32)
         side_out[0] = cot_ref[...].astype(F32).T.astype(BF16)
 
-    depth = gate_own.shape[0]
-    own = pl.ds(pl.multiple_of(core_ref[0] * depth, 128), depth)
-    far = pl.ds(pl.multiple_of((1 - core_ref[0]) * depth, 128), depth)
+    own = pl.ds(pl.multiple_of(core * half_width, 128), half_width)
+    far = pl.ds(pl.multiple_of((1 - core) * half_width, 128), half_width)
 
     def strip_of_hidden(down_ref):
         def ahead(near_ref, far_ref):
@@ -1738,17 +1932,25 @@
             upstream[:, window] += dot_dims(gate_back, gate_ref[...], 1, 1) + dot_dims(
                 up_back, up_ref[...], 1, 1
             )
-        wide = pair_out.shape[1] // 2
         for base, back in ((0, gate_back), (wide, up_back)):
             turned = back.astype(F32).T.astype(BF16)
-            for owner in range(pair_out.shape[0]):
-                pair_out[owner, base : base + wide, :] = turned[owner * wide : (owner + 1) * wide]
-
-    @pl.when(step < 2)
+            for index in range(strip_owners):
+                pair_out[plane * strip_owners + index, base : base + wide, :] = turned[
+                    index * wide : (index + 1) * wide
+                ]
+
+        @pl.when(step < len(EARLY))
+        def _():
+            for turned_side in range(2):
+                for chain in range(2):
+                    swap_copy(chain, turned_side * 4 + 2 - step).start()
+
+
+    @pl.when(plane // 2 == core)
     def _():
         strip_of_hidden(down_own)
 
-    @pl.when(step >= 2)
+    @pl.when(plane // 2 != core)
     def _():
         strip_of_hidden(down_far)
 
@@ -1773,27 +1975,33 @@
         )
         mixed_back_out[...] = dot_dims(w_out_ref[...], middle_low[...], 1, 1).astype(BF16)
         side_out[1] = middle_low[...].astype(F32).T.astype(BF16)
-
-
-def ffn_call(core, tokens, mixed_t, w_out, gain, cot, gate, up, down):
+        for chain in range(2):
+            for other in range(2):
+                near_copy(chain, other).wait()
+
+        for depth in EARLY:
+            for slot in (4 + depth, depth):
+                for chain in range(2):
+                    swap_copy(chain, slot).wait()
+
+
+def ffn_call(call_id, tokens, mixed_t, w_out, gain, cot, gate, up, down):
     rows, width = tokens.shape
     half_depth, hidden_width = gate[0].shape
     steps = 4
     chunk = hidden_width // steps
-    owners = RING // steps
     wide = hidden_width // RING
 
     def whole(*shape):
-        return pl.BlockSpec(shape, lambda i, core_ref: (0,) * len(shape))
-
-    def turn(i, core_ref):
-        return lax.rem(i + 2 * core_ref[0], steps)
-
-    columns = pl.BlockSpec((half_depth, chunk), lambda i, core_ref: (0, turn(i, core_ref)))
+        return pl.BlockSpec(shape, lambda i: (0,) * len(shape))
+
+    def turn(i):
+        return lax.rem(lax.axis_index("ctx") // 4 + 6 - i, steps)
+
+    columns = pl.BlockSpec((half_depth, chunk), lambda i: (0, turn(i)))
     return pl.pallas_call(
         ffn_kernel,
-        grid_spec=pltpu.PrefetchScalarGridSpec(
-            num_scalar_prefetch=1,
+        grid_spec=pl.GridSpec(
             grid=(steps,),
             in_specs=[
                 whole(rows, width),
@@ -1805,23 +2013,25 @@
                 columns,
                 columns,
                 columns,
-                pl.BlockSpec((chunk, width), lambda i, core_ref: (jnp.minimum(i, 1), 0)),
-                pl.BlockSpec((chunk, width), lambda i, core_ref: (jnp.maximum(i - 2, 0), 0)),
+                pl.BlockSpec((chunk, width), lambda i: (lax.rem(turn(i), 2), 0)),
+                pl.BlockSpec((chunk, width), lambda i: (lax.rem(turn(i), 2), 0)),
             ],
             out_specs=(
-                pl.BlockSpec(
-                    (owners, 2 * wide, rows), lambda i, core_ref: (turn(i, core_ref), 0, 0)
-                ),
-                pl.BlockSpec((rows, chunk), lambda i, core_ref: (0, turn(i, core_ref))),
+                whole(RING, 2 * wide, rows),
+                pl.BlockSpec((rows, chunk), lambda i: (0, turn(i))),
                 whole(rows, width),
                 whole(rows, width),
                 whole(2, width, rows),
                 whole(width, rows),
                 whole(rows, width),
                 whole(1, width),
+                HBM_SPEC,
+                HBM_SPEC,
             ),
             scratch_shapes=[pltpu.VMEM((rows, width), F32)] * 3
-            + [pltpu.VMEM((rows, width), BF16)],
+            + [pltpu.VMEM((rows, width), BF16)]
+            + [pltpu.SemaphoreType.DMA((2, 8))] * 2
+            + [pltpu.SemaphoreType.DMA((2, 2))] * 2,
         ),
         out_shape=(
             jax.ShapeDtypeStruct((RING, 2 * wide, rows), BF16),
@@ -1832,10 +2042,14 @@
             jax.ShapeDtypeStruct((width, rows), BF16),
             jax.ShapeDtypeStruct((rows, width), F32),
             jax.ShapeDtypeStruct((1, width), F32),
+            jax.ShapeDtypeStruct((2, 8, wide, rows), BF16),
+            jax.ShapeDtypeStruct((2, 2, rows, half_depth), BF16),
         ),
-        compiler_params=pltpu.CompilerParams(vmem_limit_bytes=63 << 20),
+        compiler_params=pltpu.CompilerParams(
+            collective_id=call_id, has_side_effects=True, vmem_limit_bytes=63 << 20
+        ),
         name="ffn_both_ways",
-    )(core, tokens, mixed_t, w_out, gain, cot, *gate, *up, *down)
+    )(tokens, mixed_t, w_out, gain, cot, *gate, *up, *down)
 
 
 def settle_kernel(*refs):
@@ -1944,8 +2158,10 @@
         grad_mixed,
         grad_middle,
         ffn_terms,
+        swapped,
+        ffn_near,
     ) = ffn_call(
-        lax.axis_index("fsdp").astype(jnp.int32)[None],
+        2,
         tokens[0],
         mixed_t,
         o_full,
@@ -1973,7 +2189,7 @@
             attn_gain[None, :],
             ffn_terms,
         ),
-        (tokens[0], query_raw, key_raw, kvq_full, grad_middle),
+        (tokens[0], query_raw, key_raw, kvq_full, grad_middle, swapped, ffn_near),
     )
     d_tokens, gate, up, down, out, query, key, value, attn, ffn, query_gains, key_gains = (
         settle_call(d_tokens, gate_t, up_t, down_t, out_t, qkv_grads, gain_totals)

time: 249 us -> 234 us (0.940)
  Pallas kernels: 247 us -> 230 us
    pallas_call x1, Pallas kernels: 165 us -> 146 us  [back_call(): pl.pallas_call(back_kernel, out_shape=(jax.ShapeDtypeStruct((wide, width...]
    pallas_call x1, Pallas kernels: 29.7 us -> 32.9 us  [ffn_call(): pl.pallas_call(ffn_kernel, grid_spec=pl.GridSpec(grid=(steps,), in_specs=...]
where the time goes in v7:
time: 234 us; the launch traced here: 232 us
  Pallas kernels  230 us (98%)
    pallas_call x1, Pallas kernels, back_call(): pl.pallas_call(back_kernel, out_shape=(jax.ShapeDtypeStruct((wide, width...  146 us
    pallas_call x1, Pallas kernels, front_call(): pl.pallas_call(front_kernel, out_shape=(jax.ShapeDtypeStruct((HALF + 1, 4...  47.4 us
    pallas_call x1, Pallas kernels, ffn_call(): pl.pallas_call(ffn_kernel, grid_spec=pl.GridSpec(grid=(steps,), in_specs=...  32.9 us

profile of v7, /device:TPU:15, one launch (start us, length us, event | category | flops | bytes accessed | tf_op | source)
XLA Modules:
  0.0 231.9 jit_solution(10923528079290217108)
XLA Ops:
  0.6 47.4 %front_heads.1 = (bf16[9,256,256]{2,1,0:T(8,128)(2,1)}, s32[8,1,256]{2,1,0:T(1,128)}, bf16[256,1024]{1,0:T(8,128)(2,1)}, bf16[8,128,256]{2,1,0:T(8,128)(2,1)}, b...) custom-call(f32[1,1024]{1,0:T(1,128)} %bitcast.29, ...), custom_call_target="tpu_custom_call" | custom-call | tf_op jit(solution)/shard_map/front_heads/pallas_call | solution.py:1769
  48.1 32.9 %ffn_both_ways.1 = (bf16[16,576,256]{2,1,0:T(8,128)(2,1)}, bf16[256,4608]{1,0:T(8,128)(2,1)}, bf16[256,1024]{1,0:T(8,128)(2,1)}, bf16[256,1024]{1,0:T(8,128)(2,1...) custom-call(bf16[256,1024]{1,0:T(8,128)(2,1)} %bitcast.22, ...), custom_call_target="tpu_custom_call" | custom-call | tf_op jit(solution)/shard_map/ffn_both_ways/pallas_call | solution.py:2002
  81.0 0.0 copy-start
  81.0 145.7 %backward_spread.1 = (f32[288,512]{1,0:T(8,128)}, f32[288,512]{1,0:T(8,128)}, f32[64,2304]{1,0:T(8,128)}, f32[64,512]{1,0:T(8,128)}, f32[128,512]{1,0:T(8,128)}, /*index=5*/f32[256,1024]{1,0:T(8,128)}, f32[4,1024]{1,0:T(4,128)}) custom-call(bf16[16,576,256]{2,1,0:T(8,128)(2,1)} %get-tuple-element.62.pair_hbm, ...), custom_call_target="tpu_custom_call" | custom-call | tf_op jit(solution)/shard_map/backward_spread/pallas_call | solution.py:1323
  226.7 4.3 %settle_results.1 = (f32[256,1024]{1,0:T(8,128)}, f32[288,512]{1,0:T(8,128)}, f32[288,512]{1,0:T(8,128)}, f32[64,2304]{1,0:T(8,128)}, f32[64,512]{1,0:T(8,128)},...) custom-call(f32[256,1024]{1,0:T(8,128)} %get-tuple-element.80.refs_0, ...), custom_call_target="tpu_custom_call" | custom-call | tf_op jit(solution)/shard_map/settle_results/pallas_call | solution.py:2094
  231.1 0.0 copy-done
  231.1 0.8 copy.29
Async XLA Ops:
  81.0 150.1 %copy-start = (bf16[256,1024]{1,0:T(8,128)(2,1)S(1)}, bf16[256,1024]{1,0:T(8,128)(2,1)}, u32[]{:S(2)}) copy-start(bf16[256,1024]{1,0:T(8,128)(2,1)} %get-tuple-element.61) | copy-start | bytes 1572868

commit v8 on v7

--- a/solution.py
+++ b/solution.py
@@ -1038,12 +1038,12 @@
             def _():
                 near_side(3)
                 far_side(3)
-                swap(0)
 
             @pl.when(j == 4)
             def _():
                 relay(1)
                 onward(1)
+                swap(0)
 
             @pl.when(j == 6)
             def _():
@@ -1151,11 +1151,12 @@
             return total + terms
 
 
+        along.stage_two()
         relay(3)
         near_side(0)
+        onward(3)
         deeper(1)
         far_side(0)
-        onward(3)
 
         def arrive(step, nothing):
             back_copy(step).wait_recv()
@@ -1192,6 +1193,7 @@
             return carry
 
         lax.fori_loop(0, 8, tail_one, 0)
+        along.stage_three()
         relay(0)
         onward(0)
         deeper(3)
@@ -1239,7 +1241,6 @@
 
     gain_swap = core_copy(gain_own, gain_came, 22)
     gain_swap.start()
-    along.stage_two()
 
     def gain_copy(step):
         peer = (lax.rem(place + step, RING), core)
@@ -1259,7 +1260,6 @@
     gain_all[place] = gain_own[...] + gain_came[...]
     lax.fori_loop(1, RING, gain_start, 0)
     lax.fori_loop(0, 4, tail_two, 0)
-    along.stage_three()
     lax.fori_loop(1, 4, tail_three, 0)
     along.close(deep_finish)
     for chain in chains:
@@ -1655,7 +1655,7 @@
         total = total + jnp.sum(probs, axis=0, keepdims=True)
         return total, acc + jnp.dot(values, probs.astype(BF16), preferred_element_type=F32)
 
-    def inner(i):
+    def fetch(i, nothing):
         @pl.when(i - 1 != member)
         def _():
             step = lax.rem(member - i + 1 + HALF, HALF)
@@ -1664,6 +1664,9 @@
             block_copy(step).wait_recv()
 
         key_nat[i] = transposed(qkv_out[i, 2 * HEAD_DIM : 3 * HEAD_DIM, :])
+        return nothing
+
+    def inner(i):
         query_t, start = query_of(i)
         places = (base + i) * BLOCK + lax.broadcasted_iota(jnp.int32, (1, BLOCK), 1)
         query_place = jnp.concatenate([places] * 2, axis=1)
@@ -1719,18 +1722,29 @@
         def _():
             mixed_copy(lax.rem(i - 1 - member + HALF, HALF)).start()
 
-    def per_query(i, nothing):
-        @pl.when(i <= HALF)
+    def order(turn):
+        return turn + turn // 5 * (5 + lax.rem(turn + 3 + member, 4) - turn)
+
+    def per_query(turn, nothing):
+        @pl.when(turn <= 4)
         def _():
-            inner(i)
-
-        @pl.when(i > lag)
+            fetch(turn, 0)
+
+        @pl.when(turn == 5)
         def _():
-            outer(i - lag)
+            lax.fori_loop(5, HALF + 1, fetch, 0)
+
+        @pl.when(turn <= HALF)
+        def _():
+            inner(order(turn))
+
+        @pl.when(turn > lag)
+        def _():
+            outer(order(turn - lag))
 
         return nothing
 
-    lag = 3
+    lag = 1
     lax.fori_loop(1, HALF + lag + 1, per_query, 0)
     mixed_out[member] = part_out[member]
 
@@ -1820,7 +1834,7 @@
     up_far,
     down_own,
     down_far,
-    pair_out,
+    pair_hbm,
     hidden_out,
     output_out,
     ffn_out,
@@ -1830,6 +1844,8 @@
     terms_out,
     swap_out,
     near_out,
+    pair_out,
+    pair_sem,
     middle,
     result,
     upstream,
@@ -1857,6 +1873,10 @@
             device_id=peer,
             device_id_type=MESH,
         )
+
+    def keep_pair(turn):
+        window = pl.ds(lax.rem(z + 6 - turn, 4) * strip_owners, strip_owners)
+        return pltpu.make_async_copy(pair_out.at[window], pair_hbm.at[window], pair_sem.at[turn])
 
     def near_copy(chain, other):
         target = core if other == 0 else 1 - core
@@ -1938,6 +1958,7 @@
                 pair_out[plane * strip_owners + index, base : base + wide, :] = turned[
                     index * wide : (index + 1) * wide
                 ]
+        keep_pair(step).start()
 
         @pl.when(step < len(EARLY))
         def _():
@@ -1975,6 +1996,8 @@
         )
         mixed_back_out[...] = dot_dims(w_out_ref[...], middle_low[...], 1, 1).astype(BF16)
         side_out[1] = middle_low[...].astype(F32).T.astype(BF16)
+        for turn in range(4):
+            keep_pair(turn).wait()
         for chain in range(2):
             for other in range(2):
                 near_copy(chain, other).wait()
@@ -2017,7 +2040,7 @@
                 pl.BlockSpec((chunk, width), lambda i: (lax.rem(turn(i), 2), 0)),
             ],
             out_specs=(
-                whole(RING, 2 * wide, rows),
+                HBM_SPEC,
                 pl.BlockSpec((rows, chunk), lambda i: (0, turn(i))),
                 whole(rows, width),
                 whole(rows, width),
@@ -2028,7 +2051,11 @@
                 HBM_SPEC,
                 HBM_SPEC,
             ),
-            scratch_shapes=[pltpu.VMEM((rows, width), F32)] * 3
+            scratch_shapes=[
+                pltpu.VMEM((RING, 2 * wide, rows), BF16),
+                pltpu.SemaphoreType.DMA((4,)),
+            ]
+            + [pltpu.VMEM((rows, width), F32)] * 3
             + [pltpu.VMEM((rows, width), BF16)]
             + [pltpu.SemaphoreType.DMA((2, 8))] * 2
             + [pltpu.SemaphoreType.DMA((2, 2))] * 2,
@@ -2053,7 +2080,7 @@
 
 
 def settle_kernel(*refs):
-    count = 6
+    count = 7
     sources, gains, rest = refs[:count], refs[count], refs[count + 1 :]
     targets, gain_targets, rest = rest[: count + 2], rest[count + 2 : count + 6], rest[count + 6 :]
     held, in_sem, out_sem = rest[:count], rest[count], rest[count + 1]
@@ -2083,8 +2110,8 @@
         store.wait()
 
 
-def settle_call(tokens, gate_t, up_t, down_t, out_t, qkv_t, gains):
-    sources = (tokens, gate_t, up_t, down_t, out_t, qkv_t)
+def settle_call(output, tokens, gate_t, up_t, down_t, out_t, qkv_t, gains):
+    sources = (output, tokens, gate_t, up_t, down_t, out_t, qkv_t)
     lanes = qkv_t.shape[1]
     query = HEADS * HEAD_DIM // RING
     pair = KV_HEADS * HEAD_DIM // RING
@@ -2093,11 +2120,12 @@
     gain_shapes = [(1, gains.shape[1])] * 2 + [(1, HEAD_DIM)] * 2
     return pl.pallas_call(
         settle_kernel,
-        out_shape=tuple(jax.ShapeDtypeStruct(shape, F32) for shape in shapes + gain_shapes),
+        out_shape=(jax.ShapeDtypeStruct(output.shape, output.dtype),)
+        + tuple(jax.ShapeDtypeStruct(shape, F32) for shape in shapes[1:] + gain_shapes),
         in_specs=[HBM_SPEC] * len(sources) + [VMEM_SPEC],
         out_specs=(HBM_SPEC,) * len(shapes) + (VMEM_SPEC,) * 4,
-        scratch_shapes=[pltpu.VMEM(source.shape, F32) for source in sources]
-        + [pltpu.SemaphoreType.DMA((6,)), pltpu.SemaphoreType.DMA((8,))],
+        scratch_shapes=[pltpu.VMEM(source.shape, source.dtype) for source in sources]
+        + [pltpu.SemaphoreType.DMA((7,)), pltpu.SemaphoreType.DMA((9,))],
         compiler_params=pltpu.CompilerParams(vmem_limit_bytes=63 << 20),
         name="settle_results",
     )(*sources, gains)
@@ -2191,8 +2219,8 @@
         ),
         (tokens[0], query_raw, key_raw, kvq_full, grad_middle, swapped, ffn_near),
     )
-    d_tokens, gate, up, down, out, query, key, value, attn, ffn, query_gains, key_gains = (
-        settle_call(d_tokens, gate_t, up_t, down_t, out_t, qkv_grads, gain_totals)
+    output, d_tokens, gate, up, down, out, query, key, value, attn, ffn, query_gains, key_gains = (
+        settle_call(output, d_tokens, gate_t, up_t, down_t, out_t, qkv_grads, gain_totals)
     )
     return (
         output[None],

time: 234 us -> 230 us (0.983)
  Pallas kernels: 230 us -> 227 us
where the time goes in v8:
time: 230 us; the launch traced here: 228 us
  Pallas kernels  227 us (99%)
    pallas_call x1, Pallas kernels, back_call(): pl.pallas_call(back_kernel, out_shape=(jax.ShapeDtypeStruct((wide, width...  145 us
    pallas_call x1, Pallas kernels, front_call(): pl.pallas_call(front_kernel, out_shape=(jax.ShapeDtypeStruct((HALF + 1, 4...  45.8 us
    pallas_call x1, Pallas kernels, ffn_call(): pl.pallas_call(ffn_kernel, grid_spec=pl.GridSpec(grid=(steps,), in_specs=...  31.5 us

profile of v8, /device:TPU:15, one launch (start us, length us, event | category | flops | bytes accessed | tf_op | source)
XLA Modules:
  0.0 228.0 jit_solution(7134943841435523422)
XLA Ops:
  0.6 45.8 %front_heads.1 = (bf16[9,256,256]{2,1,0:T(8,128)(2,1)}, s32[8,1,256]{2,1,0:T(1,128)}, bf16[256,1024]{1,0:T(8,128)(2,1)}, bf16[8,128,256]{2,1,0:T(8,128)(2,1)}, b...) custom-call(f32[1,1024]{1,0:T(1,128)} %bitcast.28, ...), custom_call_target="tpu_custom_call" | custom-call | tf_op jit(solution)/shard_map/front_heads/pallas_call | solution.py:1783
  46.5 31.5 %ffn_both_ways.1 = (bf16[16,576,256]{2,1,0:T(8,128)(2,1)}, bf16[256,4608]{1,0:T(8,128)(2,1)}, bf16[256,1024]{1,0:T(8,128)(2,1)}, bf16[256,1024]{1,0:T(8,128)(2,1...) custom-call(bf16[256,1024]{1,0:T(8,128)(2,1)} %bitcast.22, ...), custom_call_target="tpu_custom_call" | custom-call | tf_op jit(solution)/shard_map/ffn_both_ways/pallas_call | solution.py:2025
  78.0 145.3 %backward_spread.1 = (f32[288,512]{1,0:T(8,128)}, f32[288,512]{1,0:T(8,128)}, f32[64,2304]{1,0:T(8,128)}, f32[64,512]{1,0:T(8,128)}, f32[128,512]{1,0:T(8,128)}, /*index=5*/f32[256,1024]{1,0:T(8,128)}, f32[4,1024]{1,0:T(4,128)}) custom-call(bf16[16,576,256]{2,1,0:T(8,128)(2,1)} %get-tuple-element.63.pair_hbm, ...), custom_call_target="tpu_custom_call" | custom-call | tf_op jit(solution)/shard_map/backward_spread/pallas_call | solution.py:1323
  223.3 4.5 %settle_results.1 = (bf16[256,1024]{1,0:T(8,128)(2,1)}, f32[256,1024]{1,0:T(8,128)}, f32[288,512]{1,0:T(8,128)}, f32[288,512]{1,0:T(8,128)}, f32[64,2304]{1,0:T(...) custom-call(bf16[256,1024]{1,0:T(8,128)(2,1)} %get-tuple-element.62., ...), custom_call_target="tpu_custom_call" | custom-call | tf_op jit(solution)/shard_map/settle_results/pallas_call | solution.py:2121

commit v9 on v8

--- a/solution.py
+++ b/solution.py
@@ -1744,7 +1744,7 @@
 
         return nothing
 
-    lag = 1
+    lag = 0
     lax.fori_loop(1, HALF + lag + 1, per_query, 0)
     mixed_out[member] = part_out[member]
 

time: 230 us -> 229 us (level)
  no operation moved by 1% of the time
where the time goes in v9:
time: 229 us; the launch traced here: 227 us
  Pallas kernels  226 us (99%)
    pallas_call x1, Pallas kernels, back_call(): pl.pallas_call(back_kernel, out_shape=(jax.ShapeDtypeStruct((wide, width...  145 us
    pallas_call x1, Pallas kernels, front_call(): pl.pallas_call(front_kernel, out_shape=(jax.ShapeDtypeStruct((HALF + 1, 4...  44.5 us
    pallas_call x1, Pallas kernels, ffn_call(): pl.pallas_call(ffn_kernel, grid_spec=pl.GridSpec(grid=(steps,), in_specs=...  31.7 us

profile of v9, /device:TPU:15, one launch (start us, length us, event | category | flops | bytes accessed | tf_op | source)
XLA Modules:
  0.0 226.9 jit_solution(5182523968741893177)
XLA Ops:
  0.6 44.5 %front_heads.1 = (bf16[9,256,256]{2,1,0:T(8,128)(2,1)}, s32[8,1,256]{2,1,0:T(1,128)}, bf16[256,1024]{1,0:T(8,128)(2,1)}, bf16[8,128,256]{2,1,0:T(8,128)(2,1)}, b...) custom-call(f32[1,1024]{1,0:T(1,128)} %bitcast.28, ...), custom_call_target="tpu_custom_call" | custom-call | tf_op jit(solution)/shard_map/front_heads/pallas_call | solution.py:1783
  45.1 31.7 %ffn_both_ways.1 = (bf16[16,576,256]{2,1,0:T(8,128)(2,1)}, bf16[256,4608]{1,0:T(8,128)(2,1)}, bf16[256,1024]{1,0:T(8,128)(2,1)}, bf16[256,1024]{1,0:T(8,128)(2,1...) custom-call(bf16[256,1024]{1,0:T(8,128)(2,1)} %bitcast.22, ...), custom_call_target="tpu_custom_call" | custom-call | tf_op jit(solution)/shard_map/ffn_both_ways/pallas_call | solution.py:2025
  76.9 145.4 %backward_spread.1 = (f32[288,512]{1,0:T(8,128)}, f32[288,512]{1,0:T(8,128)}, f32[64,2304]{1,0:T(8,128)}, f32[64,512]{1,0:T(8,128)}, f32[128,512]{1,0:T(8,128)}, /*index=5*/f32[256,1024]{1,0:T(8,128)}, f32[4,1024]{1,0:T(4,128)}) custom-call(bf16[16,576,256]{2,1,0:T(8,128)(2,1)} %get-tuple-element.63.pair_hbm, ...), custom_call_target="tpu_custom_call" | custom-call | tf_op jit(solution)/shard_map/backward_spread/pallas_call | solution.py:1323
  222.2 4.5 %settle_results.1 = (bf16[256,1024]{1,0:T(8,128)(2,1)}, f32[256,1024]{1,0:T(8,128)}, f32[288,512]{1,0:T(8,128)}, f32[288,512]{1,0:T(8,128)}, f32[64,2304]{1,0:T(...) custom-call(bf16[256,1024]{1,0:T(8,128)(2,1)} %get-tuple-element.62., ...), custom_call_target="tpu_custom_call" | custom-call | tf_op jit(solution)/shard_map/settle_results/pallas_call | solution.py:2121
